TPU v7x, 512 devices: a whole 4x4x16 slice. The times are simulated.
512 devices in a mesh: seq: 128 (over x, z, core), ch: 4 (over y).
Axes of the slice: x: 4, y: 4, z: 16, core: 2. Of those that a mesh axis runs over, the one named last changes fastest.
Arguments:
- signal: bfloat16 [512, 16448], P('seq'), may hold values from -6 to 6
- cotangent: bfloat16 [512, 16448], P('seq'), may hold values from -6 to 6
- counts: int32 [128], replicated, may hold values from 1 to 4, as said below
- freq_gain: float32 [64], replicated, may hold values from 0.5 to 1.5
- freq_in: bfloat16 [64, 256], P(None, 'ch'), may hold values from -0.75 to 0.75
- freq_taps: float32 [3, 256], P(None, 'ch'), may hold values from -3.5 to 3.5
- freq_out: bfloat16 [256, 64], P('ch'), may hold values from -0.375 to 0.375
- time_gain: float32 [64], replicated, may hold values from 0.5 to 1.5
- time_in: bfloat16 [64, 256], P(None, 'ch'), may hold values from -0.75 to 0.75
- time_taps: float32 [3, 3, 256], P(None, None, 'ch'), may hold values from -3.5 to 3.5
- time_out: bfloat16 [256, 64], P('ch'), may hold values from -0.375 to 0.375
Outputs:
- output: bfloat16 [512, 16448], P('seq')
- d_signal: bfloat16 [512, 16448], P('seq')
- grad_freq_gain: float32 [64], replicated
- grad_freq_in: float32 [64, 256], P(None, 'ch')
- grad_freq_taps: float32 [3, 256], P(None, 'ch')
- grad_freq_out: float32 [256, 64], P('ch')
- grad_time_gain: float32 [64], replicated
- grad_time_in: float32 [64, 256], P(None, 'ch')
- grad_time_taps: float32 [3, 3, 256], P(None, None, 'ch')
- grad_time_out: float32 [256, 64], P('ch')
Inputs may be any that keep to these rules, and one draw needn't show every extreme that they name: counts[i] is the number of valid leading frames of frames i * 4 to (i + 1) * 4 - 1; some block is full.
All inputs are finite; a program needn't handle non-finite values.
Results may differ from a plain program's by a relative error of at most 0.024.
Values may be sent and summed in bfloat16 or wider, within the bound.
No kernel may reach another device: no remote copies, remote signals or barrier semaphores. Data moves between devices by JAX's collectives and lax.ppermute only.
A program may use at most 64 MiB of HBM per device.

v0:
```python
import math

import jax
import jax.numpy as jnp
from jax import lax
from jax.sharding import PartitionSpec as P

EPS = 1e-05


def offset_rows(values, offset, axis_pos):
    length = values.shape[axis_pos]
    widths = [(0, 0)] * values.ndim
    widths[axis_pos] = (max(-offset, 0), max(offset, 0))
    padded = jnp.pad(values, widths)
    return lax.slice_in_dim(padded, max(offset, 0), max(offset, 0) + length, axis=axis_pos)


def dilated(values, tap_rows, spacing, axis_pos):
    return (
        tap_rows[0] * offset_rows(values, -spacing, axis_pos)
        + tap_rows[1] * values
        + tap_rows[2] * offset_rows(values, spacing, axis_pos)
    )


def dilated_back(grads, tap_rows, spacing, axis_pos):
    return (
        tap_rows[0] * offset_rows(grads, spacing, axis_pos)
        + tap_rows[1] * grads
        + tap_rows[2] * offset_rows(grads, -spacing, axis_pos)
    )


def tap_sums(drive, source, spacing, axis_pos):
    over_dims = tuple(range(drive.ndim - 1))
    return jnp.stack(
        [
            jnp.sum(drive * offset_rows(source, -spacing, axis_pos), axis=over_dims),
            jnp.sum(drive * source, axis=over_dims),
            jnp.sum(drive * offset_rows(source, spacing, axis_pos), axis=over_dims),
        ]
    )


def silu_slope(drive):
    sigmoid_part = jax.nn.sigmoid(drive)
    return sigmoid_part * (1.0 + drive * (1.0 - sigmoid_part))


def inverse_norm(features):
    return lax.rsqrt(jnp.mean(features * features, axis=-1, keepdims=True) + EPS)


def norm_back(d_normed, features, norm_scale, gain):
    summed = jnp.sum(gain * d_normed * features, axis=-1, keepdims=True)
    return (
        norm_scale * gain * d_normed
        - features * norm_scale * norm_scale * norm_scale * summed / features.shape[-1]
    )


def spacing_for(layer_idx, frame_block):
    if layer_idx == 0:
        return 1
    return frame_block * 4 ** (layer_idx - 1)


def band_whole(values, bin_count, padded_bins):
    row_count, channels = (values.shape[0], values.shape[2])
    padded = jnp.pad(values, ((0, 0), (0, padded_bins - bin_count), (0, 0)))
    arrived = lax.all_to_all(
        padded.reshape(row_count, padded_bins * channels),
        "seq",
        split_axis=1,
        concat_axis=0,
        tiled=True,
    )
    return arrived.reshape(arrived.shape[0], -1, channels)


def time_whole(values, bin_count):
    row_count, band_bins, channels = values.shape
    arrived = lax.all_to_all(
        values.reshape(row_count, band_bins * channels),
        "seq",
        split_axis=0,
        concat_axis=1,
        tiled=True,
    )
    return arrived.reshape(arrived.shape[0], -1, channels)[:, :bin_count]


def band_total(partial_sum):
    return lax.psum(partial_sum.astype(jnp.bfloat16), "ch").astype(jnp.float32)


def time_path(
    band_x, d_two, valid, gain, weight_in, taps, weight_out, out_mix, back_mix, frame_block
):
    layer_count = taps.shape[0]
    band_scale = inverse_norm(band_x)
    band_normed = (band_x * band_scale * gain).astype(jnp.bfloat16)
    hidden = (
        jnp.einsum("tbc,ch->tbh", band_normed, weight_in, preferred_element_type=jnp.float32)
        * valid
    )
    states = [hidden]
    drives = []
    for layer_idx in range(layer_count):
        drive = dilated(hidden, taps[layer_idx], spacing_for(layer_idx, frame_block), 0)
        drives.append(drive)
        hidden = hidden + jax.nn.silu(drive)
        states.append(hidden)
    top_hidden = hidden.astype(jnp.bfloat16)
    x_two = (band_x + out_mix(top_hidden)).astype(jnp.bfloat16)
    grad_tout = jnp.einsum("tbh,tbc->hc", top_hidden, d_two, preferred_element_type=jnp.float32)
    d_hidden = jnp.einsum("tbc,hc->tbh", d_two, weight_out, preferred_element_type=jnp.float32)
    tap_list = [None] * layer_count
    for layer_idx in reversed(range(layer_count)):
        spacing = spacing_for(layer_idx, frame_block)
        d_drive = d_hidden * silu_slope(drives[layer_idx])
        tap_list[layer_idx] = tap_sums(d_drive, states[layer_idx], spacing, 0)
        d_hidden = d_hidden + dilated_back(d_drive, taps[layer_idx], spacing, 0)
    d_pre = (d_hidden * valid).astype(jnp.bfloat16)
    grad_tin = jnp.einsum("tbc,tbh->ch", band_normed, d_pre, preferred_element_type=jnp.float32)
    d_normed = back_mix(d_pre)
    grad_tgain = jnp.sum(d_normed * band_x * band_scale, axis=(0, 1))
    d_one = (d_two.astype(jnp.float32) + norm_back(d_normed, band_x, band_scale, gain)).astype(
        jnp.bfloat16
    )
    return (x_two, d_one, (grad_tgain, grad_tin, jnp.stack(tap_list), grad_tout))


def shards(
    signal,
    cotangent,
    counts,
    freq_gain,
    freq_in,
    freq_taps,
    freq_out,
    time_gain,
    time_in,
    time_taps,
    time_out,
):
    frame_block = signal.shape[0]
    channels = freq_gain.shape[0]
    bin_count = signal.shape[1] // channels
    seq_count = lax.axis_size("seq")
    frame_count = frame_block * seq_count
    grad_scale = 1.0 / math.sqrt(frame_count * bin_count)
    x_time = signal.reshape(frame_block, bin_count, channels).astype(jnp.float32)
    freq_scale = inverse_norm(x_time)
    freq_normed = (x_time * freq_scale * freq_gain).astype(jnp.bfloat16)
    freq_hidden = jnp.einsum(
        "tfc,ch->tfh", freq_normed, freq_in, preferred_element_type=jnp.float32
    )
    freq_drive = dilated(freq_hidden, freq_taps, 1, 1)
    freq_active = jax.nn.silu(freq_drive).astype(jnp.bfloat16)
    freq_part = jnp.einsum("tfh,hc->tfc", freq_active, freq_out, preferred_element_type=jnp.float32)
    cot_time = cotangent.reshape(frame_block, bin_count, channels)
    freq_mixed = lax.psum(freq_part.astype(jnp.bfloat16), "ch").astype(jnp.float32)
    x_one = (x_time + freq_mixed).astype(jnp.bfloat16)
    valid = (
        (jnp.arange(frame_block)[None, :] < counts[:, None])
        .astype(jnp.float32)
        .reshape(frame_count)[:, None, None]
    )
    padded_bins = (bin_count + seq_count - 1) // seq_count * seq_count
    band_x = band_whole(x_one, bin_count, padded_bins).astype(jnp.float32)
    d_two = band_whole(cot_time, bin_count, padded_bins)

    def mix_forward(top_rows):
        return band_total(
            jnp.einsum("tbh,hc->tbc", top_rows, time_out, preferred_element_type=jnp.float32)
        )

    def mix_backward(d_rows):
        return band_total(
            jnp.einsum("tbh,ch->tbc", d_rows, time_in, preferred_element_type=jnp.float32)
        )

    x_two, d_one, time_grads = time_path(
        band_x,
        d_two,
        valid,
        time_gain,
        time_in,
        time_taps,
        time_out,
        mix_forward,
        mix_backward,
        frame_block,
    )
    output_time = time_whole(x_two, bin_count)
    d_one_time = time_whole(d_one, bin_count)
    grad_fout = jnp.einsum(
        "tfh,tfc->hc", freq_active, d_one_time, preferred_element_type=jnp.float32
    )
    d_active = jnp.einsum("tfc,hc->tfh", d_one_time, freq_out, preferred_element_type=jnp.float32)
    d_freq_drive = d_active * silu_slope(freq_drive)
    grad_ftaps = tap_sums(d_freq_drive, freq_hidden, 1, 1)
    d_freq_hidden = dilated_back(d_freq_drive, freq_taps, 1, 1).astype(jnp.bfloat16)
    grad_fin = jnp.einsum(
        "tfc,tfh->ch", freq_normed, d_freq_hidden, preferred_element_type=jnp.float32
    )
    d_freq_normed = lax.psum(
        jnp.einsum(
            "tfh,ch->tfc", d_freq_hidden, freq_in, preferred_element_type=jnp.float32
        ).astype(jnp.bfloat16),
        "ch",
    ).astype(jnp.float32)
    grad_fgain = jnp.sum(d_freq_normed * x_time * freq_scale, axis=(0, 1))
    d_signal = (
        d_one_time.astype(jnp.float32) + norm_back(d_freq_normed, x_time, freq_scale, freq_gain)
    ).astype(jnp.bfloat16)
    freq_grads = (grad_fgain, grad_fin, grad_ftaps, grad_fout)
    seq_grads = freq_grads + time_grads
    summed = lax.psum(seq_grads, "seq")
    all_grads = tuple(summed)
    output = output_time.reshape(frame_block, bin_count * channels)
    return (
        output,
        d_signal.reshape(frame_block, bin_count * channels),
        all_grads[0] * grad_scale,
        all_grads[1] * grad_scale,
        all_grads[2] * grad_scale,
        all_grads[3] * grad_scale,
        all_grads[4] * grad_scale,
        all_grads[5] * grad_scale,
        all_grads[6] * grad_scale,
        all_grads[7] * grad_scale,
    )


def solution(mesh):
    return jax.shard_map(
        shards,
        mesh=mesh,
        in_specs=(
            P("seq", None),
            P("seq", None),
            P(),
            P(),
            P(None, "ch"),
            P(None, "ch"),
            P("ch", None),
            P(),
            P(None, "ch"),
            P(None, None, "ch"),
            P("ch", None),
        ),
        out_specs=(
            P("seq", None),
            P("seq", None),
            P(),
            P(None, "ch"),
            P(None, "ch"),
            P("ch", None),
            P(),
            P(None, "ch"),
            P(None, None, "ch"),
            P("ch", None),
        ),
        check_vma=False,
    )
```

profile of v0, /device:TPU:1, one launch (start us, length us, event | category | flops | bytes accessed | tf_op | source)
XLA Modules:
  0.0 633.5 jit_solution(5427711675760783707)
XLA Ops:
  7.2 1.1 reshape.129
  8.8 0.9 copy.87
  9.7 20.5 %all-to-all-start.2 = ((bf16[4,128,192]{2,0,1:T(4,128)(2,1)}), bf16[4,128,192]{2,0,1:T(4,128)(2,1)S(1)}, u32[]{:S(2)}, u32[]{:S(2)}) async-start(bf16[4,128,192]{2,0,1:T(4,128)(2,1)} %copy.87), calls=%async_computation.2 | async-start | bytes 524288 | tf_op jit(solution)/shard_map/all_to_all | solution.py:72
  31.0 0.7 copy-done.17
  31.7 0.6 copy-done.16
  32.6 1.0 multiply_convert_fusion.1
  33.7 0.9 convolution_convert_fusion.3
  34.6 56.3 %all-reduce.25.cloned.1.call-done = bf16[4,257,64]{1,2,0:T(8,128)(2,1)} async-done(((bf16[4,257,64]{1,2,0:T(8,128)(2,1)}), bf16[4,257,64]{1,2,0:T(8,128)(2,1)}) %all-reduce.25.cloned.1.call-update) | async-done | bytes 131600 | tf_op jit(solution)/shard_map/psum | solution.py:164
  90.9 1.0 add_convert_fusion.3
  92.5 0.9 copy.79
  93.4 18.8 %all-to-all-start = ((bf16[4,128,192]{2,0,1:T(4,128)(2,1)}), bf16[4,128,192]{2,0,1:T(4,128)(2,1)S(1)}, u32[]{:S(2)}, u32[]{:S(2)}) async-start(bf16[4,128,192]{2,0,1:T(4,128)(2,1)} %copy.79), calls=%async_computation | async-start | bytes 524288 | tf_op jit(solution)/shard_map/all_to_all | solution.py:72
  113.8 20.9 %all-to-all-done = bf16[4,128,192]{2,0,1:T(4,128)(2,1)S(1)} async-done(((bf16[4,128,192]{2,0,1:T(4,128)(2,1)}), bf16[4,128,192]{2,0,1:T(4,128)(2,1)S(1)}, u32[]{:S(2)}, u32[]{:S(2)}) %all-to-all-start) | async-done | bytes 196640 | tf_op jit(solution)/shard_map/all_to_all | solution.py:72
  135.5 0.6 multiply_reduce_fusion
  137.9 0.9 multiply_reduce_fusion.4
  138.8 0.9 multiply_reduce_fusion.7
  139.7 0.9 multiply_reduce_fusion.10
  140.9 0.9 convolution_convert_fusion
  141.8 45.7 %all-reduce.27.cloned.1.call-done = bf16[512,3,64]{0,2,1:T(8,128)(2,1)} async-done(((bf16[512,3,64]{0,2,1:T(8,128)(2,1)}), bf16[512,3,64]{0,2,1:T(8,128)(2,1)}) %all-reduce.27.cloned.1.call-update) | async-done | bytes 196624 | tf_op jit(solution)/shard_map/psum | solution.py:95
  187.5 1.3 fusion.10
  189.2 1.0 all_to_all.54
  190.2 18.7 %all-to-all-start.3 = ((bf16[128,4,192]{2,1,0:T(4,128)(2,1)}), bf16[128,4,192]{2,1,0:T(4,128)(2,1)S(1)}, u32[]{:S(2)}, u32[]{:S(2)}) async-start(bf16[128,4,192]{2,1,0:T(4,128)(2,1)} %all_to_all.54), calls=%async_computation.3 | async-start | bytes 524288 | tf_op jit(solution)/shard_map/all_to_all | solution.py:84
  209.0 0.6 pad_maximum_fusion
  209.6 0.8 convolution_bitcast_fusion
  210.4 0.9 convolution_bitcast_fusion.1
  211.3 0.9 convolution_convert_fusion.2
  212.2 19.1 %all-to-all-done.3 = bf16[128,4,192]{2,1,0:T(4,128)(2,1)S(1)} async-done(((bf16[128,4,192]{2,1,0:T(4,128)(2,1)}), bf16[128,4,192]{2,1,0:T(4,128)(2,1)S(1)}, u32[]{:S(2)}, u32[]{:S(2)}) %all-to-all-start.3) | async-done | bytes 196640 | tf_op jit(solution)/shard_map/all_to_all | solution.py:84
  231.6 0.7 copy-done.1
  232.6 0.7 multiply_reduce_fusion.13
  233.3 0.9 convolution_convert_fusion.1
  234.2 0.6 pad_maximum_fusion.1
  235.0 0.9 convolution_bitcast_fusion.2
  235.9 0.9 convolution_bitcast_fusion.3
  236.7 43.9 %all-reduce.31.cloned.1.call-done = (bf16[512,3,64]{0,2,1:T(8,128)(2,1)}, bf16[4,257,64]{1,2,0:T(8,128)(2,1)}) async-done(((bf16[512,3,64]{0,2,1:T(8,128)(2,1)}, bf16[4,257,64]{1,2,0:T(8,128)(2,1)}), (bf16[512,3,64]{0,2,1:T(8,128)(2,1)}, bf16[4,257,64]{1,2,0:T(8,128)(2,1)})) %all-reduce.31.cloned.1.call-update) | async-done | bytes 328208 | tf_op jit(solution)/shard_map/psum | solution.py:95
  280.6 1.7 fusion.34
  282.3 0.7 fusion.31
  283.7 0.9 reshape.132
  284.9 1.0 all_to_all.48
  285.9 18.8 %all-to-all-start.1 = ((bf16[128,4,192]{2,1,0:T(4,128)(2,1)}), bf16[128,4,192]{2,1,0:T(4,128)(2,1)S(1)}, u32[]{:S(2)}, u32[]{:S(2)}) async-start(bf16[128,4,192]{2,1,0:T(4,128)(2,1)} %all_to_all.48), calls=%async_computation.1 | async-start | bytes 524288 | tf_op jit(solution)/shard_map/all_to_all | solution.py:84
  304.7 314.1 %all-reduce.29.cloned.1.call-done = (f32[64]{0:T(128)}, f32[64,64]{1,0:T(8,128)}, f32[3,64]{1,0:T(4,128)}, f32[64,64]{1,0:T(8,128)}, f32[64]{0:T(128)}, /*index=...) async-done(((f32[64]{0:T(128)}, f32[64,64]{1,0:T(8,128)}, f32[3,64]{1,0:T(4,128)}, f32[64,64]{1,0:T(8,128)}, f32[64]{0:T(128)}, /*index=5*/f32[64,64]{1,0:T(8,128)}, ...) | async-done | bytes 69136 | tf_op jit(solution)/shard_map/psum | solution.py:221
  618.8 1.4 broadcast_multiply_fusion
  620.2 0.6 broadcast_multiply_fusion.4
  620.8 0.6 broadcast_multiply_fusion.5
  621.4 0.6 copy-done.20
  622.5 0.7 copy-done.19
  623.7 0.6 broadcast_multiply_fusion.1
  624.5 0.6 broadcast_multiply_fusion.2
  625.2 0.6 broadcast_multiply_fusion.3
  626.2 0.9 reshape.128
  (88 shorter events, 10.4 us)
Async XLA Ops:
  7.2 130.7 %copy-start = (bf16[64,64]{1,0:T(8,128)(2,1)S(1)}, bf16[64,64]{1,0:T(8,128)(2,1)}, u32[]{:S(2)}) copy-start(bf16[64,64]{1,0:T(8,128)(2,1)} %param.21) | copy-start | bytes 24580
  9.7 20.6 %copy-start.5 = (bf16[4,16448]{1,0:T(4,128)(2,1)S(1)}, bf16[4,16448]{1,0:T(4,128)(2,1)}, u32[]{:S(2)}) copy-start(bf16[4,16448]{1,0:T(4,128)(2,1)} %param.11) | copy-start | bytes 394756
  9.7 83.8 %all-to-all-start.2 = ((bf16[4,128,192]{2,0,1:T(4,128)(2,1)}), bf16[4,128,192]{2,0,1:T(4,128)(2,1)S(1)}, u32[]{:S(2)}, u32[]{:S(2)}) async-start(bf16[4,128,192]{2,0,1:T(4,128)(2,1)} %copy.87), calls=%async_computation.2 | async-start | bytes 524288 | tf_op jit(solution)/shard_map/all_to_all | solution.py:72
  30.2 60.7 %all-reduce.25.cloned.1.call-start = ((), (), s32[]{:S(2)}) async-start(), calls=%async_computation.4 | async-start | bytes 393216 | tf_op jit(solution)/shard_map/psum | solution.py:164
  30.7 1.0 copy-start.7
  31.0 0.7 copy-start.17
  31.7 0.7 copy-start.16
  32.6 1.1 copy-start.11
  93.4 19.1 %copy-start.18 = (s32[128]{0:T(128)S(1)}, s32[128]{0:T(128)}, u32[]{:S(2)}) copy-start(s32[128]{0:T(128)} %param.13) | copy-start | bytes 1540
  93.4 41.2 %all-to-all-start = ((bf16[4,128,192]{2,0,1:T(4,128)(2,1)}), bf16[4,128,192]{2,0,1:T(4,128)(2,1)S(1)}, u32[]{:S(2)}, u32[]{:S(2)}) async-start(bf16[4,128,192]{2,0,1:T(4,128)(2,1)} %copy.79), calls=%async_computation | async-start | bytes 524288 | tf_op jit(solution)/shard_map/all_to_all | solution.py:72
  112.3 75.3 %all-reduce.27.cloned.1.call-start = ((), (), s32[]{:S(2)}) async-start(), calls=%async_computation.5 | async-start | bytes 393216 | tf_op jit(solution)/shard_map/psum | solution.py:95
  112.6 0.7 copy-start.13
  136.1 0.7 copy-start.15
  136.2 0.7 copy-start.6
  190.2 41.1 %all-to-all-start.3 = ((bf16[128,4,192]{2,1,0:T(4,128)(2,1)}), bf16[128,4,192]{2,1,0:T(4,128)(2,1)S(1)}, u32[]{:S(2)}, u32[]{:S(2)}) async-start(bf16[128,4,192]{2,1,0:T(4,128)(2,1)} %all_to_all.54), calls=%async_computation.3 | async-start | bytes 524288 | tf_op jit(solution)/shard_map/all_to_all | solution.py:84
  208.9 71.7 %all-reduce.31.cloned.1.call-start = ((), (), s32[]{:S(2)}) async-start(), calls=%async_computation.7 | async-start | bytes 786432 | tf_op jit(solution)/shard_map/psum | solution.py:95
  231.3 1.0 copy-start.1
  234.2 384.6 %all-reduce.29.cloned.1.call-start = ((), (), s32[]{:S(2)}) async-start(), calls=%async_computation.6 | async-start | bytes 280576 | tf_op jit(solution)/shard_map/psum | solution.py:221
  280.6 1.7 copy-start.2
  280.6 1.7 copy-start.3
  282.3 0.9 copy-start.4
  285.9 340.0 %all-to-all-start.1 = ((bf16[128,4,192]{2,1,0:T(4,128)(2,1)}), bf16[128,4,192]{2,1,0:T(4,128)(2,1)S(1)}, u32[]{:S(2)}, u32[]{:S(2)}) async-start(bf16[128,4,192]{2,1,0:T(4,128)(2,1)} %all_to_all.48), calls=%async_computation.1 | async-start | bytes 524288 | tf_op jit(solution)/shard_map/all_to_all | solution.py:84
  618.8 1.4 copy-start.12
  618.8 4.9 copy-start.10
  620.2 0.7 copy-start.14
  621.4 0.6 copy-start.20
  622.5 0.7 copy-start.19
  623.7 0.8 copy-start.9
  624.5 0.8 copy-start.8
Sparse Core Ops, SparseCore 0:
  34.8 56.0 all-reduce.24
  141.9 45.5 all-reduce.26
  234.3 46.2 all-reduce.30
  286.1 332.6 all-reduce.28
where the time goes:
time: 634 us
  waiting for transfers between devices  500 us (79%)
  starting transfers between devices  77.2 us (12%)
  other arithmetic  17.1 us (3%)
  local copies, waits for them, and re-layouts  16.4 us (3%)
  between operations  14.2 us (2%)
  matrix products  8.71 us (1%)
    psum x1, waiting for transfers between devices, shards(): summed = lax.psum(seq_grads, 'seq')  314 us
    psum x2, waiting for transfers between devices, band_total(): return lax.psum(partial_sum.astype(jnp.bfloat16), 'ch').astype(jnp.float32)  89.6 us
    psum x1, waiting for transfers between devices, shards(): lax.psum(freq_part.astype(jnp.bfloat16), 'ch').astype(jnp.float32)  56.3 us
    all_to_all x2, starting transfers between devices, band_whole(): lax.all_to_all(padded.reshape(row_count, padded_bins * channels), 'seq',...  39.4 us
    all_to_all x2, starting transfers between devices, time_whole(): lax.all_to_all(values.reshape(row_count, band_bins * channels), 'seq', sp...  37.5 us
    all_to_all x2, waiting for transfers between devices, band_whole(): lax.all_to_all(padded.reshape(row_count, padded_bins * channels), 'seq',...  20.9 us
    all_to_all x2, waiting for transfers between devices, time_whole(): lax.all_to_all(values.reshape(row_count, band_bins * channels), 'seq', sp...  19.1 us
  transfers between devices with their start and end apart: 8, of which 6 were waited for; matrix products, arithmetic and copies ran while one was open for 3% of the time, Pallas kernels for 0%

commit v1 on v0

v1 whole, which is shorter than its diff:
```python
import math

import jax
import jax.numpy as jnp
from jax import lax
from jax.sharding import Mesh, PartitionSpec as P

EPS = 1e-05
FR = 4
ROWS = 80
LEAD = 8
BF = jnp.bfloat16
F32 = jnp.float32


def nt(a, b):
    return lax.dot_general(a, b, (((1,), (1,)), ((), ())), preferred_element_type=F32)


def nn(a, b):
    return lax.dot_general(a, b, (((1,), (0,)), ((), ())), preferred_element_type=F32)


def tn(a, b):
    return lax.dot_general(a, b, (((0,), (0,)), ((), ())), preferred_element_type=F32)


def roll_rows(values, amount):
    return jnp.roll(values, amount, 0)


def sigmoid(values):
    return 0.5 * jnp.tanh(0.5 * values) + 0.5


def inverse_norm(features):
    return lax.rsqrt(jnp.mean(features * features, axis=-1, keepdims=True) + EPS)


def norm_back(d_normed, features, scale, gain):
    scaled = d_normed * gain
    summed = jnp.sum(scaled * features, axis=-1, keepdims=True)
    return scale * scaled - features * (scale * scale * scale * summed * (1.0 / features.shape[-1]))


def bins_conv(values, taps):
    return taps[0:1] * roll_rows(values, 1) + taps[1:2] * values + taps[2:3] * roll_rows(values, -1)


def freq_forward(pair, weights, taps, gain):
    features = pair[:, :64].astype(F32)
    scale = inverse_norm(features)
    normed = (features * scale * gain).astype(BF)
    hidden = nt(normed, weights[:, :64])
    drive = bins_conv(hidden, taps)
    active = (drive * sigmoid(drive)).astype(BF)
    mixed = nn(active, weights[:, 64:])
    x_one = (features + mixed).astype(BF)
    return jnp.concatenate([x_one, pair[:, 64:]], axis=1), hidden


def own_bins(last_plane):
    row = lax.broadcasted_iota(jnp.int32, (ROWS, 1), 0)
    upper = LEAD + 64 + last_plane
    one = jnp.where((row >= LEAD) & (row < upper), 1.0, 0.0).astype(F32)
    return jnp.concatenate([one] * FR, axis=0)


def freq_backward(pair, hidden, back, weights, taps, gain, last_plane):
    own = own_bins(last_plane)
    features = pair[:, :64].astype(F32)
    scale = inverse_norm(features)
    grad = back[:, 64:]
    grad_own = grad.astype(F32) * own
    normed = (features * scale * gain * own).astype(BF)
    drive = bins_conv(hidden, taps)
    gate = sigmoid(drive)
    active = drive * gate
    slope = gate + active * (1.0 - gate)
    grad_out = tn(active.astype(BF), grad_own.astype(BF))
    d_drive = nt(grad, weights[:, 64:]) * slope
    d_own = d_drive * own
    tap_rows = [
        jnp.sum(d_own * roll_rows(hidden, 1), axis=0, keepdims=True),
        jnp.sum(d_own * hidden, axis=0, keepdims=True),
        jnp.sum(d_own * roll_rows(hidden, -1), axis=0, keepdims=True),
    ]
    d_hidden = (
        taps[0:1] * roll_rows(d_drive, -1) + taps[1:2] * d_drive + taps[2:3] * roll_rows(d_drive, 1)
    ).astype(BF)
    grad_in = tn(d_hidden, normed)
    d_normed = nn(d_hidden, weights[:, :64])
    grad_gain = jnp.sum(d_normed * features * scale * own, axis=0, keepdims=True)
    d_signal = (grad.astype(F32) + norm_back(d_normed, features, scale, gain)).astype(BF)
    return (
        jnp.concatenate([back[:, :64], d_signal], axis=1),
        jnp.concatenate([grad_out, grad_in], axis=1),
        jnp.concatenate(tap_rows, axis=0),
        grad_gain,
    )


def groups_on(values, count):
    split = 8 * abs(count)
    if count > 0:
        head = jnp.concatenate(
            [jnp.concatenate([values[8 * i + 4 : 8 * i + 8], values[8 * i : 8 * i + 4]], axis=0) for i in range(count)],
            axis=0,
        )
        return jnp.concatenate([values[split:], head], axis=0)
    base = values.shape[0] - split
    tail = jnp.concatenate(
        [
            jnp.concatenate([values[base + 8 * i + 4 : base + 8 * i + 8], values[base + 8 * i : base + 8 * i + 4]], axis=0)
            for i in range(-count)
        ],
        axis=0,
    )
    return jnp.concatenate([tail, values[:base]], axis=0)


def later(values, spacing):
    if spacing == 1:
        place = lax.broadcasted_iota(jnp.int32, values.shape, 0) & 3
        return jnp.where(place == 3, roll_rows(groups_on(values, 1), 3), roll_rows(values, -1))
    return groups_on(values, spacing // FR)


def earlier(values, spacing):
    if spacing == 1:
        place = lax.broadcasted_iota(jnp.int32, values.shape, 0) & 3
        return jnp.where(place == 0, roll_rows(groups_on(values, -1), -3), roll_rows(values, 1))
    return groups_on(values, -(spacing // FR))


def own_rows(values):
    tiles = values.reshape(values.shape[0] // 8, 8, values.shape[1])
    return jnp.sum(jnp.sum(tiles, axis=0)[:4], axis=0, keepdims=True)


def time_path(pair, marks, weights, taps, gain, share):
    valid, inside = marks[:, 0:1], marks[:, 1:2]
    place = lax.broadcasted_iota(jnp.int32, (pair.shape[0], 1), 0) & 7
    counted = jnp.where(place < 4, share, 0.0).astype(F32)
    features = pair[:, :64].astype(F32)
    grad = pair[:, 64:]
    scale = inverse_norm(features)
    normed = features * scale * gain
    weight_in, weight_out = weights[:, :64], weights[:, 64:]
    state = nt(normed.astype(BF), weight_in) * valid
    states, slopes = [], []
    for layer in range(3):
        spacing = (1, 4, 16)[layer]
        row = taps[3 * layer : 3 * layer + 3]
        drive = row[0:1] * earlier(state, spacing) + row[1:2] * state + row[2:3] * later(state, spacing)
        gate = sigmoid(drive)
        active = drive * gate
        states.append(state)
        slopes.append(gate + active * (1.0 - gate))
        state = state + active
        if layer < 2:
            state = state * inside
    top = state.astype(BF)
    output = (features + nn(top, weight_out)).astype(BF)
    grad_out = tn(top, (grad.astype(F32) * counted).astype(BF))
    d_state = nt(grad, weight_out)
    tap_rows = [None] * 9
    for layer in reversed(range(3)):
        spacing = (1, 4, 16)[layer]
        row = taps[3 * layer : 3 * layer + 3]
        d_drive = d_state * slopes[layer]
        if layer < 2:
            d_drive = d_drive * inside
        held = states[layer]
        tap_rows[3 * layer] = own_rows(d_drive * earlier(held, spacing))
        tap_rows[3 * layer + 1] = own_rows(d_drive * held)
        tap_rows[3 * layer + 2] = own_rows(d_drive * later(held, spacing))
        d_state = d_state + (
            row[0:1] * later(d_drive, spacing) + row[1:2] * d_drive + row[2:3] * earlier(d_drive, spacing)
        )
    d_pre = (d_state * valid).astype(BF)
    grad_in = tn(d_pre, (normed * counted).astype(BF))
    d_normed = nn(d_pre, weight_in)
    grad_gain = own_rows(d_normed * features * scale) * share
    d_one = (grad.astype(F32) + norm_back(d_normed, features, scale, gain)).astype(BF)
    return (
        jnp.concatenate([output, d_one], axis=1),
        jnp.concatenate([grad_out, grad_in], axis=1),
        jnp.concatenate(tap_rows, axis=0) * share,
        grad_gain,
    )


def plane_rows(values, plane):
    frames, width = values.shape
    padded = jnp.pad(values, ((0, 0), (LEAD * 64, (ROWS - LEAD + 192) * 64 - width)))
    cut = lax.dynamic_slice(padded, (0, plane * 4096), (frames, ROWS * 64))
    return cut.reshape(frames * ROWS, 64)


def begin(signal, cotangent, freq_in, freq_taps, freq_out, time_in, time_taps, time_out, plane):
    pair = jnp.concatenate([plane_rows(signal, plane), plane_rows(cotangent, plane)], axis=1)
    taps = jnp.concatenate([freq_taps, time_taps.reshape(9, 64)], axis=0)
    high = lax.reduce_precision(taps, 8, 7)
    low = lax.reduce_precision(taps - high, 8, 7)
    packed = jnp.concatenate(
        [
            jnp.concatenate([freq_in.T, freq_out], axis=1),
            jnp.concatenate([time_in.T, time_out], axis=1),
            jnp.concatenate([high, low], axis=1).astype(BF),
            jnp.zeros((4, 128), BF),
        ],
        axis=0,
    )
    return pair, packed


def unpack(gathered):
    freq_w = gathered[:, :64].reshape(256, 128)
    time_w = gathered[:, 64:128].reshape(256, 128)
    tap_rows = gathered[:, 128:140].astype(F32)
    taps = (tap_rows[:, :, :64] + tap_rows[:, :, 64:]).transpose(1, 0, 2).reshape(12, 256)
    return freq_w, time_w, taps


def to_bands(own, halo):
    both = jnp.concatenate([own.reshape(FR, ROWS, 128), halo.reshape(FR, ROWS, 128)], axis=0)
    mine = both[:, LEAD : LEAD + 64].reshape(2 * FR, 32, 2, 128).transpose(1, 2, 0, 3)
    edge = jnp.stack([both[:, LEAD - 1], both[:, LEAD + 64]], axis=0)[:, None]
    edge = jnp.pad(edge, ((0, 30), (0, 0), (0, 0), (0, 0)))
    return jnp.concatenate([mine, edge], axis=1).reshape(32, 24, 128)


def frame_marks(counts, x_at):
    by_plane = jnp.pad(counts.reshape(4, 32), ((1, 1), (0, 0)))
    window = lax.dynamic_slice(by_plane, (x_at, 0), (3, 32))
    spot = jnp.arange(32)
    halo_count = jnp.where(spot >= 16, window[0], window[2])
    halo_in = jnp.where(spot >= 16, (spot >= 21) & (x_at > 0), (spot <= 10) & (x_at < 3))
    limit = jnp.stack([window[1], halo_count], axis=1)
    valid = (jnp.arange(4) < limit[:, :, None]) & jnp.stack([spot >= 0, halo_in], axis=1)[:, :, None]
    inside = jnp.stack([spot >= 0, halo_in], axis=1)[:, :, None] & (jnp.arange(4) >= 0)
    return jnp.stack([valid.reshape(256), inside.reshape(256)], axis=1).astype(F32)


def to_frames(bands):
    return bands.reshape(3, 32, 8, 128)[:, :, :4].transpose(1, 0, 2, 3).reshape(32, 12, 128)


def from_frames(arrived, plane):
    rows = arrived.reshape(32, 3, FR, 128)
    mine = rows[:, :2].transpose(2, 0, 1, 3).reshape(FR, 64, 128)
    left = jnp.where(plane > 0, rows[0, 2], jnp.zeros((), BF))[:, None]
    right = rows[1, 2][:, None]
    return jnp.concatenate(
        [jnp.zeros((FR, LEAD - 1, 128), BF), left, mine, right, jnp.zeros((FR, ROWS - LEAD - 65, 128), BF)], axis=1
    ).reshape(FR * ROWS, 128)


def to_planes(done, freq_w, freq_t, freq_g, time_w, time_t, time_g):
    rows = done.reshape(FR, ROWS, 128)[:, LEAD : LEAD + 65].reshape(FR * 65, 128)
    rows = jnp.broadcast_to(rows, (4, FR * 65, 128))
    taps = jnp.concatenate([freq_t, time_t], axis=0).reshape(12, 4, 64).transpose(1, 0, 2).reshape(4, 6, 128)
    gains = jnp.broadcast_to(jnp.concatenate([freq_g, time_g], axis=1), (4, 1, 128))
    grads = jnp.concatenate(
        [freq_w.reshape(4, 64, 128), time_w.reshape(4, 64, 128), taps, gains, jnp.zeros((4, 1, 128), F32)], axis=1
    )
    return jnp.concatenate([rows, grads.astype(BF)], axis=1)


def outputs_of(arrived):
    rows = arrived[:, : FR * 65].reshape(4, FR, 65, 128)
    whole = jnp.concatenate([rows[0, :, :64], rows[1, :, :64], rows[2, :, :64], rows[3]], axis=1)
    return whole[:, :, :64].reshape(FR, -1), whole[:, :, 64:].reshape(FR, -1)


def grads_of(total, scale):
    total = total * scale
    taps = total[128:134].reshape(12, 64)
    return (
        total[134, :64],
        total[:64, 64:].T,
        taps[:3],
        total[:64, :64],
        total[134, 64:],
        total[64:128, 64:].T,
        taps[3:].reshape(3, 3, 64),
        total[64:128, :64],
    )


def halo_pairs():
    pairs = []
    for x_at in range(4):
        for spot in range(32):
            if spot <= 10 and x_at < 3:
                pairs.append(((x_at + 1) * 32 + spot, x_at * 32 + spot))
            if spot >= 21 and x_at > 0:
                pairs.append(((x_at - 1) * 32 + spot, x_at * 32 + spot))
    return pairs


SEQ = ("x", "z", "core")


def exchange(values, axes):
    return lax.all_to_all(values, axes, 0, 0)


def shards(
    signal, cotangent, counts, freq_gain, freq_in, freq_taps, freq_out, time_gain, time_in, time_taps, time_out
):
    plane = lax.axis_index("ch")
    x_at = lax.axis_index("x")
    spot = lax.axis_index(("z", "core"))
    grad_scale = 1.0 / math.sqrt(FR * 128 * (signal.shape[1] // 64))
    pair, packed = begin(signal, cotangent, freq_in, freq_taps, freq_out, time_in, time_taps, time_out, plane)
    halo = lax.ppermute(pair, SEQ, halo_pairs())
    gathered = exchange(jnp.broadcast_to(packed, (4,) + packed.shape), "ch")
    freq_w, time_w, taps = unpack(gathered)
    freq_t, time_t = taps[:3], taps[3:]
    gain_f, gain_t = freq_gain[None], time_gain[None]
    x_own, hidden = freq_forward(pair, freq_w, freq_t, gain_f)
    x_halo, _ = freq_forward(halo, freq_w, freq_t, gain_f)
    bands = exchange(to_bands(x_own, x_halo), ("z", "core")).reshape(32, 3, 8, 128)
    marks = frame_marks(counts, x_at)
    edge_share = jnp.where((plane == 3) & (spot == 1), 1.0, 0.0).astype(F32)
    mixed, sums = [], None
    for slot in range(3):
        share = edge_share if slot == 2 else jnp.ones((), F32)
        got = time_path(bands[:, slot].reshape(256, 128), marks, time_w, time_t, gain_t, share)
        mixed.append(got[0])
        sums = got[1:] if sums is None else tuple(a + b for a, b in zip(sums, got[1:]))
    arrived = exchange(to_frames(jnp.stack(mixed)), ("z", "core"))
    back = from_frames(arrived, plane)
    last_plane = jnp.where(plane == 3, 1, 0)
    done, grad_w, grad_t, grad_g = freq_backward(pair, hidden, back, freq_w, freq_t, gain_f, last_plane)
    planes = exchange(to_planes(done, grad_w, grad_t, grad_g, *sums), "ch")
    output, d_signal = outputs_of(planes)
    part = jnp.sum(planes[:, FR * 65 :].astype(F32), axis=0)
    part = jnp.sum(exchange(part.reshape(8, 17, 128), ("x", "core")), axis=0)
    part = jnp.sum(exchange(jnp.broadcast_to(part, (16, 17, 128)), "z"), axis=0)
    total = exchange(jnp.broadcast_to(part, (8, 17, 128)), ("x", "core")).reshape(136, 128)
    return (output, d_signal) + grads_of(total, grad_scale)


def solution(mesh):
    torus = Mesh(mesh.devices.reshape(4, 16, 2, 4), ("x", "z", "core", "ch"))
    return jax.shard_map(
        shards,
        mesh=torus,
        in_specs=(
            P(SEQ, None),
            P(SEQ, None),
            P(),
            P(),
            P(None, "ch"),
            P(None, "ch"),
            P("ch", None),
            P(),
            P(None, "ch"),
            P(None, None, "ch"),
            P("ch", None),
        ),
        out_specs=(
            P(SEQ, None),
            P(SEQ, None),
            P(),
            P(None, "ch"),
            P(None, "ch"),
            P("ch", None),
            P(),
            P(None, "ch"),
            P(None, None, "ch"),
            P("ch", None),
        ),
        check_vma=False,
    )
```

time: 634 us -> 253 us (0.40)
  waiting for transfers between devices: 500 us -> 44.6 us
  local copies, waits for them, and re-layouts: 16.4 us -> 102 us
  starting transfers between devices: 77.2 us -> 41.1 us
  blocking collectives: 0 us -> 20.3 us
  between operations: 14.2 us -> 3.77 us
  other arithmetic: 17.1 us -> 26.1 us
    psum x4 -> x0, waiting for transfers between devices: 460 us -> none  [the longest x1 314 us: shards(): summed = lax.psum(seq_grads, 'seq')]
    concatenate x0 -> x56, local copies, waits for them, and re-layouts: none -> 38.5 us  [the longest x6 17.2 us: groups_on(): return jnp.concatenate([values[split:], head], axis=0)]
    all_to_all x4 -> x5, starting transfers between devices: 76.9 us -> 39.8 us  [exchange(): return lax.all_to_all(values, axes, 0, 0)]
    unnamed x45 -> x518, local copies, waits for them, and re-layouts: 5.62 us -> 32.7 us
    all_to_all x0 -> x2, blocking collectives: none -> 20.3 us  [exchange(): return lax.all_to_all(values, axes, 0, 0)]
    slice x1 -> x78, local copies, waits for them, and re-layouts: 0.02 us -> 19.6 us  [the longest x24 4.76 us: roll_rows(): return jnp.roll(values, amount, 0)]
    reduce_sum x5 -> x43, other arithmetic: 4.81 us -> 14.8 us  [the longest x39 14.5 us: own_rows(): return jnp.sum(jnp.sum(tiles, axis=0)[:4], axis=0, keepdims=True)]
    all_to_all x4 -> x5, waiting for transfers between devices: 40 us -> 44.6 us  [exchange(): return lax.all_to_all(values, axes, 0, 0)]
  transfers between devices with their start and end apart: 8 -> 6, of which waited for: 6 -> 5; matrix products, arithmetic and copies ran while one was open for 3% -> 5% of each run, Pallas kernels for 0% -> 0%
where the time goes in v1:
time: 253 us; the launch traced here: 251 us
  local copies, waits for them, and re-layouts  102 us (40%)
  waiting for transfers between devices  44.6 us (18%)
  starting transfers between devices  41.1 us (16%)
  other arithmetic  26.1 us (10%)
  blocking collectives  20.3 us (8%)
  matrix products  12.8 us (5%)
  between operations  3.77 us (1%)
    all_to_all x5, waiting for transfers between devices, exchange(): return lax.all_to_all(values, axes, 0, 0)  44.6 us
    all_to_all x5, starting transfers between devices, exchange(): return lax.all_to_all(values, axes, 0, 0)  39.8 us
    unnamed x518, local copies, waits for them, and re-layouts  32.7 us
    all_to_all x2, blocking collectives, exchange(): return lax.all_to_all(values, axes, 0, 0)  20.3 us
    concatenate x6, local copies, waits for them, and re-layouts, groups_on(): return jnp.concatenate([values[split:], head], axis=0)  17.2 us
    concatenate x6, local copies, waits for them, and re-layouts, groups_on(): return jnp.concatenate([tail, values[:base]], axis=0)  17 us
    reduce_sum x39, other arithmetic, own_rows(): return jnp.sum(jnp.sum(tiles, axis=0)[:4], axis=0, keepdims=True)  14.5 us
    dot_general x9, matrix products, nt(): lax.dot_general(a, b, (((1,), (1,)), ((), ())), preferred_element_type=F32)  6.76 us
  transfers between devices with their start and end apart: 6, of which 5 were waited for; matrix products, arithmetic and copies ran while one was open for 5% of the time, Pallas kernels for 0%

profile of v1, /device:TPU:1, one launch (start us, length us, event | category | flops | bytes accessed | tf_op | source)
XLA Modules:
  0.0 250.5 jit_solution(4435217329687858830)
XLA Ops:
  0.6 0.9 pad_dynamic-slice_fusion
  2.0 1.3 collective-permute-start
  5.7 5.0 %all-to-all-start = ((bf16[4,144,128]{2,1,0:T(8,128)(2,1)}), bf16[4,144,128]{2,1,0:T(8,128)(2,1)S(1)}, u32[]{:S(2)}, u32[]{:S(2)}) async-start(bf16[4,144,128]{2,1,0:T(8,128)(2,1)} %broadcast_in_dim.42), calls=%async_computation | async-start | bytes 294912 | tf_op jit(solution)/shard_map/all_to_all | solution.py:307
  12.8 2.9 %all-to-all-done = bf16[4,144,128]{2,1,0:T(8,128)(2,1)S(1)} async-done(((bf16[4,144,128]{2,1,0:T(8,128)(2,1)}), bf16[4,144,128]{2,1,0:T(8,128)(2,1)S(1)}, u32[]{:S(2)}, u32[]{:S(2)}) %all-to-all-start) | async-done | bytes 147488 | tf_op jit(solution)/shard_map/all_to_all | solution.py:307
  20.4 18.1 %all-to-all-start.1 = ((bf16[32,24,128]{2,1,0:T(8,128)(2,1)}), bf16[32,24,128]{2,1,0:T(8,128)(2,1)S(1)}, u32[]{:S(2)}, u32[]{:S(2)}) async-start(bf16[32,24,128]{2,1,0:T(8,128)(2,1)} %fusion.77), calls=%async_computation.1 | async-start | bytes 393216 | tf_op jit(solution)/shard_map/all_to_all | solution.py:307
  42.8 14.2 %all-to-all-done.1 = bf16[32,24,128]{2,1,0:T(8,128)(2,1)S(1)} async-done(((bf16[32,24,128]{2,1,0:T(8,128)(2,1)}), bf16[32,24,128]{2,1,0:T(8,128)(2,1)S(1)}, u32[]{:S(2)}, u32[]{:S(2)}) %all-to-all-start.1) | async-done | bytes 196640 | tf_op jit(solution)/shard_map/all_to_all | solution.py:307
  58.6 1.0 fusion.188
  59.5 1.0 fusion.182
  65.7 1.0 add_multiply_fusion.5
  66.8 1.0 add_multiply_fusion.2
  70.1 1.0 add_multiply_fusion.8
  72.6 0.8 fusion.250
  76.6 3.8 %concatenate.457 = f32[256,256]{1,0:T(8,128)S(1)} concatenate(f32[4,256]{1,0:T(4,128)} %get-tuple-element.212, f32[4,256]{1,0:T(4,128)} %get-tuple-element.211, f32[4,256]{1,0:T(4,128)} %get-tuple-element.210, f32[4,256]{1,0:T(4,128)} %get-tuple-element.209, f32[4,256]{1,0:T(4,128)} %get-tuple-element.208, f32[4,256]{1,0:T(4,128)} %get-tuple-element.207, ...), dimensions={0} | concatenate | bytes 524288 | tf_op jit(solution)/shard_map/concatenate | solution.py:119
  80.4 6.9 %concatenate.458 = f32[256,256]{1,0:T(8,128)} concatenate(f32[224,256]{1,0:T(8,128)} %get-tuple-element.196, f32[4,256]{1,0:T(4,128)} %get-tuple-element.205, f32[4,256]{1,0:T(4,128)} %get-tuple-element.204, f32[4,256]{1,0:T(4,128)} %get-tuple-element.203, f32[4,256]{1,0:T(4,128)} %get-tuple-element.202, f32[4,256]{1,0:T(4,128)} %get-tuple-element.201, ...), dimensions={0} | concatenate | bytes 524288 | tf_op jit(solution)/shard_map/concatenate | solution.py:110
  87.3 6.8 %concatenate.436 = f32[256,256]{1,0:T(8,128)} concatenate(f32[4,256]{1,0:T(4,128)} %get-tuple-element.284, f32[4,256]{1,0:T(4,128)} %get-tuple-element.283, f32[4,256]{1,0:T(4,128)} %get-tuple-element.282, f32[4,256]{1,0:T(4,128)} %get-tuple-element.281, f32[4,256]{1,0:T(4,128)} %get-tuple-element.280, f32[4,256]{1,0:T(4,128)} %get-tuple-element.279, ...), dimensions={0} | concatenate | bytes 524288 | tf_op jit(solution)/shard_map/concatenate | solution.py:119
  94.1 6.8 %concatenate.437 = f32[256,256]{1,0:T(8,128)} concatenate(f32[224,256]{1,0:T(8,128)} %get-tuple-element.268, f32[4,256]{1,0:T(4,128)} %get-tuple-element.277, f32[4,256]{1,0:T(4,128)} %get-tuple-element.276, f32[4,256]{1,0:T(4,128)} %get-tuple-element.275, f32[4,256]{1,0:T(4,128)} %get-tuple-element.274, f32[4,256]{1,0:T(4,128)} %get-tuple-element.273, ...), dimensions={0} | concatenate | bytes 524288 | tf_op jit(solution)/shard_map/concatenate | solution.py:110
  101.0 2.2 add_convert_fusion.2
  103.3 3.1 %bitcast_reduce_fusion.9 = (f32[8,256]{1,0:T(8,128)}, f32[8,256]{1,0:T(8,128)}, f32[8,256]{1,0:T(8,128)}, f32[256,256]{1,0:T(8,128)S(1)}, f32[8,256]{1,0:T(8,128...) fusion(f32[256,256]{1,0:T(8,128)S(1)} %copy-done.13, ...), kind=kOutput, calls=%fused_computation.138 | convolution fusion | flops 12105728 | bytes 4140032 | tf_op jit(solution)/shard_map/dot_general | solution.py:17
  109.4 3.1 %concatenate.438 = f32[256,256]{1,0:T(8,128)} concatenate(f32[224,256]{1,0:T(8,128)S(1)} %get-tuple-element.265, f32[4,256]{1,0:T(4,128)S(1)} %get-tuple-element.264, f32[4,256]{1,0:T(4,128)S(1)} %get-tuple-element.263, f32[4,256]{1,0:T(4,128)S(1)} %get-tuple-element.262, f32[4,256]{1,0:T(4,128)S(1)} %get-tuple-element.261, f32[4,256]{1,0:T(4,128)S(1)} %get-tuple-element.260, ...), dimensions={0} | concatenate | bytes 524288 | tf_op jit(solution)/shard_map/concatenate | solution.py:110
  112.6 3.1 %concatenate.439 = f32[256,256]{1,0:T(8,128)} concatenate(f32[4,256]{1,0:T(4,128)S(1)} %get-tuple-element.257, f32[4,256]{1,0:T(4,128)S(1)} %get-tuple-element.256, f32[4,256]{1,0:T(4,128)S(1)} %get-tuple-element.255, f32[4,256]{1,0:T(4,128)S(1)} %get-tuple-element.254, f32[4,256]{1,0:T(4,128)S(1)} %get-tuple-element.253, f32[4,256]{1,0:T(4,128)S(1)} %get-tuple-element.252, ...), dimensions={0} | concatenate | bytes 524288 | tf_op jit(solution)/shard_map/concatenate | solution.py:119
  115.7 2.0 bitcast_reduce_fusion.21
  117.8 0.9 copy-done.43
  118.8 1.6 bitcast_reduce_fusion.24
  122.2 0.8 fusion.262
  124.8 3.1 %concatenate.481 = f32[256,256]{1,0:T(8,128)} concatenate(f32[4,256]{1,0:T(4,128)S(1)} %copy-done.168, f32[4,256]{1,0:T(4,128)S(1)} %copy-done.167, f32[4,256]{1,0:T(4,128)S(1)} %copy-done.166, f32[4,256]{1,0:T(4,128)S(1)} %copy-done.165, f32[4,256]{1,0:T(4,128)S(1)} %copy-done.164, f32[4,256]{1,0:T(4,128)S(1)} %copy-done.163, f32[4,256]{1,0:T(4,128)S(1)} %copy-done.162, ...), dimensions={0} | concatenate | bytes 524288 | tf_op jit(solution)/shard_map/concatenate | solution.py:119
  128.0 1.9 bitcast_reduce_fusion.3
  129.9 0.9 copy-done.40
  130.9 0.9 bitcast_reduce_fusion.6
  133.6 0.9 fusion.280
  137.3 1.6 bitcast_reduce_fusion.12
  138.9 0.9 copy-done.38
  139.9 0.9 bitcast_reduce_fusion.15
  143.3 0.8 fusion.242
  152.0 0.9 fusion.2
  153.5 1.3 fusion.34
  155.6 0.9 fusion.151
  156.5 0.9 fusion.161
  168.6 5.4 %all-to-all-start.2 = ((bf16[32,12,128]{2,1,0:T(8,128)(2,1)}), bf16[32,12,128]{2,1,0:T(8,128)(2,1)S(1)}, u32[]{:S(2)}, u32[]{:S(2)}) async-start(bf16[32,12,128]{2,1,0:T(8,128)(2,1)} %copy.226), calls=%async_computation.2 | async-start | bytes 262144 | tf_op jit(solution)/shard_map/all_to_all | solution.py:307
  177.6 12.6 %all-to-all-done.2 = bf16[32,12,128]{2,1,0:T(8,128)(2,1)S(1)} async-done(((bf16[32,12,128]{2,1,0:T(8,128)(2,1)}), bf16[32,12,128]{2,1,0:T(8,128)(2,1)S(1)}, u32[]{:S(2)}, u32[]{:S(2)}) %all-to-all-start.2) | async-done | bytes 98336 | tf_op jit(solution)/shard_map/all_to_all | solution.py:307
  191.7 0.8 copy-done.1
  196.2 9.4 %all_to_all.35 = bf16[4,396,128]{2,1,0:T(8,128)(2,1)S(1)} all-to-all(bf16[4,396,128]{2,1,0:T(8,128)(2,1)S(1)} %concatenate.542), channel_id=1, replica_groups=mesh['x'=4,'z'=16,'core'=2,'ch'=4] {'ch'}, dimensions={0} | all-to-all | bytes 811008 | tf_op jit(solution)/shard_map/all_to_all | solution.py:307
  205.6 11.0 %all_to_all.36 = f32[8,17,128]{2,1,0:T(8,128)S(1)} all-to-all(f32[8,17,128]{2,1,0:T(8,128)S(1)} %reshape.607), channel_id=1, replica_groups=mesh['x'=4,'z'=16,'core'=2,'ch'=4] {'x','core'}, dimensions={0} | all-to-all | bytes 139264 | tf_op jit(solution)/shard_map/all_to_all | solution.py:307
  217.3 3.5 %all-to-all-start.5 = ((f32[16,17,128]{2,1,0:T(8,128)}), f32[16,17,128]{2,1,0:T(8,128)S(1)}, u32[]{:S(2)}, u32[]{:S(2)}) async-start(f32[16,17,128]{2,1,0:T(8,128)} %broadcast_in_dim.55), calls=%async_computation.5 | async-start | bytes 393216 | tf_op jit(solution)/shard_map/all_to_all | solution.py:307
  221.4 11.8 %all-to-all-done.5 = f32[16,17,128]{2,1,0:T(8,128)S(1)} async-done(((f32[16,17,128]{2,1,0:T(8,128)}), f32[16,17,128]{2,1,0:T(8,128)S(1)}, u32[]{:S(2)}, u32[]{:S(2)}) %all-to-all-start.5) | async-done | bytes 139296 | tf_op jit(solution)/shard_map/all_to_all | solution.py:307
  233.9 7.7 %all-to-all-start.6 = ((f32[8,17,128]{2,1,0:T(8,128)}), f32[8,17,128]{2,1,0:T(8,128)S(1)}, u32[]{:S(2)}, u32[]{:S(2)}) async-start(f32[8,17,128]{2,1,0:T(8,128)} %broadcast_in_dim.56), calls=%async_computation.6 | async-start | bytes 196608 | tf_op jit(solution)/shard_map/all_to_all | solution.py:307
  241.8 0.9 reshape.606
  242.6 0.9 reshape.605
  243.5 3.1 %all-to-all-done.6 = f32[8,17,128]{2,1,0:T(8,128)S(1)} async-done(((f32[8,17,128]{2,1,0:T(8,128)}), f32[8,17,128]{2,1,0:T(8,128)S(1)}, u32[]{:S(2)}, u32[]{:S(2)}) %all-to-all-start.6) | async-done | bytes 69664 | tf_op jit(solution)/shard_map/all_to_all | solution.py:307
  (803 shorter events, 74.6 us)
Async XLA Ops:
  1.7 15.9 %copy-start.4 = (bf16[320,64]{0,1:T(8,128)(2,1)}, bf16[320,64]{0,1:T(8,128)(2,1)S(1)}, u32[]{:S(2)}) copy-start(bf16[320,64]{0,1:T(8,128)(2,1)S(1)} %copy.206) | copy-start | bytes 122884
  2.0 10.7 %collective-permute-start = (bf16[320,128]{0,1:T(8,128)(2,1)S(1)}, bf16[320,128]{0,1:T(8,128)(2,1)S(1)}, u32[]{:S(2)}, u32[]{:S(2)}) collective-permute-start(bf16[320,128]{0,1:T(8,128)(2,1)S(1)} %pad_maximum_fusion.36), channel_id=1, source_target_pairs={{128,0},{132,4},{136,8},{140,12},{144,16},{148,20},{152,24},{156,2... | collective-permute-start | bytes 245768 | tf_op jit(solution)/shard_map/ppermute | solution.py:318
  5.7 9.9 %all-to-all-start = ((bf16[4,144,128]{2,1,0:T(8,128)(2,1)}), bf16[4,144,128]{2,1,0:T(8,128)(2,1)S(1)}, u32[]{:S(2)}, u32[]{:S(2)}) async-start(bf16[4,144,128]{2,1,0:T(8,128)(2,1)} %broadcast_in_dim.42), calls=%async_computation | async-start | bytes 294912 | tf_op jit(solution)/shard_map/all_to_all | solution.py:307
  12.1 3.5 %copy-start.82 = (f32[320]{0:T(512)}, f32[320]{0:T(512)S(1)}, u32[]{:S(2)}) copy-start(f32[320]{0:T(512)S(1)} %add_rsqrt_fusion.1) | copy-start | bytes 3844
  15.6 3.2 %copy-start.47 = (bf16[4,64,128]{2,1,0:T(8,128)(2,1)}, bf16[4,64,128]{2,1,0:T(8,128)(2,1)S(1)}, u32[]{:S(2)}) copy-start(bf16[4,64,128]{2,1,0:T(8,128)(2,1)S(1)} %get-tuple-element.381) | copy-start | bytes 196612
  20.4 36.7 %all-to-all-start.1 = ((bf16[32,24,128]{2,1,0:T(8,128)(2,1)}), bf16[32,24,128]{2,1,0:T(8,128)(2,1)S(1)}, u32[]{:S(2)}, u32[]{:S(2)}) async-start(bf16[32,24,128]{2,1,0:T(8,128)(2,1)} %fusion.77), calls=%async_computation.1 | async-start | bytes 393216 | tf_op jit(solution)/shard_map/all_to_all | solution.py:307
  39.7 30.4 %copy-start.105 = (pred[256]{0:T(512)(128)(4,1)}, pred[256]{0:T(512)(128)(4,1)S(1)}, u32[]{:S(2)}) copy-start(pred[256]{0:T(512)(128)(4,1)S(1)} %get-tuple-element.426) | copy-start | bytes 772
  39.7 30.4 %copy-start.107 = (pred[256]{0:T(512)(128)(4,1)}, pred[256]{0:T(512)(128)(4,1)S(1)}, u32[]{:S(2)}) copy-start(pred[256]{0:T(512)(128)(4,1)S(1)} %get-tuple-element.427) | copy-start | bytes 772
  40.3 24.0 %copy-start.84 = (f32[256,1]{0,1:T(1,128)}, f32[256,1]{0,1:T(1,128)S(1)}, u32[]{:S(2)}) copy-start(f32[256,1]{0,1:T(1,128)S(1)} %get-tuple-element.420) | copy-start | bytes 3076
  41.3 29.9 %copy-start.70 = (f32[256]{0:T(256)}, f32[256]{0:T(256)S(1)}, u32[]{:S(2)}) copy-start(f32[256]{0:T(256)S(1)} %mul.1332) | copy-start | bytes 3076
  41.4 29.8 %copy-start.73 = (f32[256]{0:T(256)}, f32[256]{0:T(256)S(1)}, u32[]{:S(2)}) copy-start(f32[256]{0:T(256)S(1)} %mul.1329) | copy-start | bytes 3076
  41.5 29.7 %copy-start.76 = (f32[256]{0:T(256)}, f32[256]{0:T(256)S(1)}, u32[]{:S(2)}) copy-start(f32[256]{0:T(256)S(1)} %mul.1326) | copy-start | bytes 3076
  57.1 6.3 %copy-start.36 = (bf16[256,128]{1,0:T(8,128)(2,1)}, bf16[256,128]{1,0:T(8,128)(2,1)S(1)}, u32[]{:S(2)}) copy-start(bf16[256,128]{1,0:T(8,128)(2,1)S(1)} %get-tuple-element.377) | copy-start | bytes 196612
  66.7 4.6 %copy-start.92 = (f32[4,256]{1,0:T(4,128)}, f32[4,256]{1,0:T(4,128)S(1)}, u32[]{:S(2)}) copy-start(f32[4,256]{1,0:T(4,128)S(1)} %get-tuple-element.213) | copy-start | bytes 12292
  66.7 4.6 %copy-start.93 = (f32[4,256]{1,0:T(4,128)}, f32[4,256]{1,0:T(4,128)S(1)}, u32[]{:S(2)}) copy-start(f32[4,256]{1,0:T(4,128)S(1)} %get-tuple-element.214) | copy-start | bytes 12292
  66.7 4.6 %copy-start.94 = (f32[4,256]{1,0:T(4,128)}, f32[4,256]{1,0:T(4,128)S(1)}, u32[]{:S(2)}) copy-start(f32[4,256]{1,0:T(4,128)S(1)} %get-tuple-element.215) | copy-start | bytes 12292
  66.7 4.6 %copy-start.95 = (f32[4,256]{1,0:T(4,128)}, f32[4,256]{1,0:T(4,128)S(1)}, u32[]{:S(2)}) copy-start(f32[4,256]{1,0:T(4,128)S(1)} %get-tuple-element.216) | copy-start | bytes 12292
  66.7 4.5 %copy-start.20 = (f32[248,256]{1,0:T(8,128)}, f32[248,256]{1,0:T(8,128)S(1)}, u32[]{:S(2)}) copy-start(f32[248,256]{1,0:T(8,128)S(1)} %get-tuple-element.217) | copy-start | bytes 761860
  66.8 4.5 %copy-start.22 = (f32[248,256]{1,0:T(8,128)}, f32[248,256]{1,0:T(8,128)S(1)}, u32[]{:S(2)}) copy-start(f32[248,256]{1,0:T(8,128)S(1)} %get-tuple-element.218) | copy-start | bytes 761860
  75.8 25.1 %copy-start.10 = (f32[256,256]{1,0:T(8,128)}, f32[256,256]{1,0:T(8,128)S(1)}, u32[]{:S(2)}) copy-start(f32[256,256]{1,0:T(8,128)S(1)} %concatenate.478) | copy-start | bytes 786436
  76.6 24.3 %copy-start.11 = (f32[256,256]{1,0:T(8,128)}, f32[256,256]{1,0:T(8,128)S(1)}, u32[]{:S(2)}) copy-start(f32[256,256]{1,0:T(8,128)S(1)} %concatenate.479) | copy-start | bytes 786436
  80.4 20.5 %copy-start.12 = (f32[256,256]{1,0:T(8,128)}, f32[256,256]{1,0:T(8,128)S(1)}, u32[]{:S(2)}) copy-start(f32[256,256]{1,0:T(8,128)S(1)} %concatenate.457) | copy-start | bytes 786436
  112.6 3.2 %copy-start.9 = (f32[256,256]{1,0:T(8,128)S(1)}, f32[256,256]{1,0:T(8,128)}, u32[]{:S(2)}) copy-start(f32[256,256]{1,0:T(8,128)} %fusion.188) | copy-start | bytes 786436
  112.6 3.2 %copy-start.25 = (f32[248,256]{1,0:T(8,128)S(1)}, f32[248,256]{1,0:T(8,128)}, u32[]{:S(2)}) copy-start(f32[248,256]{1,0:T(8,128)} %copy-done.24) | copy-start | bytes 761860
  112.6 3.2 %copy-start.71 = (f32[256]{0:T(256)S(1)}, f32[256]{0:T(256)}, u32[]{:S(2)}) copy-start(f32[256]{0:T(256)} %copy-done.70) | copy-start | bytes 3076
  112.6 3.2 %copy-start.74 = (f32[256]{0:T(256)S(1)}, f32[256]{0:T(256)}, u32[]{:S(2)}) copy-start(f32[256]{0:T(256)} %copy-done.73) | copy-start | bytes 3076
  123.8 4.1 %copy-start.19 = (f32[248,256]{1,0:T(8,128)S(1)}, f32[248,256]{1,0:T(8,128)}, u32[]{:S(2)}) copy-start(f32[248,256]{1,0:T(8,128)} %copy-done.18) | copy-start | bytes 761860
  124.8 3.2 %copy-start.7 = (f32[256,256]{1,0:T(8,128)S(1)}, f32[256,256]{1,0:T(8,128)}, u32[]{:S(2)}) copy-start(f32[256,256]{1,0:T(8,128)} %fusion.182) | copy-start | bytes 786436
  124.8 3.2 %copy-start.17 = (f32[248,256]{1,0:T(8,128)S(1)}, f32[248,256]{1,0:T(8,128)}, u32[]{:S(2)}) copy-start(f32[248,256]{1,0:T(8,128)} %copy-done.16) | copy-start | bytes 761860
  124.8 3.2 %copy-start.72 = (f32[256]{0:T(256)S(1)}, f32[256]{0:T(256)}, u32[]{:S(2)}) copy-start(f32[256]{0:T(256)} %copy-done.70) | copy-start | bytes 3076
  124.8 3.2 %copy-start.75 = (f32[256]{0:T(256)S(1)}, f32[256]{0:T(256)}, u32[]{:S(2)}) copy-start(f32[256]{0:T(256)} %copy-done.73) | copy-start | bytes 3076
  124.8 3.2 %copy-start.87 = (f32[256]{0:T(256)S(1)}, f32[256]{0:T(256)}, u32[]{:S(2)}) copy-start(f32[256]{0:T(256)} %mul.1339) | copy-start | bytes 3076
  144.2 3.1 %copy-start.116 = (f32[8,256]{1,0:T(8,128)S(1)}, f32[8,256]{1,0:T(8,128)}, u32[]{:S(2)}) copy-start(f32[8,256]{1,0:T(8,128)} %get-tuple-element.74) | copy-start | bytes 24580
  144.2 4.8 %copy-start.113 = (f32[8,256]{1,0:T(8,128)S(1)}, f32[8,256]{1,0:T(8,128)}, u32[]{:S(2)}) copy-start(f32[8,256]{1,0:T(8,128)} %get-tuple-element.412) | copy-start | bytes 24580
  145.1 4.6 %copy-start.112 = (f32[8,256]{1,0:T(8,128)S(1)}, f32[8,256]{1,0:T(8,128)}, u32[]{:S(2)}) copy-start(f32[8,256]{1,0:T(8,128)} %get-tuple-element.413) | copy-start | bytes 24580
  145.1 5.2 %copy-start.111 = (f32[8,256]{1,0:T(8,128)S(1)}, f32[8,256]{1,0:T(8,128)}, u32[]{:S(2)}) copy-start(f32[8,256]{1,0:T(8,128)} %get-tuple-element.415) | copy-start | bytes 24580
  145.1 5.7 %copy-start.110 = (f32[8,256]{1,0:T(8,128)S(1)}, f32[8,256]{1,0:T(8,128)}, u32[]{:S(2)}) copy-start(f32[8,256]{1,0:T(8,128)} %get-tuple-element.416) | copy-start | bytes 24580
  145.1 6.3 %copy-start.109 = (f32[8,256]{1,0:T(8,128)S(1)}, f32[8,256]{1,0:T(8,128)}, u32[]{:S(2)}) copy-start(f32[8,256]{1,0:T(8,128)} %get-tuple-element.417) | copy-start | bytes 24580
  145.8 6.1 %copy-start.35 = (bf16[256,256]{1,0:T(8,128)(2,1)S(1)}, bf16[256,256]{1,0:T(8,128)(2,1)}, u32[]{:S(2)}) copy-start(bf16[256,256]{1,0:T(8,128)(2,1)} %get-tuple-element.408) | copy-start | bytes 393220
  145.8 7.1 %copy-start.108 = (pred[256]{0:T(512)(128)(4,1)S(1)}, pred[256]{0:T(512)(128)(4,1)}, u32[]{:S(2)}) copy-start(pred[256]{0:T(512)(128)(4,1)} %copy-done.107) | copy-start | bytes 772
  146.7 9.8 %copy-start.62 = (bf16[256,64]{0,1:T(8,128)(2,1)}, bf16[256,64]{0,1:T(8,128)(2,1)S(1)}, u32[]{:S(2)}) copy-start(bf16[256,64]{0,1:T(8,128)(2,1)S(1)} %copy.265) | copy-start | bytes 98308
  146.7 5.2 %copy-start.28 = (bf16[256,64]{0,1:T(8,128)(2,1)S(1)}, bf16[256,64]{0,1:T(8,128)(2,1)}, u32[]{:S(2)}) copy-start(bf16[256,64]{0,1:T(8,128)(2,1)} %copy-done.27) | copy-start | bytes 98308
  146.7 6.1 %copy-start.46 = (f32[255,256]{1,0:T(8,128)S(1)}, f32[255,256]{1,0:T(8,128)}, u32[]{:S(2)}) copy-start(f32[255,256]{1,0:T(8,128)} %get-tuple-element.161) | copy-start | bytes 783364
  168.6 21.6 %all-to-all-start.2 = ((bf16[32,12,128]{2,1,0:T(8,128)(2,1)}), bf16[32,12,128]{2,1,0:T(8,128)(2,1)S(1)}, u32[]{:S(2)}, u32[]{:S(2)}) async-start(bf16[32,12,128]{2,1,0:T(8,128)(2,1)} %copy.226), calls=%async_computation.2 | async-start | bytes 262144 | tf_op jit(solution)/shard_map/all_to_all | solution.py:307
  174.5 2.9 %copy-start.59 = (f32[256,64]{1,0:T(8,128)S(1)}, f32[256,64]{1,0:T(8,128)}, u32[]{:S(2)}) copy-start(f32[256,64]{1,0:T(8,128)} %fusion.161) | copy-start | bytes 196612
  174.5 2.9 %copy-start.58 = (f32[256,64]{1,0:T(8,128)S(1)}, f32[256,64]{1,0:T(8,128)}, u32[]{:S(2)}) copy-start(f32[256,64]{1,0:T(8,128)} %fusion.151) | copy-start | bytes 196612
  217.3 15.9 %all-to-all-start.5 = ((f32[16,17,128]{2,1,0:T(8,128)}), f32[16,17,128]{2,1,0:T(8,128)S(1)}, u32[]{:S(2)}, u32[]{:S(2)}) async-start(f32[16,17,128]{2,1,0:T(8,128)} %broadcast_in_dim.55), calls=%async_computation.5 | async-start | bytes 393216 | tf_op jit(solution)/shard_map/all_to_all | solution.py:307
  233.9 12.7 %all-to-all-start.6 = ((f32[8,17,128]{2,1,0:T(8,128)}), f32[8,17,128]{2,1,0:T(8,128)S(1)}, u32[]{:S(2)}, u32[]{:S(2)}) async-start(f32[8,17,128]{2,1,0:T(8,128)} %broadcast_in_dim.56), calls=%async_computation.6 | async-start | bytes 196608 | tf_op jit(solution)/shard_map/all_to_all | solution.py:307
  (207 other events, 227.0 us)

commit v2 on v1

--- a/solution.py
+++ b/solution.py
@@ -3,6 +3,8 @@
 import jax
 import jax.numpy as jnp
 from jax import lax
+from jax.experimental import pallas as pl
+from jax.experimental.pallas import tpu as pltpu
 from jax.sharding import Mesh, PartitionSpec as P
 
 EPS = 1e-05
@@ -26,7 +28,7 @@
 
 
 def roll_rows(values, amount):
-    return jnp.roll(values, amount, 0)
+    return pltpu.roll(values, amount % values.shape[0], 0)
 
 
 def sigmoid(values):
@@ -47,88 +49,113 @@
     return taps[0:1] * roll_rows(values, 1) + taps[1:2] * values + taps[2:3] * roll_rows(values, -1)
 
 
-def freq_forward(pair, weights, taps, gain):
-    features = pair[:, :64].astype(F32)
+HALVES = (slice(0, 128), slice(128, 256))
+
+
+def freq_forward_kernel(own_ref, halo_ref, weight_ref, taps_ref, gain_ref, own_out, halo_out, hidden_out):
+    gain = gain_ref[...]
+    for pair_ref, out_ref in ((own_ref, own_out), (halo_ref, halo_out)):
+        features = pair_ref[:, :64].astype(F32)
+        normed = (features * inverse_norm(features) * gain).astype(BF)
+        mixed = features
+        for lanes in HALVES:
+            hidden = nt(normed, weight_ref[lanes, :64])
+            if out_ref is own_out:
+                hidden_out[:, lanes] = hidden
+            drive = bins_conv(hidden, taps_ref[:, lanes])
+            active = (drive * sigmoid(drive)).astype(BF)
+            mixed = mixed + nn(active, weight_ref[lanes, 64:])
+        out_ref[:, :64] = mixed.astype(BF)
+        out_ref[:, 64:] = pair_ref[:, 64:]
+
+
+def freq_forward(pair, halo, weights, taps, gain):
+    rows = pair.shape[0]
+    return pl.pallas_call(
+        freq_forward_kernel,
+        out_shape=(
+            jax.ShapeDtypeStruct((rows, 128), BF),
+            jax.ShapeDtypeStruct((rows, 128), BF),
+            jax.ShapeDtypeStruct((rows, 256), F32),
+        ),
+        name="freq_forward",
+    )(pair, halo, weights, taps, gain)
+
+
+def freq_backward_kernel(flag_ref, pair_ref, hidden_ref, back_ref, weight_ref, taps_ref, gain_ref, out_ref, grad_ref, tap_ref, gain_out):
+    gain = gain_ref[...]
+    row = lax.broadcasted_iota(jnp.int32, (ROWS, 1), 0)
+    upper = LEAD + 64 + flag_ref[0]
+    one = jnp.where((row >= LEAD) & (row < upper), 1.0, 0.0).astype(F32)
+    own = jnp.concatenate([one] * FR, axis=0)
+    features = pair_ref[:, :64].astype(F32)
     scale = inverse_norm(features)
-    normed = (features * scale * gain).astype(BF)
-    hidden = nt(normed, weights[:, :64])
-    drive = bins_conv(hidden, taps)
-    active = (drive * sigmoid(drive)).astype(BF)
-    mixed = nn(active, weights[:, 64:])
-    x_one = (features + mixed).astype(BF)
-    return jnp.concatenate([x_one, pair[:, 64:]], axis=1), hidden
-
-
-def own_bins(last_plane):
-    row = lax.broadcasted_iota(jnp.int32, (ROWS, 1), 0)
-    upper = LEAD + 64 + last_plane
-    one = jnp.where((row >= LEAD) & (row < upper), 1.0, 0.0).astype(F32)
-    return jnp.concatenate([one] * FR, axis=0)
+    grad = back_ref[:, 64:]
+    grad_wide = grad.astype(F32)
+    grad_own = (grad_wide * own).astype(BF)
+    normed = (features * scale * gain * own).astype(BF)
+    d_normed = None
+    for lanes in HALVES:
+        taps = taps_ref[:, lanes]
+        hidden = hidden_ref[:, lanes]
+        before, after = roll_rows(hidden, 1), roll_rows(hidden, -1)
+        drive = taps[0:1] * before + taps[1:2] * hidden + taps[2:3] * after
+        gate = sigmoid(drive)
+        active = drive * gate
+        slope = gate + active * (1.0 - gate)
+        grad_ref[lanes, :64] = tn(active.astype(BF), grad_own)
+        d_drive = nt(grad, weight_ref[lanes, 64:]) * slope
+        d_own = d_drive * own
+        tap_ref[0:1, lanes] = jnp.sum(d_own * before, axis=0, keepdims=True)
+        tap_ref[1:2, lanes] = jnp.sum(d_own * hidden, axis=0, keepdims=True)
+        tap_ref[2:3, lanes] = jnp.sum(d_own * after, axis=0, keepdims=True)
+        d_hidden = (
+            taps[0:1] * roll_rows(d_drive, -1) + taps[1:2] * d_drive + taps[2:3] * roll_rows(d_drive, 1)
+        ).astype(BF)
+        grad_ref[lanes, 64:] = tn(d_hidden, normed)
+        part = nn(d_hidden, weight_ref[lanes, :64])
+        d_normed = part if d_normed is None else d_normed + part
+    gain_out[...] = jnp.sum(d_normed * features * (scale * own), axis=0, keepdims=True)
+    out_ref[:, :64] = back_ref[:, :64]
+    out_ref[:, 64:] = (grad_wide + norm_back(d_normed, features, scale, gain)).astype(BF)
 
 
 def freq_backward(pair, hidden, back, weights, taps, gain, last_plane):
-    own = own_bins(last_plane)
-    features = pair[:, :64].astype(F32)
-    scale = inverse_norm(features)
-    grad = back[:, 64:]
-    grad_own = grad.astype(F32) * own
-    normed = (features * scale * gain * own).astype(BF)
-    drive = bins_conv(hidden, taps)
-    gate = sigmoid(drive)
-    active = drive * gate
-    slope = gate + active * (1.0 - gate)
-    grad_out = tn(active.astype(BF), grad_own.astype(BF))
-    d_drive = nt(grad, weights[:, 64:]) * slope
-    d_own = d_drive * own
-    tap_rows = [
-        jnp.sum(d_own * roll_rows(hidden, 1), axis=0, keepdims=True),
-        jnp.sum(d_own * hidden, axis=0, keepdims=True),
-        jnp.sum(d_own * roll_rows(hidden, -1), axis=0, keepdims=True),
-    ]
-    d_hidden = (
-        taps[0:1] * roll_rows(d_drive, -1) + taps[1:2] * d_drive + taps[2:3] * roll_rows(d_drive, 1)
-    ).astype(BF)
-    grad_in = tn(d_hidden, normed)
-    d_normed = nn(d_hidden, weights[:, :64])
-    grad_gain = jnp.sum(d_normed * features * scale * own, axis=0, keepdims=True)
-    d_signal = (grad.astype(F32) + norm_back(d_normed, features, scale, gain)).astype(BF)
-    return (
-        jnp.concatenate([back[:, :64], d_signal], axis=1),
-        jnp.concatenate([grad_out, grad_in], axis=1),
-        jnp.concatenate(tap_rows, axis=0),
-        grad_gain,
+    vmem = pl.BlockSpec(memory_space=pltpu.VMEM)
+    return pl.pallas_call(
+        freq_backward_kernel,
+        out_shape=(
+            jax.ShapeDtypeStruct(pair.shape, BF),
+            jax.ShapeDtypeStruct((256, 128), F32),
+            jax.ShapeDtypeStruct((3, 256), F32),
+            jax.ShapeDtypeStruct((1, 64), F32),
+        ),
+        in_specs=[pl.BlockSpec(memory_space=pltpu.SMEM)] + [vmem] * 6,
+        name="freq_backward",
+    )(last_plane.reshape(1), pair, hidden, back, weights, taps, gain)
+
+
+def turned(tiles):
+    return jnp.concatenate(
+        [roll_rows(tiles[8 * i : 8 * i + 8], 4) for i in range(tiles.shape[0] // 8)], axis=0
     )
 
 
 def groups_on(values, count):
-    split = 8 * abs(count)
     if count > 0:
-        head = jnp.concatenate(
-            [jnp.concatenate([values[8 * i + 4 : 8 * i + 8], values[8 * i : 8 * i + 4]], axis=0) for i in range(count)],
-            axis=0,
-        )
-        return jnp.concatenate([values[split:], head], axis=0)
-    base = values.shape[0] - split
-    tail = jnp.concatenate(
-        [
-            jnp.concatenate([values[base + 8 * i + 4 : base + 8 * i + 8], values[base + 8 * i : base + 8 * i + 4]], axis=0)
-            for i in range(-count)
-        ],
-        axis=0,
-    )
-    return jnp.concatenate([tail, values[:base]], axis=0)
-
-
-def later(values, spacing):
+        return jnp.concatenate([values[8 * count :], turned(values[: 8 * count])], axis=0)
+    base = values.shape[0] + 8 * count
+    return jnp.concatenate([turned(values[base:]), values[:base]], axis=0)
+
+
+def later(values, spacing, place):
     if spacing == 1:
-        place = lax.broadcasted_iota(jnp.int32, values.shape, 0) & 3
         return jnp.where(place == 3, roll_rows(groups_on(values, 1), 3), roll_rows(values, -1))
     return groups_on(values, spacing // FR)
 
 
-def earlier(values, spacing):
+def earlier(values, spacing, place):
     if spacing == 1:
-        place = lax.broadcasted_iota(jnp.int32, values.shape, 0) & 3
         return jnp.where(place == 0, roll_rows(groups_on(values, -1), -3), roll_rows(values, 1))
     return groups_on(values, -(spacing // FR))
 
@@ -138,57 +165,97 @@
     return jnp.sum(jnp.sum(tiles, axis=0)[:4], axis=0, keepdims=True)
 
 
-def time_path(pair, marks, weights, taps, gain, share):
-    valid, inside = marks[:, 0:1], marks[:, 1:2]
-    place = lax.broadcasted_iota(jnp.int32, (pair.shape[0], 1), 0) & 7
-    counted = jnp.where(place < 4, share, 0.0).astype(F32)
-    features = pair[:, :64].astype(F32)
-    grad = pair[:, 64:]
+def time_kernel(flag_ref, pair_ref, marks_ref, weight_ref, taps_ref, gain_ref, out_ref, grad_ref, tap_ref, gain_out):
+    slot = pl.program_id(0)
+    share = jnp.where((slot < 2) | (flag_ref[0] > 0), 1.0, 0.0).astype(F32)
+
+    @pl.when(slot == 0)
+    def _():
+        grad_ref[...] = jnp.zeros_like(grad_ref)
+        tap_ref[...] = jnp.zeros_like(tap_ref)
+        gain_out[...] = jnp.zeros_like(gain_out)
+
+    pair = pair_ref[:, 0].astype(F32).reshape(256, 128)
+    gain = gain_ref[...]
+    valid, inside = marks_ref[:, 0:1], marks_ref[:, 1:2]
+    spot = lax.broadcasted_iota(jnp.int32, (256, 1), 0)
+    counted = jnp.where((spot & 7) < 4, share, 0.0).astype(F32)
+    place = lax.broadcasted_iota(jnp.int32, (256, 128), 0) & 3
+    features, grad_wide = pair[:, :64], pair[:, 64:]
+    grad = grad_wide.astype(BF)
+    grad_own = (grad_wide * counted).astype(BF)
     scale = inverse_norm(features)
     normed = features * scale * gain
-    weight_in, weight_out = weights[:, :64], weights[:, 64:]
-    state = nt(normed.astype(BF), weight_in) * valid
-    states, slopes = [], []
-    for layer in range(3):
-        spacing = (1, 4, 16)[layer]
-        row = taps[3 * layer : 3 * layer + 3]
-        drive = row[0:1] * earlier(state, spacing) + row[1:2] * state + row[2:3] * later(state, spacing)
-        gate = sigmoid(drive)
-        active = drive * gate
-        states.append(state)
-        slopes.append(gate + active * (1.0 - gate))
-        state = state + active
-        if layer < 2:
-            state = state * inside
-    top = state.astype(BF)
-    output = (features + nn(top, weight_out)).astype(BF)
-    grad_out = tn(top, (grad.astype(F32) * counted).astype(BF))
-    d_state = nt(grad, weight_out)
-    tap_rows = [None] * 9
-    for layer in reversed(range(3)):
-        spacing = (1, 4, 16)[layer]
-        row = taps[3 * layer : 3 * layer + 3]
-        d_drive = d_state * slopes[layer]
-        if layer < 2:
-            d_drive = d_drive * inside
-        held = states[layer]
-        tap_rows[3 * layer] = own_rows(d_drive * earlier(held, spacing))
-        tap_rows[3 * layer + 1] = own_rows(d_drive * held)
-        tap_rows[3 * layer + 2] = own_rows(d_drive * later(held, spacing))
-        d_state = d_state + (
-            row[0:1] * later(d_drive, spacing) + row[1:2] * d_drive + row[2:3] * earlier(d_drive, spacing)
-        )
-    d_pre = (d_state * valid).astype(BF)
-    grad_in = tn(d_pre, (normed * counted).astype(BF))
-    d_normed = nn(d_pre, weight_in)
-    grad_gain = own_rows(d_normed * features * scale) * share
-    d_one = (grad.astype(F32) + norm_back(d_normed, features, scale, gain)).astype(BF)
-    return (
-        jnp.concatenate([output, d_one], axis=1),
-        jnp.concatenate([grad_out, grad_in], axis=1),
-        jnp.concatenate(tap_rows, axis=0) * share,
-        grad_gain,
-    )
+    normed_own = (normed * counted).astype(BF)
+    normed = normed.astype(BF)
+    mixed, d_normed = features, None
+    for lanes in HALVES:
+        weight_in, weight_out = weight_ref[lanes, :64], weight_ref[lanes, 64:]
+        state = nt(normed, weight_in) * valid
+        states, slopes = [], []
+        for layer in range(3):
+            spacing = (1, 4, 16)[layer]
+            row = taps_ref[3 * layer : 3 * layer + 3, lanes]
+            drive = (
+                row[0:1] * earlier(state, spacing, place) + row[1:2] * state + row[2:3] * later(state, spacing, place)
+            )
+            gate = sigmoid(drive)
+            active = drive * gate
+            states.append(state)
+            slopes.append(gate + active * (1.0 - gate))
+            state = state + active
+            if layer < 2:
+                state = state * inside
+        top = state.astype(BF)
+        mixed = mixed + nn(top, weight_out)
+        grad_ref[lanes, :64] += tn(top, grad_own)
+        d_state = nt(grad, weight_out)
+        for layer in reversed(range(3)):
+            spacing = (1, 4, 16)[layer]
+            row = taps_ref[3 * layer : 3 * layer + 3, lanes]
+            d_drive = d_state * slopes[layer]
+            if layer < 2:
+                d_drive = d_drive * inside
+            held = states[layer]
+            for j, moved in enumerate((earlier(held, spacing, place), held, later(held, spacing, place))):
+                tap_ref[3 * layer + j : 3 * layer + j + 1, lanes] += own_rows(d_drive * moved) * share
+            d_state = d_state + (
+                row[0:1] * later(d_drive, spacing, place)
+                + row[1:2] * d_drive
+                + row[2:3] * earlier(d_drive, spacing, place)
+            )
+        d_pre = (d_state * valid).astype(BF)
+        grad_ref[lanes, 64:] += tn(d_pre, normed_own)
+        part = nn(d_pre, weight_in)
+        d_normed = part if d_normed is None else d_normed + part
+    gain_out[...] += own_rows(d_normed * features * scale) * share
+    d_one = grad_wide + norm_back(d_normed, features, scale, gain)
+    out_ref[:, 0] = jnp.concatenate([mixed, d_one], axis=1).reshape(32, 8, 128).astype(BF)
+
+
+def time_path(bands, marks, weights, taps, gain, flag):
+    whole = lambda shape: pl.BlockSpec(shape, lambda slot: (0, 0))
+    slots = pl.BlockSpec((32, 1, 8, 128), lambda slot: (0, slot, 0, 0))
+    return pl.pallas_call(
+        time_kernel,
+        grid=(3,),
+        out_shape=(
+            jax.ShapeDtypeStruct((32, 3, 8, 128), BF),
+            jax.ShapeDtypeStruct((256, 128), F32),
+            jax.ShapeDtypeStruct((9, 256), F32),
+            jax.ShapeDtypeStruct((1, 64), F32),
+        ),
+        in_specs=[
+            pl.BlockSpec(memory_space=pltpu.SMEM),
+            slots,
+            whole((256, 2)),
+            whole((256, 128)),
+            whole((9, 256)),
+            whole((1, 64)),
+        ],
+        out_specs=(slots, whole((256, 128)), whole((9, 256)), whole((1, 64))),
+        name="time_path",
+    )(flag.reshape(1), bands, marks, weights, taps, gain)
 
 
 def plane_rows(values, plane):
@@ -244,7 +311,7 @@
 
 
 def to_frames(bands):
-    return bands.reshape(3, 32, 8, 128)[:, :, :4].transpose(1, 0, 2, 3).reshape(32, 12, 128)
+    return bands[:, :, :4].reshape(32, 12, 128)
 
 
 def from_frames(arrived, plane):
@@ -320,18 +387,12 @@
     freq_w, time_w, taps = unpack(gathered)
     freq_t, time_t = taps[:3], taps[3:]
     gain_f, gain_t = freq_gain[None], time_gain[None]
-    x_own, hidden = freq_forward(pair, freq_w, freq_t, gain_f)
-    x_halo, _ = freq_forward(halo, freq_w, freq_t, gain_f)
+    x_own, x_halo, hidden = freq_forward(pair, halo, freq_w, freq_t, gain_f)
     bands = exchange(to_bands(x_own, x_halo), ("z", "core")).reshape(32, 3, 8, 128)
     marks = frame_marks(counts, x_at)
-    edge_share = jnp.where((plane == 3) & (spot == 1), 1.0, 0.0).astype(F32)
-    mixed, sums = [], None
-    for slot in range(3):
-        share = edge_share if slot == 2 else jnp.ones((), F32)
-        got = time_path(bands[:, slot].reshape(256, 128), marks, time_w, time_t, gain_t, share)
-        mixed.append(got[0])
-        sums = got[1:] if sums is None else tuple(a + b for a, b in zip(sums, got[1:]))
-    arrived = exchange(to_frames(jnp.stack(mixed)), ("z", "core"))
+    edge = jnp.where((plane == 3) & (spot == 1), 1, 0)
+    mixed, *sums = time_path(bands, marks, time_w, time_t, gain_t, edge)
+    arrived = exchange(to_frames(mixed), ("z", "core"))
     back = from_frames(arrived, plane)
     last_plane = jnp.where(plane == 3, 1, 0)
     done, grad_w, grad_t, grad_g = freq_backward(pair, hidden, back, freq_w, freq_t, gain_f, last_plane)

time: 253 us -> 154 us (0.61)
  local copies, waits for them, and re-layouts: 102 us -> 24.2 us
  other arithmetic: 26.1 us -> 2.18 us
  matrix products: 12.8 us -> 0 us
  Pallas kernels: 0 us -> 12.4 us
  waiting for transfers between devices: 44.6 us -> 51.7 us
  between operations: 3.77 us -> 1.17 us
    concatenate x53 -> x0, local copies, waits for them, and re-layouts: 37.7 us -> none  [the longest x6 17.2 us: groups_on(): return jnp.concatenate([values[split:], head], axis=0)]
    unnamed x518 -> x42, local copies, waits for them, and re-layouts: 32.7 us -> 7.06 us
    slice x67 -> x8, local copies, waits for them, and re-layouts: 17.8 us -> 2.36 us  [the longest x6 1.39 us: shards(): freq_t, time_t = (taps[:3], taps[3:])]
    reduce_sum x45 -> x0, other arithmetic: 14.8 us -> none  [the longest x39 14.5 us: own_rows(): return jnp.sum(jnp.sum(tiles, axis=0)[:4], axis=0, keepdims=True)]
    pallas_call x0 -> x3, Pallas kernels: none -> 12.4 us  [the longest x1 7.06 us: time_path(): pl.pallas_call(time_kernel, grid=(3,), out_shape=(jax.ShapeDtypeStruct((3...]
    dot_general x20 -> x0, matrix products: 10.1 us -> none  [the longest x9 6.76 us: nt(): lax.dot_general(a, b, (((1,), (1,)), ((), ())), preferred_element_type=F32)]
    all_to_all x5, waiting for transfers between devices: 44.6 us -> 51.7 us  [exchange(): return lax.all_to_all(values, axes, 0, 0)]
    convert_element_type x5 -> x0, other arithmetic: 4.04 us -> none  [the longest x1 2.21 us: time_path(): top = state.astype(BF)]
where the time goes in v2:
time: 154 us; the launch traced here: 153 us
  waiting for transfers between devices  51.7 us (34%)
  starting transfers between devices  40.8 us (26%)
  local copies, waits for them, and re-layouts  24.2 us (16%)
  blocking collectives  20.3 us (13%)
  Pallas kernels  12.4 us (8%)
  other arithmetic  2.18 us (1%)
    all_to_all x5, waiting for transfers between devices, exchange(): return lax.all_to_all(values, axes, 0, 0)  51.7 us
    all_to_all x5, starting transfers between devices, exchange(): return lax.all_to_all(values, axes, 0, 0)  39.5 us
    all_to_all x2, blocking collectives, exchange(): return lax.all_to_all(values, axes, 0, 0)  20.3 us
    pallas_call x1, Pallas kernels, time_path(): pl.pallas_call(time_kernel, grid=(3,), out_shape=(jax.ShapeDtypeStruct((3...  7.06 us
    unnamed x42, local copies, waits for them, and re-layouts  7.06 us
  transfers between devices with their start and end apart: 6, of which 5 were waited for; matrix products, arithmetic and copies ran while one was open for 5% of the time, Pallas kernels for 0%

profile of v2, /device:TPU:1, one launch (start us, length us, event | category | flops | bytes accessed | tf_op | source)
XLA Modules:
  0.0 152.7 jit_solution(6215875043236711153)
XLA Ops:
  0.6 0.9 pad_dynamic-slice_fusion
  1.9 1.3 collective-permute-start
  3.3 0.6 copy-done.11
  4.0 0.6 copy-done.13
  4.7 0.6 copy-done.7
  5.5 0.7 broadcast_in_dim.41
  6.2 5.0 %all-to-all-start = ((bf16[4,144,128]{2,1,0:T(8,128)(2,1)}), bf16[4,144,128]{2,1,0:T(8,128)(2,1)S(1)}, u32[]{:S(2)}, u32[]{:S(2)}) async-start(bf16[4,144,128]{2,1,0:T(8,128)(2,1)} %broadcast_in_dim.41), calls=%async_computation | async-start | bytes 294912 | tf_op jit(solution)/shard_map/all_to_all | solution.py:374
  11.2 0.7 copy-done.14
  11.9 4.1 %all-to-all-done = bf16[4,144,128]{2,1,0:T(8,128)(2,1)S(1)} async-done(((bf16[4,144,128]{2,1,0:T(8,128)(2,1)}), bf16[4,144,128]{2,1,0:T(8,128)(2,1)S(1)}, u32[]{:S(2)}, u32[]{:S(2)}) %all-to-all-start) | async-done | bytes 147488 | tf_op jit(solution)/shard_map/all_to_all | solution.py:374
  16.1 0.7 fusion.11
  16.8 0.7 slice.118.taps_ref
  17.5 0.6 copy-done.4
  18.2 2.6 %freq_forward.1 = (bf16[320,128]{1,0:T(8,128)(2,1)}, bf16[320,128]{1,0:T(8,128)(2,1)}, f32[320,256]{1,0:T(8,128)}) custom-call(bf16[320,128]{1,0:T(8,128)(2,1)} %copy-done.1, bf16[320,128]{1,0:T(8,128)(2,1)} %copy-done.4, bf16[256,128]{1,0:T(8,128)(2,1)} %bitcast.70, f32[3,256]{1,0:T(4,128)} %slice.118.taps_ref, f32[1,64]{1,0:T(1,128)} %bitcast.90), custom_call_target="tpu_custom_call" | custom-call | tf_op jit(solution)/shard_map/freq_forward/pallas_call | solution.py:74
  20.8 1.0 copy.137
  21.9 0.7 maximum_bitcast_fusion
  22.6 18.1 %all-to-all-start.1 = ((bf16[32,24,128]{2,1,0:T(8,128)(2,1)}), bf16[32,24,128]{2,1,0:T(8,128)(2,1)S(1)}, u32[]{:S(2)}, u32[]{:S(2)}) async-start(bf16[32,24,128]{2,1,0:T(8,128)(2,1)} %maximum_bitcast_fusion), calls=%async_computation.1 | async-start | bytes 393216 | tf_op jit(solution)/shard_map/all_to_all | solution.py:374
  41.6 0.8 copy.143.marks_ref
  42.4 0.7 slice.127.taps_ref
  43.1 16.5 %all-to-all-done.1 = bf16[32,24,128]{2,1,0:T(8,128)(2,1)S(1)} async-done(((bf16[32,24,128]{2,1,0:T(8,128)(2,1)}), bf16[32,24,128]{2,1,0:T(8,128)(2,1)S(1)}, u32[]{:S(2)}, u32[]{:S(2)}) %all-to-all-start.1) | async-done | bytes 196640 | tf_op jit(solution)/shard_map/all_to_all | solution.py:374
  59.6 0.7 copy-done
  60.2 7.1 %time_path.1 = (bf16[32,3,8,128]{3,2,1,0:T(8,128)(2,1)}, f32[256,128]{1,0:T(8,128)}, f32[9,256]{1,0:T(8,128)}, f32[1,64]{1,0:T(1,128)}) custom-call(s32[1]{0:T(128)} %bitcast.6.flag_ref, bf16[32,3,8,128]{3,2,1,0:T(8,128)(2,1)} %bitcast.69, f32[256,2]{1,0:T(8,128)} %copy.143.marks_ref, bf16[256,128]{1,0:T(8,128)(2,1)} %bitcast.82, f32[9,256]{1,0:T(8,128)} %slice.127.taps_ref, ...), custom_call_target="tpu_custom_call" | custom-call | tf_op jit(solution)/shard_map/time_path/pallas_call | solution.py:239
  67.3 1.0 slice.128
  68.3 0.7 copy.145
  69.0 5.1 %all-to-all-start.2 = ((bf16[32,12,128]{2,1,0:T(8,128)(2,1)}), bf16[32,12,128]{2,1,0:T(8,128)(2,1)S(1)}, u32[]{:S(2)}, u32[]{:S(2)}) async-start(bf16[32,12,128]{2,1,0:T(8,128)(2,1)} %copy.145), calls=%async_computation.2 | async-start | bytes 262144 | tf_op jit(solution)/shard_map/all_to_all | solution.py:374
  74.1 16.1 %all-to-all-done.2 = bf16[32,12,128]{2,1,0:T(8,128)(2,1)S(1)} async-done(((bf16[32,12,128]{2,1,0:T(8,128)(2,1)}), bf16[32,12,128]{2,1,0:T(8,128)(2,1)S(1)}, u32[]{:S(2)}, u32[]{:S(2)}) %all-to-all-start.2) | async-done | bytes 98336 | tf_op jit(solution)/shard_map/all_to_all | solution.py:374
  90.4 1.9 %concatenate.54 = bf16[4,80,128]{2,1,0:T(8,128)(2,1)} concatenate(bf16[4,7,128]{2,1,0:T(8,128)(2,1)S(1)} %broadcast.102, bf16[4,1,128]{2,1,0:T(2,128)(2,1)S(1)} %get-tuple-element.112, bf16[4,64,128]{2,1,0:T(8,128)(2,1)S(1)} %bitcast.83, bf16[4,1,128]{2,1,0:T(2,128)(2,1)S(1)} %get-tuple-element.111, bf16[4,7,128]{2,1,0:T(8,128)(2,1)S(1)} %broadcast.102), dimensions={1} | concatenate | bytes 163840 | tf_op jit(solution)/shard_map/concatenate | solution.py:322
  92.3 2.8 %freq_backward.1 = (bf16[320,128]{1,0:T(8,128)(2,1)}, f32[256,128]{1,0:T(8,128)}, f32[3,256]{1,0:T(4,128)}, f32[1,64]{1,0:T(1,128)}) custom-call(s32[1]{0:T(128)} %bitcast.flag_ref, bf16[320,128]{1,0:T(8,128)(2,1)} %copy-done.1, f32[320,256]{1,0:T(8,128)} %get-tuple-element.21.hidden_ref, bf16[320,128]{1,0:T(8,128)(2,1)} %bitcast.74, ...), custom_call_target="tpu_custom_call" | custom-call | tf_op jit(solution)/shard_map/freq_backward/pallas_call | solution.py:125
  95.1 0.7 convert.34
  96.0 0.9 copy-done.3
  96.9 0.6 copy-done.15
  97.7 0.7 concatenate.58
  98.4 9.4 %all_to_all.35 = bf16[4,396,128]{2,1,0:T(8,128)(2,1)S(1)} all-to-all(bf16[4,396,128]{2,1,0:T(8,128)(2,1)S(1)} %concatenate.58), channel_id=1, replica_groups=mesh['x'=4,'z'=16,'core'=2,'ch'=4] {'ch'}, dimensions={0} | all-to-all | bytes 811008 | tf_op jit(solution)/shard_map/all_to_all | solution.py:374
  107.8 11.0 %all_to_all.36 = f32[8,17,128]{2,1,0:T(8,128)S(1)} all-to-all(f32[8,17,128]{2,1,0:T(8,128)S(1)} %reshape.245), channel_id=1, replica_groups=mesh['x'=4,'z'=16,'core'=2,'ch'=4] {'x','core'}, dimensions={0} | all-to-all | bytes 139264 | tf_op jit(solution)/shard_map/all_to_all | solution.py:374
  118.8 0.7 broadcast_in_dim.49
  119.5 3.5 %all-to-all-start.5 = ((f32[16,17,128]{2,1,0:T(8,128)}), f32[16,17,128]{2,1,0:T(8,128)S(1)}, u32[]{:S(2)}, u32[]{:S(2)}) async-start(f32[16,17,128]{2,1,0:T(8,128)} %broadcast_in_dim.49), calls=%async_computation.5 | async-start | bytes 393216 | tf_op jit(solution)/shard_map/all_to_all | solution.py:374
  123.2 0.3 fusion.10
  123.7 11.8 %all-to-all-done.5 = f32[16,17,128]{2,1,0:T(8,128)S(1)} async-done(((f32[16,17,128]{2,1,0:T(8,128)}), f32[16,17,128]{2,1,0:T(8,128)S(1)}, u32[]{:S(2)}, u32[]{:S(2)}) %all-to-all-start.5) | async-done | bytes 139296 | tf_op jit(solution)/shard_map/all_to_all | solution.py:374
  135.5 0.6 broadcast_in_dim.50
  136.1 7.7 %all-to-all-start.6 = ((f32[8,17,128]{2,1,0:T(8,128)}), f32[8,17,128]{2,1,0:T(8,128)S(1)}, u32[]{:S(2)}, u32[]{:S(2)}) async-start(f32[8,17,128]{2,1,0:T(8,128)} %broadcast_in_dim.50), calls=%async_computation.6 | async-start | bytes 196608 | tf_op jit(solution)/shard_map/all_to_all | solution.py:374
  144.0 0.9 reshape.243
  144.8 0.9 reshape.244
  145.7 3.1 %all-to-all-done.6 = f32[8,17,128]{2,1,0:T(8,128)S(1)} async-done(((f32[8,17,128]{2,1,0:T(8,128)}), f32[8,17,128]{2,1,0:T(8,128)S(1)}, u32[]{:S(2)}, u32[]{:S(2)}) %all-to-all-start.6) | async-done | bytes 69664 | tf_op jit(solution)/shard_map/all_to_all | solution.py:374
  148.9 0.6 fusion.12
  149.6 0.6 slice.176
  150.2 0.6 slice_bitcast_fusion.4
  150.7 0.7 copy.153
  151.4 0.7 copy.154
  152.1 0.6 reshape.247
  (100 shorter events, 2.9 us)
Async XLA Ops:
  1.8 1.4 copy-start.12
  1.8 1.4 copy-start.10
  1.9 3.6 %copy-start.1 = (bf16[320,128]{1,0:T(8,128)(2,1)}, bf16[320,128]{1,0:T(8,128)(2,1)S(1)}, u32[]{:S(2)}) copy-start(bf16[320,128]{1,0:T(8,128)(2,1)S(1)} %pad_maximum_fusion.1.own_ref.pair_ref) | copy-start | bytes 245764
  1.9 15.6 %collective-permute-start = (bf16[320,128]{1,0:T(8,128)(2,1)S(1)}, bf16[320,128]{1,0:T(8,128)(2,1)S(1)}, u32[]{:S(2)}, u32[]{:S(2)}) collective-permute-start(bf16[320,128]{1,0:T(8,128)(2,1)S(1)} %pad_maximum_fusion.1.own_ref.pair_ref), channel_id=1, source_target_pairs={{128,0},{132,4},{136,8},{140,12},{144,16},{148,20},{152,24},{156,2... | collective-permute-start | bytes 245768 | tf_op jit(solution)/shard_map/ppermute | solution.py:385
  3.2 0.7 copy-start.11
  3.9 0.7 copy-start.13
  4.0 0.8 copy-start.8
  4.6 0.7 copy-start.7
  6.2 9.9 %all-to-all-start = ((bf16[4,144,128]{2,1,0:T(8,128)(2,1)}), bf16[4,144,128]{2,1,0:T(8,128)(2,1)S(1)}, u32[]{:S(2)}, u32[]{:S(2)}) async-start(bf16[4,144,128]{2,1,0:T(8,128)(2,1)} %broadcast_in_dim.41), calls=%async_computation | async-start | bytes 294912 | tf_op jit(solution)/shard_map/all_to_all | solution.py:374
  11.2 0.7 copy-start.14
  17.5 0.6 copy-start.4
  20.8 1.0 copy-start.5
  22.6 36.9 %all-to-all-start.1 = ((bf16[32,24,128]{2,1,0:T(8,128)(2,1)}), bf16[32,24,128]{2,1,0:T(8,128)(2,1)S(1)}, u32[]{:S(2)}, u32[]{:S(2)}) async-start(bf16[32,24,128]{2,1,0:T(8,128)(2,1)} %maximum_bitcast_fusion), calls=%async_computation.1 | async-start | bytes 393216 | tf_op jit(solution)/shard_map/all_to_all | solution.py:374
  59.6 0.7 copy-start
  69.0 5.1 %copy-start.9 = (f32[9,256]{1,0:T(8,128)S(1)}, f32[9,256]{1,0:T(8,128)}, u32[]{:S(2)}) copy-start(f32[9,256]{1,0:T(8,128)} %get-tuple-element.29) | copy-start | bytes 27652
  69.0 5.1 %copy-start.2 = (f32[256,128]{1,0:T(8,128)S(1)}, f32[256,128]{1,0:T(8,128)}, u32[]{:S(2)}) copy-start(f32[256,128]{1,0:T(8,128)} %get-tuple-element.27) | copy-start | bytes 393220
  69.0 21.3 %all-to-all-start.2 = ((bf16[32,12,128]{2,1,0:T(8,128)(2,1)}), bf16[32,12,128]{2,1,0:T(8,128)(2,1)S(1)}, u32[]{:S(2)}, u32[]{:S(2)}) async-start(bf16[32,12,128]{2,1,0:T(8,128)(2,1)} %copy.145), calls=%async_computation.2 | async-start | bytes 262144 | tf_op jit(solution)/shard_map/all_to_all | solution.py:374
  95.1 0.9 copy-start.6
  96.0 0.9 copy-start.3
  96.9 0.7 copy-start.15
  96.9 0.7 copy-start.16
  119.5 15.9 %all-to-all-start.5 = ((f32[16,17,128]{2,1,0:T(8,128)}), f32[16,17,128]{2,1,0:T(8,128)S(1)}, u32[]{:S(2)}, u32[]{:S(2)}) async-start(f32[16,17,128]{2,1,0:T(8,128)} %broadcast_in_dim.49), calls=%async_computation.5 | async-start | bytes 393216 | tf_op jit(solution)/shard_map/all_to_all | solution.py:374
  136.1 12.7 %all-to-all-start.6 = ((f32[8,17,128]{2,1,0:T(8,128)}), f32[8,17,128]{2,1,0:T(8,128)S(1)}, u32[]{:S(2)}, u32[]{:S(2)}) async-start(f32[8,17,128]{2,1,0:T(8,128)} %broadcast_in_dim.50), calls=%async_computation.6 | async-start | bytes 196608 | tf_op jit(solution)/shard_map/all_to_all | solution.py:374

commit v3 on v2

v3 whole, which is shorter than its diff:
```python
import functools
import math

import jax
import jax.numpy as jnp
from jax import lax
from jax.experimental import pallas as pl
from jax.experimental.pallas import tpu as pltpu
from jax.sharding import Mesh, PartitionSpec as P

EPS = 1e-05
FR = 4
ROWS = 80
LEAD = 8
BF = jnp.bfloat16
F32 = jnp.float32


def nt(a, b):
    return lax.dot_general(a, b, (((1,), (1,)), ((), ())), preferred_element_type=F32)


def nn(a, b):
    return lax.dot_general(a, b, (((1,), (0,)), ((), ())), preferred_element_type=F32)


def tn(a, b):
    return lax.dot_general(a, b, (((0,), (0,)), ((), ())), preferred_element_type=F32)


def roll_rows(values, amount):
    return pltpu.roll(values, amount % values.shape[0], 0)


def sigmoid(values):
    return 0.5 * jnp.tanh(0.5 * values) + 0.5


def inverse_norm(features):
    return lax.rsqrt(jnp.mean(features * features, axis=-1, keepdims=True) + EPS)


def norm_back(d_normed, features, scale, gain):
    scaled = d_normed * gain
    summed = jnp.sum(scaled * features, axis=-1, keepdims=True)
    return scale * scaled - features * (scale * scale * scale * summed * (1.0 / features.shape[-1]))


def bins_conv(values, taps):
    return taps[0:1] * roll_rows(values, 1) + taps[1:2] * values + taps[2:3] * roll_rows(values, -1)


HALVES = (slice(0, 128), slice(128, 256))


def freq_forward_kernel(own_ref, halo_ref, weight_ref, taps_ref, gain_ref, own_out, halo_out, hidden_out):
    gain = gain_ref[...]
    for pair_ref, out_ref in ((own_ref, own_out), (halo_ref, halo_out)):
        features = pair_ref[...].astype(F32)
        normed = (features * inverse_norm(features) * gain).astype(BF)
        mixed = features
        for lanes in HALVES:
            hidden = nt(normed, weight_ref[lanes, :64])
            if out_ref is own_out:
                hidden_out[:, lanes] = hidden
            drive = bins_conv(hidden, taps_ref[:, lanes])
            active = (drive * sigmoid(drive)).astype(BF)
            mixed = mixed + nn(active, weight_ref[lanes, 64:])
        out_ref[...] = mixed.astype(BF)


def freq_forward(pair, halo, weights, taps, gain):
    rows = pair.shape[0]
    return pl.pallas_call(
        freq_forward_kernel,
        out_shape=(
            jax.ShapeDtypeStruct((rows, 64), BF),
            jax.ShapeDtypeStruct((rows, 64), BF),
            jax.ShapeDtypeStruct((rows, 256), F32),
        ),
        name="freq_forward",
    )(pair, halo, weights, taps, gain)


def freq_backward_kernel(flag_ref, pair_ref, hidden_ref, back_ref, weight_ref, taps_ref, gain_ref, out_ref, grad_ref, tap_ref, gain_out):
    gain = gain_ref[...]
    row = lax.broadcasted_iota(jnp.int32, (ROWS, 1), 0)
    upper = LEAD + 64 + flag_ref[0]
    one = jnp.where((row >= LEAD) & (row < upper), 1.0, 0.0).astype(F32)
    own = jnp.concatenate([one] * FR, axis=0)
    features = pair_ref[...].astype(F32)
    scale = inverse_norm(features)
    grad = back_ref[:, 64:]
    grad_wide = grad.astype(F32)
    grad_own = (grad_wide * own).astype(BF)
    normed = (features * scale * gain * own).astype(BF)
    d_normed = None
    for lanes in HALVES:
        taps = taps_ref[:, lanes]
        hidden = hidden_ref[:, lanes]
        before, after = roll_rows(hidden, 1), roll_rows(hidden, -1)
        drive = taps[0:1] * before + taps[1:2] * hidden + taps[2:3] * after
        gate = sigmoid(drive)
        active = drive * gate
        slope = gate + active * (1.0 - gate)
        grad_ref[lanes, :64] = tn(active.astype(BF), grad_own)
        d_drive = nt(grad, weight_ref[lanes, 64:]) * slope
        d_own = d_drive * own
        tap_ref[0:1, lanes] = jnp.sum(d_own * before, axis=0, keepdims=True)
        tap_ref[1:2, lanes] = jnp.sum(d_own * hidden, axis=0, keepdims=True)
        tap_ref[2:3, lanes] = jnp.sum(d_own * after, axis=0, keepdims=True)
        d_hidden = (
            taps[0:1] * roll_rows(d_drive, -1) + taps[1:2] * d_drive + taps[2:3] * roll_rows(d_drive, 1)
        ).astype(BF)
        grad_ref[lanes, 64:] = tn(d_hidden, normed)
        part = nn(d_hidden, weight_ref[lanes, :64])
        d_normed = part if d_normed is None else d_normed + part
    gain_out[...] = jnp.sum(d_normed * features * (scale * own), axis=0, keepdims=True)
    out_ref[:, :64] = back_ref[:, :64]
    out_ref[:, 64:] = (grad_wide + norm_back(d_normed, features, scale, gain)).astype(BF)


def freq_backward(pair, hidden, back, weights, taps, gain, last_plane):
    vmem = pl.BlockSpec(memory_space=pltpu.VMEM)
    return pl.pallas_call(
        freq_backward_kernel,
        out_shape=(
            jax.ShapeDtypeStruct(back.shape, BF),
            jax.ShapeDtypeStruct((256, 128), F32),
            jax.ShapeDtypeStruct((3, 256), F32),
            jax.ShapeDtypeStruct((1, 64), F32),
        ),
        in_specs=[pl.BlockSpec(memory_space=pltpu.SMEM)] + [vmem] * 6,
        name="freq_backward",
    )(last_plane.reshape(1), pair, hidden, back, weights, taps, gain)


def turned(tiles):
    return jnp.concatenate(
        [roll_rows(tiles[8 * i : 8 * i + 8], 4) for i in range(tiles.shape[0] // 8)], axis=0
    )


def groups_on(values, count):
    if count > 0:
        return jnp.concatenate([values[8 * count :], turned(values[: 8 * count])], axis=0)
    base = values.shape[0] + 8 * count
    return jnp.concatenate([turned(values[base:]), values[:base]], axis=0)


def later(values, spacing, place):
    if spacing == 1:
        return jnp.where(place == 3, roll_rows(groups_on(values, 1), 3), roll_rows(values, -1))
    return groups_on(values, spacing // FR)


def earlier(values, spacing, place):
    if spacing == 1:
        return jnp.where(place == 0, roll_rows(groups_on(values, -1), -3), roll_rows(values, 1))
    return groups_on(values, -(spacing // FR))


def own_rows(values):
    tiles = values.reshape(values.shape[0] // 8, 8, values.shape[1])
    return jnp.sum(jnp.sum(tiles, axis=0)[:4], axis=0, keepdims=True)


def one_bin(message, slot):
    if slot < 2:
        both = message[:, 0:8].astype(F32).reshape(256, 128)
        return both[:, 64 * slot : 64 * slot + 64]
    edge = message[:, 8:12].astype(F32)
    return jnp.concatenate([edge[:, :, :64], edge[:, :, 64:]], axis=1).reshape(256, 64)


def time_kernel(
    flag_ref, x_ref, cot_ref, marks_ref, weight_ref, taps_ref, gain_ref, out_ref, grad_ref, tap_ref, gain_out
):
    gain = gain_ref[...]
    valid, inside = marks_ref[:, 0:1], marks_ref[:, 1:2]
    spot = lax.broadcasted_iota(jnp.int32, (256, 1), 0)
    place = lax.broadcasted_iota(jnp.int32, (256, 128), 0) & 3
    for slot in range(3):
        share = jnp.where(flag_ref[0] > 0, 1.0, 0.0).astype(F32) if slot == 2 else 1.0

        def keep(ref, rows, lanes, value):
            if slot == 0:
                ref[rows, lanes] = value
            else:
                ref[rows, lanes] += value

        counted = jnp.where((spot & 7) < 4, share, 0.0).astype(F32)
        features, grad_wide = one_bin(x_ref, slot), one_bin(cot_ref, slot)
        grad = grad_wide.astype(BF)
        grad_own = (grad_wide * counted).astype(BF)
        scale = inverse_norm(features)
        normed = features * scale * gain
        normed_own = (normed * counted).astype(BF)
        normed = normed.astype(BF)
        mixed, d_normed = features, None
        for lanes in HALVES:
            weight_in, weight_out = weight_ref[lanes, :64], weight_ref[lanes, 64:]
            state = nt(normed, weight_in) * valid
            states, slopes = [], []
            for layer in range(3):
                spacing = (1, 4, 16)[layer]
                row = taps_ref[3 * layer : 3 * layer + 3, lanes]
                drive = (
                    row[0:1] * earlier(state, spacing, place)
                    + row[1:2] * state
                    + row[2:3] * later(state, spacing, place)
                )
                gate = sigmoid(drive)
                active = drive * gate
                states.append(state)
                slopes.append(gate + active * (1.0 - gate))
                state = state + active
                if layer < 2:
                    state = state * inside
            top = state.astype(BF)
            mixed = mixed + nn(top, weight_out)
            keep(grad_ref, lanes, slice(0, 64), tn(top, grad_own))
            d_state = nt(grad, weight_out)
            for layer in reversed(range(3)):
                spacing = (1, 4, 16)[layer]
                row = taps_ref[3 * layer : 3 * layer + 3, lanes]
                d_drive = d_state * slopes[layer]
                if layer < 2:
                    d_drive = d_drive * inside
                held = states[layer]
                for j, moved in enumerate((earlier(held, spacing, place), held, later(held, spacing, place))):
                    at = 3 * layer + j
                    keep(tap_ref, slice(at, at + 1), lanes, own_rows(d_drive * moved) * share)
                d_state = d_state + (
                    row[0:1] * later(d_drive, spacing, place)
                    + row[1:2] * d_drive
                    + row[2:3] * earlier(d_drive, spacing, place)
                )
            d_pre = (d_state * valid).astype(BF)
            keep(grad_ref, lanes, slice(64, 128), tn(d_pre, normed_own))
            part = nn(d_pre, weight_in)
            d_normed = part if d_normed is None else d_normed + part
        keep(gain_out, slice(0, 1), slice(0, 64), own_rows(d_normed * features * scale) * share)
        d_one = grad_wide + norm_back(d_normed, features, scale, gain)
        both = jnp.concatenate([mixed, d_one], axis=1).reshape(32, 8, 128)
        out_ref[:, 4 * slot : 4 * slot + 4] = both[:, :4].astype(BF)


def time_path(x_one, cot, marks, weights, taps, gain, flag):
    vmem = pl.BlockSpec(memory_space=pltpu.VMEM)
    return pl.pallas_call(
        time_kernel,
        out_shape=(
            jax.ShapeDtypeStruct((32, 12, 128), BF),
            jax.ShapeDtypeStruct((256, 128), F32),
            jax.ShapeDtypeStruct((9, 256), F32),
            jax.ShapeDtypeStruct((1, 64), F32),
        ),
        in_specs=[pl.BlockSpec(memory_space=pltpu.SMEM)] + [vmem] * 6,
        name="time_path",
    )(flag.reshape(1), x_one, cot, marks, weights, taps, gain)


def finish_kernel(scale, part_ref, freq_gain, freq_in, freq_taps, freq_out, time_gain, time_in, time_taps, time_out):
    freq_out[...] = part_ref[0:64, :64] * scale
    freq_in[...] = (part_ref[0:64, 64:] * scale).T
    time_out[...] = part_ref[64:128, :64] * scale
    time_in[...] = (part_ref[64:128, 64:] * scale).T
    gains = part_ref[134:135, :] * scale
    freq_gain[...] = gains[:, :64]
    time_gain[...] = gains[:, 64:]
    taps = part_ref[128:134, :] * scale
    for at in range(12):
        half = 64 * (at % 2)
        row = taps[at // 2 : at // 2 + 1, half : half + 64]
        if at < 3:
            freq_taps[at : at + 1, :] = row
        else:
            time_taps[at - 3 : at - 2, :] = row


def finish(total, scale):
    shape = lambda *dims: jax.ShapeDtypeStruct(dims, F32)
    got = pl.pallas_call(
        functools.partial(finish_kernel, scale),
        out_shape=(
            shape(1, 64),
            shape(64, 64),
            shape(3, 64),
            shape(64, 64),
            shape(1, 64),
            shape(64, 64),
            shape(9, 64),
            shape(64, 64),
        ),
        name="finish",
    )(total)
    return (got[0][0], got[1], got[2], got[3], got[4][0], got[5], got[6].reshape(3, 3, 64), got[7])


def plane_lanes(values, plane):
    frames, width = values.shape
    padded = jnp.pad(values, ((0, 0), (LEAD * 64, (ROWS - LEAD + 192) * 64 - width)))
    return lax.dynamic_slice(padded, (0, plane * 4096), (frames, ROWS * 64))


def pack(freq_in, freq_taps, freq_out, time_in, time_taps, time_out):
    taps = jnp.concatenate([freq_taps, time_taps.reshape(9, 64)], axis=0)
    high = lax.reduce_precision(taps, 8, 7)
    low = lax.reduce_precision(taps - high, 8, 7)
    packed = jnp.concatenate(
        [
            jnp.concatenate([freq_in.T, freq_out], axis=1),
            jnp.concatenate([time_in.T, time_out], axis=1),
            jnp.concatenate([high, low], axis=1).astype(BF),
            jnp.zeros((4, 128), BF),
        ],
        axis=0,
    )
    return packed


def unpack(gathered):
    freq_w = gathered[:, :64].reshape(256, 128)
    time_w = gathered[:, 64:128].reshape(256, 128)
    tap_rows = gathered[:, 128:140].astype(F32)
    taps = (tap_rows[:, :, :64] + tap_rows[:, :, 64:]).transpose(1, 0, 2).reshape(12, 256)
    return freq_w, time_w, taps


def message(mine, edge):
    edge = jnp.concatenate([edge[:, :FR], edge[:, FR:]], axis=2)
    return jnp.concatenate([mine, jnp.pad(edge, ((0, 30), (0, 0), (0, 0)))], axis=1)


def lanes_message(own, halo):
    both = jnp.concatenate([own, halo], axis=0)
    mine = both[:, LEAD * 64 : LEAD * 64 + 4096].reshape(2 * FR, 32, 128).transpose(1, 0, 2)
    edge = jnp.stack([both[:, LEAD * 64 - 64 : LEAD * 64], both[:, LEAD * 64 + 4096 : LEAD * 64 + 4160]], axis=0)
    return message(mine, edge)


def rows_message(own, halo):
    both = jnp.concatenate([own.reshape(FR, ROWS, 64), halo.reshape(FR, ROWS, 64)], axis=0)
    mine = both[:, LEAD : LEAD + 64].reshape(2 * FR, 32, 128).transpose(1, 0, 2)
    return message(mine, jnp.stack([both[:, LEAD - 1], both[:, LEAD + 64]], axis=0))


def frame_marks(counts, x_at):
    by_plane = jnp.pad(counts.reshape(4, 32), ((1, 1), (0, 0)))
    window = lax.dynamic_slice(by_plane, (x_at, 0), (3, 32))
    spot = jnp.arange(32)
    halo_count = jnp.where(spot >= 16, window[0], window[2])
    halo_in = jnp.where(spot >= 16, (spot >= 21) & (x_at > 0), (spot <= 10) & (x_at < 3))
    limit = jnp.stack([window[1], halo_count], axis=1)
    valid = (jnp.arange(4) < limit[:, :, None]) & jnp.stack([spot >= 0, halo_in], axis=1)[:, :, None]
    inside = jnp.stack([spot >= 0, halo_in], axis=1)[:, :, None] & (jnp.arange(4) >= 0)
    return jnp.stack([valid.reshape(256), inside.reshape(256)], axis=1).astype(F32)


def from_frames(arrived, plane):
    rows = arrived.reshape(32, 3, FR, 128)
    mine = rows[:, :2].transpose(2, 0, 1, 3).reshape(FR, 64, 128)
    left = jnp.where(plane > 0, rows[0, 2], jnp.zeros((), BF))[:, None]
    right = rows[1, 2][:, None]
    return jnp.concatenate(
        [jnp.zeros((FR, LEAD - 1, 128), BF), left, mine, right, jnp.zeros((FR, ROWS - LEAD - 65, 128), BF)], axis=1
    ).reshape(FR * ROWS, 128)


def own_part(done):
    return done.reshape(FR, ROWS, 128)[:, LEAD : LEAD + 65].reshape(FR * 65, 128)


def grad_parts(freq_w, freq_t, freq_g, time_w, time_t, time_g):
    taps = jnp.concatenate([freq_t, time_t], axis=0).reshape(12, 4, 64).transpose(1, 0, 2).reshape(4, 6, 128)
    gains = jnp.broadcast_to(jnp.concatenate([freq_g, time_g], axis=1), (4, 1, 128))
    grads = jnp.concatenate(
        [freq_w.reshape(4, 64, 128), time_w.reshape(4, 64, 128), taps, gains, jnp.zeros((4, 1, 128), F32)], axis=1
    )
    return grads.astype(BF).reshape(4, 8, 17, 128).transpose(1, 0, 2, 3).reshape(32, 17, 128)


def outputs_of(arrived):
    rows = arrived.reshape(4, FR, 65, 128)
    whole = jnp.concatenate([rows[0, :, :64], rows[1, :, :64], rows[2, :, :64], rows[3]], axis=1)
    return whole[:, :, :64].reshape(FR, -1), whole[:, :, 64:].reshape(FR, -1)


def halo_pairs():
    pairs = []
    for x_at in range(4):
        for spot in range(32):
            if spot <= 10 and x_at < 3:
                pairs.append(((x_at + 1) * 32 + spot, x_at * 32 + spot))
            if spot >= 21 and x_at > 0:
                pairs.append(((x_at - 1) * 32 + spot, x_at * 32 + spot))
    return pairs


SEQ = ("x", "z", "core")


def exchange(values, axes):
    return lax.all_to_all(values, axes, 0, 0)


def shards(
    signal, cotangent, counts, freq_gain, freq_in, freq_taps, freq_out, time_gain, time_in, time_taps, time_out
):
    plane = lax.axis_index("ch")
    x_at = lax.axis_index("x")
    spot = lax.axis_index(("z", "core"))
    grad_scale = 1.0 / math.sqrt(FR * 128 * (signal.shape[1] // 64))
    lanes = jnp.stack([plane_lanes(signal, plane), plane_lanes(cotangent, plane)], axis=0)
    halo = lax.ppermute(lanes, SEQ, halo_pairs())
    packed = pack(freq_in, freq_taps, freq_out, time_in, time_taps, time_out)
    gathered = exchange(jnp.broadcast_to(packed, (4,) + packed.shape), "ch")
    band_cot = exchange(lanes_message(lanes[1], halo[1]), ("z", "core"))
    freq_w, time_w, taps = unpack(gathered)
    freq_t, time_t = taps[:3], taps[3:]
    gain_f, gain_t = freq_gain[None], time_gain[None]
    x_rows, x_halo = lanes[0].reshape(FR * ROWS, 64), halo[0].reshape(FR * ROWS, 64)
    own, beside, hidden = freq_forward(x_rows, x_halo, freq_w, freq_t, gain_f)
    band_x = exchange(rows_message(own, beside), ("z", "core"))
    marks = frame_marks(counts, x_at)
    edge = jnp.where((plane == 3) & (spot == 1), 1, 0)
    mixed, *sums = time_path(band_x, band_cot, marks, time_w, time_t, gain_t, edge)
    back = from_frames(exchange(mixed, ("z", "core")), plane)
    last_plane = jnp.where(plane == 3, 1, 0)
    done, *freq_sums = freq_backward(x_rows, hidden, back, freq_w, freq_t, gain_f, last_plane)
    part = exchange(grad_parts(*freq_sums, *sums), ("x", "core", "ch"))
    planes = exchange(jnp.broadcast_to(own_part(done), (4, FR * 65, 128)), "ch")
    part = jnp.sum(part.astype(F32), axis=0).astype(BF)
    part = jnp.sum(exchange(jnp.broadcast_to(part, (16, 17, 128)), "z").astype(F32), axis=0)
    total = exchange(jnp.broadcast_to(part, (8, 17, 128)), ("x", "core")).reshape(136, 128)
    return outputs_of(planes) + finish(total, grad_scale)


def solution(mesh):
    torus = Mesh(mesh.devices.reshape(4, 16, 2, 4), ("x", "z", "core", "ch"))
    return jax.shard_map(
        shards,
        mesh=torus,
        in_specs=(
            P(SEQ, None),
            P(SEQ, None),
            P(),
            P(),
            P(None, "ch"),
            P(None, "ch"),
            P("ch", None),
            P(),
            P(None, "ch"),
            P(None, None, "ch"),
            P("ch", None),
        ),
        out_specs=(
            P(SEQ, None),
            P(SEQ, None),
            P(),
            P(None, "ch"),
            P(None, "ch"),
            P("ch", None),
            P(),
            P(None, "ch"),
            P(None, None, "ch"),
            P("ch", None),
        ),
        check_vma=False,
    )
```

time: 154 us -> 166 us (1.078)
  blocking collectives: 20.3 us -> 0 us
  waiting for transfers between devices: 51.7 us -> 69.7 us
  starting transfers between devices: 40.8 us -> 54 us
  local copies, waits for them, and re-layouts: 24.2 us -> 22.1 us
  other arithmetic: 2.18 us -> 3.97 us
    all_to_all x2 -> x0, blocking collectives: 20.3 us -> none  [exchange(): return lax.all_to_all(values, axes, 0, 0)]
    all_to_all x5 -> x8, waiting for transfers between devices: 51.7 us -> 69.7 us  [exchange(): return lax.all_to_all(values, axes, 0, 0)]
    all_to_all x5 -> x8, starting transfers between devices: 39.5 us -> 52.8 us  [exchange(): return lax.all_to_all(values, axes, 0, 0)]
    another operation x1 -> x5, local copies, waits for them, and re-layouts: 0.01 us -> 2.43 us  [the longest x2 0.91 us: shards(): jnp.stack([plane_lanes(signal, plane), plane_lanes(cotangent, plane)], ax...]
    slice x9 -> x2, local copies, waits for them, and re-layouts: 2.32 us -> 0.03 us  [the longest x1 0.02 us: rows_message(): mine = both[:, LEAD:LEAD + 64].reshape(2 * FR, 32, 128).transpose(1, 0, 2)]
    unnamed x42 -> x43, local copies, waits for them, and re-layouts: 7.06 us -> 4.96 us
    pallas_call x2 -> x3, Pallas kernels: 9.82 us -> 11.1 us  [the longest x1 6.65 us: time_path(): pl.pallas_call(time_kernel, out_shape=(jax.ShapeDtypeStruct((32, 12, 128)...]
    reshape x13 -> x12, local copies, waits for them, and re-layouts: 2.82 us -> 4.01 us  [the longest x1 1.3 us: finish(): got[6].reshape(3, 3, 64)]
  transfers between devices with their start and end apart: 6 -> 9, of which waited for: 5 -> 8; matrix products, arithmetic and copies ran while one was open for 5% -> 7% of each run, Pallas kernels for 0% -> 2%
where the time goes in v3:
time: 166 us; the launch traced here: 165 us
  waiting for transfers between devices  69.7 us (42%)
  starting transfers between devices  54 us (33%)
  local copies, waits for them, and re-layouts  22.1 us (13%)
  Pallas kernels  13.7 us (8%)
  other arithmetic  3.97 us (2%)
    all_to_all x8, waiting for transfers between devices, exchange(): return lax.all_to_all(values, axes, 0, 0)  69.7 us
    all_to_all x8, starting transfers between devices, exchange(): return lax.all_to_all(values, axes, 0, 0)  52.8 us
    pallas_call x1, Pallas kernels, time_path(): pl.pallas_call(time_kernel, out_shape=(jax.ShapeDtypeStruct((32, 12, 128)...  6.65 us
    unnamed x43, local copies, waits for them, and re-layouts  4.96 us
  transfers between devices with their start and end apart: 9, of which 8 were waited for; matrix products, arithmetic and copies ran while one was open for 7% of the time, Pallas kernels for 2%

profile of v3, /device:TPU:1, one launch (start us, length us, event | category | flops | bytes accessed | tf_op | source)
XLA Modules:
  0.0 164.8 jit_solution(13515259337855247745)
XLA Ops:
  0.7 0.9 fusion.29
  1.7 1.3 collective-permute-start
  3.1 0.6 copy-done.11
  5.2 0.7 broadcast_in_dim.38
  5.9 5.1 %all-to-all-start = ((bf16[4,144,128]{2,1,0:T(8,128)(2,1)}), bf16[4,144,128]{2,1,0:T(8,128)(2,1)S(1)}, u32[]{:S(2)}, u32[]{:S(2)}) async-start(bf16[4,144,128]{2,1,0:T(8,128)(2,1)} %broadcast_in_dim.38), calls=%async_computation | async-start | bytes 294912 | tf_op jit(solution)/shard_map/all_to_all | solution.py:405
  11.2 0.6 copy-done.14
  12.0 0.8 reshape_squeeze_stack.3.own_ref.pair_ref
  13.0 0.8 reshape_squeeze.3.halo_ref
  13.8 0.7 pad_maximum_fusion.2
  14.5 1.4 all-to-all-done
  16.0 18.1 %all-to-all-start.2 = ((bf16[32,12,128]{2,1,0:T(8,128)(2,1)}), bf16[32,12,128]{2,1,0:T(8,128)(2,1)S(1)}, u32[]{:S(2)}, u32[]{:S(2)}) async-start(bf16[32,12,128]{2,1,0:T(8,128)(2,1)} %pad_maximum_fusion.2), calls=%async_computation.2 | async-start | bytes 262144 | tf_op jit(solution)/shard_map/all_to_all | solution.py:405
  34.2 0.7 slice.109.taps_ref
  34.9 0.7 fusion.28
  35.5 2.6 %freq_forward.1 = (bf16[320,64]{1,0:T(8,128)(2,1)}, bf16[320,64]{1,0:T(8,128)(2,1)}, f32[320,256]{1,0:T(8,128)}) custom-call(bf16[320,64]{1,0:T(8,128)(2,1)} %reshape_squeeze_stack.3.own_ref.pair_ref, bf16[320,64]{1,0:T(8,128)(2,1)} %reshape_squeeze.3.halo_ref, bf16[256,128]{1,0:T(8,128)(2,1)} %bitcast.71, f32[3,256]{1,0:T(4,128)} %slice.109.taps_ref, ...), custom_call_target="tpu_custom_call" | custom-call | tf_op jit(solution)/shard_map/freq_forward/pallas_call | solution.py:74
  38.2 1.0 copy.157
  39.6 0.7 pad_maximum_fusion.1
  40.3 9.7 %all-to-all-done.2.cot_ref = bf16[32,12,128]{2,1,0:T(8,128)(2,1)S(1)} async-done(((bf16[32,12,128]{2,1,0:T(8,128)(2,1)}), bf16[32,12,128]{2,1,0:T(8,128)(2,1)S(1)}, u32[]{:S(2)}, u32[]{:S(2)}) %all-to-all-start.2) | async-done | bytes 98336 | tf_op jit(solution)/shard_map/all_to_all | solution.py:405
  50.0 0.7 copy-done.2
  50.6 5.1 %all-to-all-start.1 = ((bf16[32,12,128]{2,1,0:T(8,128)(2,1)}), bf16[32,12,128]{2,1,0:T(8,128)(2,1)S(1)}, u32[]{:S(2)}, u32[]{:S(2)}) async-start(bf16[32,12,128]{2,1,0:T(8,128)(2,1)} %pad_maximum_fusion.1), calls=%async_computation.1 | async-start | bytes 262144 | tf_op jit(solution)/shard_map/all_to_all | solution.py:405
  56.4 0.8 copy.164.marks_ref
  57.2 0.7 slice.126.taps_ref
  57.9 14.0 %all-to-all-done.1.x_ref = bf16[32,12,128]{2,1,0:T(8,128)(2,1)S(1)} async-done(((bf16[32,12,128]{2,1,0:T(8,128)(2,1)}), bf16[32,12,128]{2,1,0:T(8,128)(2,1)S(1)}, u32[]{:S(2)}, u32[]{:S(2)}) %all-to-all-start.1) | async-done | bytes 98336 | tf_op jit(solution)/shard_map/all_to_all | solution.py:405
  71.9 0.7 copy-done.3
  72.6 6.7 %time_path.1 = (bf16[32,12,128]{2,1,0:T(8,128)(2,1)}, f32[256,128]{1,0:T(8,128)}, f32[9,256]{1,0:T(8,128)}, f32[1,64]{1,0:T(1,128)}) custom-call(s32[1]{0:T(128)} %bitcast.8.flag_ref, bf16[32,12,128]{2,1,0:T(8,128)(2,1)} %copy-done.3, bf16[32,12,128]{2,1,0:T(8,128)(2,1)} %copy-done.2, f32[256,2]{1,0:T(8,128)} %copy.164.marks_ref, bf16[256,128]{1,0:T(8,128)(2,1)} %bitcast.83, ...), custom_call_target="tpu_custom_call" | custom-call | tf_op jit(solution)/shard_map/time_path/pallas_call | solution.py:251
  79.2 5.0 %all-to-all-start.3 = ((bf16[32,12,128]{2,1,0:T(8,128)(2,1)}), bf16[32,12,128]{2,1,0:T(8,128)(2,1)S(1)}, u32[]{:S(2)}, u32[]{:S(2)}) async-start(bf16[32,12,128]{2,1,0:T(8,128)(2,1)} %get-tuple-element.32), calls=%async_computation.3 | async-start | bytes 262144 | tf_op jit(solution)/shard_map/all_to_all | solution.py:405
  84.2 16.1 %all-to-all-done.3 = bf16[32,12,128]{2,1,0:T(8,128)(2,1)S(1)} async-done(((bf16[32,12,128]{2,1,0:T(8,128)(2,1)}), bf16[32,12,128]{2,1,0:T(8,128)(2,1)S(1)}, u32[]{:S(2)}, u32[]{:S(2)}) %all-to-all-start.3) | async-done | bytes 98336 | tf_op jit(solution)/shard_map/all_to_all | solution.py:405
  100.5 1.9 %concatenate.64 = bf16[4,80,128]{2,1,0:T(8,128)(2,1)} concatenate(bf16[4,7,128]{2,1,0:T(8,128)(2,1)S(1)} %broadcast.102, bf16[4,1,128]{2,1,0:T(2,128)(2,1)S(1)} %get-tuple-element.58, bf16[4,64,128]{2,1,0:T(8,128)(2,1)S(1)} %bitcast.82, bf16[4,1,128]{2,1,0:T(2,128)(2,1)S(1)} %get-tuple-element.57, bf16[4,7,128]{2,1,0:T(8,128)(2,1)S(1)} %broadcast.102), dimensions={1} | concatenate | bytes 163840 | tf_op jit(solution)/shard_map/concatenate | solution.py:366
  102.4 2.8 %freq_backward.1 = (bf16[320,128]{1,0:T(8,128)(2,1)}, f32[256,128]{1,0:T(8,128)}, f32[3,256]{1,0:T(4,128)}, f32[1,64]{1,0:T(1,128)}) custom-call(s32[1]{0:T(128)} %bitcast.flag_ref, bf16[320,64]{1,0:T(8,128)(2,1)} %reshape_squeeze_stack.3.own_ref.pair_ref, f32[320,256]{1,0:T(8,128)} %get-tuple-element.29.hidden_ref, bf16[320,128]{1,0:T(8,128)(2,1)} %bitcast.74, ...), custom_call_target="tpu_custom_call" | custom-call | tf_op jit(solution)/shard_map/freq_backward/pallas_call | solution.py:125
  105.2 0.7 convert.35
  106.1 0.9 convert.33
  107.1 0.6 copy-done.15
  107.9 0.7 copy.175
  108.7 6.2 %all-to-all-start.5 = ((bf16[32,17,128]{2,1,0:T(8,128)(2,1)}), bf16[32,17,128]{2,1,0:T(8,128)(2,1)S(1)}, u32[]{:S(2)}, u32[]{:S(2)}) async-start(bf16[32,17,128]{2,1,0:T(8,128)(2,1)} %copy.175), calls=%async_computation.5 | async-start | bytes 393216 | tf_op jit(solution)/shard_map/all_to_all | solution.py:405
  115.0 8.1 %all-to-all-done.5 = bf16[32,17,128]{2,1,0:T(8,128)(2,1)S(1)} async-done(((bf16[32,17,128]{2,1,0:T(8,128)(2,1)}), bf16[32,17,128]{2,1,0:T(8,128)(2,1)S(1)}, u32[]{:S(2)}, u32[]{:S(2)}) %all-to-all-start.5) | async-done | bytes 139296 | tf_op jit(solution)/shard_map/all_to_all | solution.py:405
  123.1 0.7 broadcast_in_dim.42
  123.8 3.4 %all-to-all-start.4 = ((bf16[4,260,128]{2,1,0:T(8,128)(2,1)}), bf16[4,260,128]{2,1,0:T(8,128)(2,1)S(1)}, u32[]{:S(2)}, u32[]{:S(2)}) async-start(bf16[4,260,128]{2,1,0:T(8,128)(2,1)} %broadcast_in_dim.42), calls=%async_computation.4 | async-start | bytes 540672 | tf_op jit(solution)/shard_map/all_to_all | solution.py:405
  127.3 5.9 %all-to-all-done.4 = bf16[4,260,128]{2,1,0:T(8,128)(2,1)S(1)} async-done(((bf16[4,260,128]{2,1,0:T(8,128)(2,1)}), bf16[4,260,128]{2,1,0:T(8,128)(2,1)S(1)}, u32[]{:S(2)}, u32[]{:S(2)}) %all-to-all-start.4) | async-done | bytes 266272 | tf_op jit(solution)/shard_map/all_to_all | solution.py:405
  133.3 0.7 broadcast_in_dim.45
  133.9 3.5 %all-to-all-start.6 = ((bf16[16,17,128]{2,1,0:T(8,128)(2,1)}), bf16[16,17,128]{2,1,0:T(8,128)(2,1)S(1)}, u32[]{:S(2)}, u32[]{:S(2)}) async-start(bf16[16,17,128]{2,1,0:T(8,128)(2,1)} %broadcast_in_dim.45), calls=%async_computation.6 | async-start | bytes 196608 | tf_op jit(solution)/shard_map/all_to_all | solution.py:405
  138.0 11.3 %all-to-all-done.6 = bf16[16,17,128]{2,1,0:T(8,128)(2,1)S(1)} async-done(((bf16[16,17,128]{2,1,0:T(8,128)(2,1)}), bf16[16,17,128]{2,1,0:T(8,128)(2,1)S(1)}, u32[]{:S(2)}, u32[]{:S(2)}) %all-to-all-start.6) | async-done | bytes 69664 | tf_op jit(solution)/shard_map/all_to_all | solution.py:405
  149.3 0.6 broadcast_in_dim.46
  149.9 6.3 %all-to-all-start.7 = ((f32[8,17,128]{2,1,0:T(8,128)}), f32[8,17,128]{2,1,0:T(8,128)S(1)}, u32[]{:S(2)}, u32[]{:S(2)}) async-start(f32[8,17,128]{2,1,0:T(8,128)} %broadcast_in_dim.46), calls=%async_computation.7 | async-start | bytes 196608 | tf_op jit(solution)/shard_map/all_to_all | solution.py:405
  156.3 0.9 reshape.223
  157.2 0.9 reshape.224
  158.0 3.1 %all-to-all-done.7 = f32[8,17,128]{2,1,0:T(8,128)S(1)} async-done(((f32[8,17,128]{2,1,0:T(8,128)}), f32[8,17,128]{2,1,0:T(8,128)S(1)}, u32[]{:S(2)}, u32[]{:S(2)}) %all-to-all-start.7) | async-done | bytes 69664 | tf_op jit(solution)/shard_map/all_to_all | solution.py:405
  161.2 0.6 reshape.230.part_ref
  161.8 1.7 %finish.1 = (f32[1,64]{1,0:T(1,128)}, f32[64,64]{1,0:T(8,128)}, f32[3,64]{1,0:T(4,128)}, f32[64,64]{1,0:T(8,128)}, f32[1,64]{1,0:T(1,128)}, /*index=5*/f32[64,64]{1,0:T(8,128)}, f32[9,64]{1,0:T(8,128)}, f32[64,64]{1,0:T(8,128)}) custom-call(f32[136,128]{1,0:T(8,128)} %reshape.230.part_ref), custom_call_target="tpu_custom_call" | custom-call | tf_op jit(solution)/shard_map/finish/pallas_call | solution.py:284
  163.5 1.3 reshape.231
  (105 shorter events, 4.8 us)
Async XLA Ops:
  0.6 0.9 copy-start.1
  1.6 1.4 copy-start.12
  1.6 1.4 copy-start.10
  1.7 11.1 %collective-permute-start = (bf16[2,4,5120]{2,1,0:T(4,128)(2,1)S(1)}, bf16[2,4,5120]{2,1,0:T(4,128)(2,1)S(1)}, u32[]{:S(2)}, u32[]{:S(2)}) collective-permute-start(bf16[2,4,5120]{2,1,0:T(4,128)(2,1)S(1)} %pad_maximum_fusion.3), channel_id=1, source_target_pairs={{128,0},{132,4},{136,8},{140,12},{144,16},{148,20},{152,24},{156,2... | collective-permute-start | bytes 245768 | tf_op jit(solution)/shard_map/ppermute | solution.py:416
  3.0 0.7 copy-start.11
  3.7 0.7 copy-start.13
  3.7 0.8 copy-start.8
  4.4 0.7 copy-start.7
  5.9 5.1 %copy-start = (bf16[4,16448]{1,0:T(4,128)(2,1)S(1)}, bf16[4,16448]{1,0:T(4,128)(2,1)}, u32[]{:S(2)}) copy-start(bf16[4,16448]{1,0:T(4,128)(2,1)} %param.11) | copy-start | bytes 394756
  5.9 10.0 %all-to-all-start = ((bf16[4,144,128]{2,1,0:T(8,128)(2,1)}), bf16[4,144,128]{2,1,0:T(8,128)(2,1)S(1)}, u32[]{:S(2)}, u32[]{:S(2)}) async-start(bf16[4,144,128]{2,1,0:T(8,128)(2,1)} %broadcast_in_dim.38), calls=%async_computation | async-start | bytes 294912 | tf_op jit(solution)/shard_map/all_to_all | solution.py:405
  11.2 0.7 copy-start.14
  16.0 34.0 %all-to-all-start.2 = ((bf16[32,12,128]{2,1,0:T(8,128)(2,1)}), bf16[32,12,128]{2,1,0:T(8,128)(2,1)S(1)}, u32[]{:S(2)}, u32[]{:S(2)}) async-start(bf16[32,12,128]{2,1,0:T(8,128)(2,1)} %pad_maximum_fusion.2), calls=%async_computation.2 | async-start | bytes 262144 | tf_op jit(solution)/shard_map/all_to_all | solution.py:405
  38.2 1.0 copy-start.5
  50.0 0.7 copy-start.2
  50.6 21.3 %all-to-all-start.1 = ((bf16[32,12,128]{2,1,0:T(8,128)(2,1)}), bf16[32,12,128]{2,1,0:T(8,128)(2,1)S(1)}, u32[]{:S(2)}, u32[]{:S(2)}) async-start(bf16[32,12,128]{2,1,0:T(8,128)(2,1)} %pad_maximum_fusion.1), calls=%async_computation.1 | async-start | bytes 262144 | tf_op jit(solution)/shard_map/all_to_all | solution.py:405
  71.9 0.7 copy-start.3
  79.2 5.0 %copy-start.9 = (f32[9,256]{1,0:T(8,128)S(1)}, f32[9,256]{1,0:T(8,128)}, u32[]{:S(2)}) copy-start(f32[9,256]{1,0:T(8,128)} %get-tuple-element.37) | copy-start | bytes 27652
  79.2 5.0 %copy-start.4 = (f32[256,128]{1,0:T(8,128)S(1)}, f32[256,128]{1,0:T(8,128)}, u32[]{:S(2)}) copy-start(f32[256,128]{1,0:T(8,128)} %get-tuple-element.35) | copy-start | bytes 393220
  79.2 21.2 %all-to-all-start.3 = ((bf16[32,12,128]{2,1,0:T(8,128)(2,1)}), bf16[32,12,128]{2,1,0:T(8,128)(2,1)S(1)}, u32[]{:S(2)}, u32[]{:S(2)}) async-start(bf16[32,12,128]{2,1,0:T(8,128)(2,1)} %get-tuple-element.32), calls=%async_computation.3 | async-start | bytes 262144 | tf_op jit(solution)/shard_map/all_to_all | solution.py:405
  107.1 0.7 copy-start.15
  107.1 0.7 copy-start.16
  108.7 6.2 %copy-start.6 = (bf16[320,128]{1,0:T(8,128)(2,1)S(1)}, bf16[320,128]{1,0:T(8,128)(2,1)}, u32[]{:S(2)}) copy-start(bf16[320,128]{1,0:T(8,128)(2,1)} %get-tuple-element.33) | copy-start | bytes 245764
  108.7 14.4 %all-to-all-start.5 = ((bf16[32,17,128]{2,1,0:T(8,128)(2,1)}), bf16[32,17,128]{2,1,0:T(8,128)(2,1)S(1)}, u32[]{:S(2)}, u32[]{:S(2)}) async-start(bf16[32,17,128]{2,1,0:T(8,128)(2,1)} %copy.175), calls=%async_computation.5 | async-start | bytes 393216 | tf_op jit(solution)/shard_map/all_to_all | solution.py:405
  123.8 9.4 %all-to-all-start.4 = ((bf16[4,260,128]{2,1,0:T(8,128)(2,1)}), bf16[4,260,128]{2,1,0:T(8,128)(2,1)S(1)}, u32[]{:S(2)}, u32[]{:S(2)}) async-start(bf16[4,260,128]{2,1,0:T(8,128)(2,1)} %broadcast_in_dim.42), calls=%async_computation.4 | async-start | bytes 540672 | tf_op jit(solution)/shard_map/all_to_all | solution.py:405
  133.9 15.3 %all-to-all-start.6 = ((bf16[16,17,128]{2,1,0:T(8,128)(2,1)}), bf16[16,17,128]{2,1,0:T(8,128)(2,1)S(1)}, u32[]{:S(2)}, u32[]{:S(2)}) async-start(bf16[16,17,128]{2,1,0:T(8,128)(2,1)} %broadcast_in_dim.45), calls=%async_computation.6 | async-start | bytes 196608 | tf_op jit(solution)/shard_map/all_to_all | solution.py:405
  149.9 11.3 %all-to-all-start.7 = ((f32[8,17,128]{2,1,0:T(8,128)}), f32[8,17,128]{2,1,0:T(8,128)S(1)}, u32[]{:S(2)}, u32[]{:S(2)}) async-start(f32[8,17,128]{2,1,0:T(8,128)} %broadcast_in_dim.46), calls=%async_computation.7 | async-start | bytes 196608 | tf_op jit(solution)/shard_map/all_to_all | solution.py:405

commit v4 on v3

v4 whole, which is shorter than its diff:
```python
import functools
import math

import jax
import jax.numpy as jnp
from jax import lax
from jax.experimental import pallas as pl
from jax.experimental.pallas import tpu as pltpu
from jax.sharding import Mesh, PartitionSpec as P

EPS = 1e-05
FR = 4
ROWS = 80
LEAD = 8
BF = jnp.bfloat16
F32 = jnp.float32


def nt(a, b):
    return lax.dot_general(a, b, (((1,), (1,)), ((), ())), preferred_element_type=F32)


def nn(a, b):
    return lax.dot_general(a, b, (((1,), (0,)), ((), ())), preferred_element_type=F32)


def tn(a, b):
    return lax.dot_general(a, b, (((0,), (0,)), ((), ())), preferred_element_type=F32)


def roll_rows(values, amount):
    return pltpu.roll(values, amount % values.shape[0], 0)


def sigmoid(values):
    return 0.5 * jnp.tanh(0.5 * values) + 0.5


def inverse_norm(features):
    return lax.rsqrt(jnp.mean(features * features, axis=-1, keepdims=True) + EPS)


def norm_back(d_normed, features, scale, gain):
    scaled = d_normed * gain
    summed = jnp.sum(scaled * features, axis=-1, keepdims=True)
    return scale * scaled - features * (scale * scale * scale * summed * (1.0 / features.shape[-1]))


def bins_conv(values, taps):
    return taps[0:1] * roll_rows(values, 1) + taps[1:2] * values + taps[2:3] * roll_rows(values, -1)


HALVES = (slice(0, 128), slice(128, 256))


def half_weights(gathered_ref, half, first):
    return jnp.concatenate([gathered_ref[2 * half + i, first : first + 64, :] for i in range(2)], axis=0)


def half_taps(gathered_ref, half, first, count):
    parts = []
    for i in range(2):
        both = gathered_ref[2 * half + i, 128:144, :].astype(F32)
        parts.append((both[:, :64] + both[:, 64:])[first : first + count])
    return jnp.concatenate(parts, axis=1)


def pack_kernel(freq_in, freq_taps, freq_out, time_in, time_taps, time_out, packed_ref):
    taps = jnp.concatenate(
        [freq_taps[...]] + [time_taps[k] for k in range(3)] + [jnp.zeros((4, 64), F32)], axis=0
    )
    high = taps.astype(BF).astype(F32)
    low = taps - high
    turn = lambda ref: ref[...].astype(F32).T.astype(BF)
    freq_w = jnp.concatenate([turn(freq_in), freq_out[...]], axis=1)
    time_w = jnp.concatenate([turn(time_in), time_out[...]], axis=1)
    tap_w = jnp.concatenate([high, low], axis=1).astype(BF)
    for peer in range(4):
        packed_ref[peer, 0:64, :] = freq_w
        packed_ref[peer, 64:128, :] = time_w
        packed_ref[peer, 128:144, :] = tap_w


def pack(*weights):
    return pl.pallas_call(
        pack_kernel, out_shape=jax.ShapeDtypeStruct((4, 144, 128), BF), name="pack"
    )(*weights)


def freq_forward_kernel(
    own_ref, halo_ref, cot_ref, cot_edge_ref, gathered_ref, gain_ref, out_ref, hidden_out, rows_ref, tiles_ref
):
    gain = gain_ref[...]
    edges = []
    for part, pair_ref in enumerate((own_ref, halo_ref)):
        features = pair_ref[...].astype(F32)
        normed = (features * inverse_norm(features) * gain).astype(BF)
        mixed = features
        for half, lanes in enumerate(HALVES):
            weights = half_weights(gathered_ref, half, 0)
            hidden = nt(normed, weights[:, :64])
            if part == 0:
                hidden_out[:, lanes] = hidden
            drive = bins_conv(hidden, half_taps(gathered_ref, half, 0, 3))
            active = (drive * sigmoid(drive)).astype(BF)
            mixed = mixed + nn(active, weights[:, 64:])
        rows_ref[...] = mixed
        for f in range(FR):
            even = rows_ref[pl.ds(f * ROWS + LEAD, 32, stride=2), :]
            odd = rows_ref[pl.ds(f * ROWS + LEAD + 1, 32, stride=2), :]
            tiles_ref[pl.ds(FR * part + f, 32, stride=8), :] = jnp.concatenate([even, odd], axis=1)
        for bin_row in (LEAD - 1, LEAD + 64):
            edges.append(
                jnp.concatenate([mixed[f * ROWS + bin_row : f * ROWS + bin_row + 1] for f in range(FR)], axis=0)
            )
    out_ref[:, 0:8, :] = tiles_ref[...].reshape(32, 8, 128).astype(BF)
    out_ref[:, 8:16, :] = cot_ref[...]
    out_ref[2:32, 16:24, :] = jnp.zeros((30, 8, 128), BF)
    for side in range(2):
        x_edge = jnp.concatenate([edges[side], edges[2 + side]], axis=1)
        out_ref[side, 16:24, :] = jnp.concatenate([x_edge, cot_edge_ref[side].astype(F32)], axis=0).astype(BF)


def freq_forward(pair, halo, cot, cot_edge, gathered, gain):
    rows = pair.shape[0]
    return pl.pallas_call(
        freq_forward_kernel,
        out_shape=(jax.ShapeDtypeStruct((32, 24, 128), BF), jax.ShapeDtypeStruct((rows, 256), F32)),
        scratch_shapes=[pltpu.VMEM((rows, 64), F32), pltpu.VMEM((256, 128), F32)],
        name="freq_forward",
    )(pair, halo, cot, cot_edge, gathered, gain)


def freq_backward_kernel(
    flag_ref,
    pair_ref,
    hidden_ref,
    arrived_ref,
    gathered_ref,
    gain_ref,
    time_w_ref,
    time_t_ref,
    time_g_ref,
    out_ref,
    tiles_ref,
    back_ref,
):
    gain = gain_ref[...]
    spread = jnp.concatenate([arrived_ref[...].astype(F32), jnp.zeros((32, 4, 128), F32)], axis=1)
    tiles_ref[...] = spread.reshape(512, 128)
    back_ref[...] = jnp.zeros_like(back_ref)
    left = flag_ref[1].astype(F32)
    for f in range(FR):
        back_ref[pl.ds(f * ROWS + LEAD, 32, stride=2), :] = tiles_ref[pl.ds(f, 32, stride=16), :]
        back_ref[pl.ds(f * ROWS + LEAD + 1, 32, stride=2), :] = tiles_ref[pl.ds(FR + f, 32, stride=16), :]
        back_ref[f * ROWS + LEAD - 1 : f * ROWS + LEAD, :] = tiles_ref[8 + f : 9 + f, :] * left
        back_ref[f * ROWS + LEAD + 64 : f * ROWS + LEAD + 65, :] = tiles_ref[24 + f : 25 + f, :]
    row = lax.broadcasted_iota(jnp.int32, (ROWS, 1), 0)
    upper = LEAD + 64 + flag_ref[0]
    one = jnp.where((row >= LEAD) & (row < upper), 1.0, 0.0).astype(F32)
    own = jnp.concatenate([one] * FR, axis=0)
    features = pair_ref[...].astype(F32)
    scale = inverse_norm(features)
    output, grad_wide = back_ref[:, :64], back_ref[:, 64:]
    grad = grad_wide.astype(BF)
    grad_own = (grad_wide * own).astype(BF)
    normed = (features * scale * gain * own).astype(BF)
    d_normed = None
    tap_halves = []
    for half, lanes in enumerate(HALVES):
        weights = half_weights(gathered_ref, half, 0)
        taps = half_taps(gathered_ref, half, 0, 3)
        hidden = hidden_ref[:, lanes]
        before, after = roll_rows(hidden, 1), roll_rows(hidden, -1)
        drive = taps[0:1] * before + taps[1:2] * hidden + taps[2:3] * after
        gate = sigmoid(drive)
        active = drive * gate
        slope = gate + active * (1.0 - gate)
        grad_out = tn(active.astype(BF), grad_own)
        d_drive = nt(grad, weights[:, 64:]) * slope
        d_own = d_drive * own
        tap_halves.append(
            [jnp.sum(d_own * moved, axis=0, keepdims=True) for moved in (before, hidden, after)]
        )
        d_hidden = (
            taps[0:1] * roll_rows(d_drive, -1) + taps[1:2] * d_drive + taps[2:3] * roll_rows(d_drive, 1)
        ).astype(BF)
        grad_in = tn(d_hidden, normed)
        both = jnp.concatenate([grad_out, grad_in], axis=1).astype(BF)
        for i in range(2):
            out_ref[2 * half + i, 288:352, :] = both[64 * i : 64 * i + 64]
        part = nn(d_hidden, weights[:, :64])
        d_normed = part if d_normed is None else d_normed + part
    freq_g = jnp.sum(d_normed * features * (scale * own), axis=0, keepdims=True)
    d_signal = grad_wide + norm_back(d_normed, features, scale, gain)
    done = jnp.concatenate([output, d_signal], axis=1)
    done = jnp.concatenate([done[f * ROWS + LEAD : (f + 1) * ROWS] for f in range(FR)], axis=0).astype(BF)
    gains = jnp.concatenate([freq_g, time_g_ref[...]], axis=1)
    for peer in range(4):
        half, at = peer // 2, 64 * (peer % 2)
        rows = [tap[:, at : at + 64] for tap in tap_halves[half]]
        rows.append(time_t_ref[:, 64 * peer : 64 * peer + 64])
        taps = jnp.concatenate(rows, axis=0)
        taps = jnp.concatenate([taps, jnp.zeros((12, 64), F32)], axis=1)
        out_ref[peer, 0:288, :] = done
        out_ref[peer, 352:416, :] = time_w_ref[64 * peer : 64 * peer + 64, :].astype(BF)
        out_ref[peer, 416:432, :] = jnp.concatenate([taps, gains, jnp.zeros((3, 128), F32)], axis=0).astype(BF)


def freq_backward(pair, hidden, arrived, gathered, gain, flags, sums):
    vmem = pl.BlockSpec(memory_space=pltpu.VMEM)
    return pl.pallas_call(
        freq_backward_kernel,
        out_shape=jax.ShapeDtypeStruct((4, 432, 128), BF),
        in_specs=[pl.BlockSpec(memory_space=pltpu.SMEM)] + [vmem] * 8,
        scratch_shapes=[pltpu.VMEM((512, 128), F32), pltpu.VMEM((FR * ROWS, 128), F32)],
        name="freq_backward",
    )(flags, pair, hidden, arrived, gathered, gain, *sums)


def turned(tiles):
    return jnp.concatenate(
        [roll_rows(tiles[8 * i : 8 * i + 8], 4) for i in range(tiles.shape[0] // 8)], axis=0
    )


def groups_on(values, count):
    if count > 0:
        return jnp.concatenate([values[8 * count :], turned(values[: 8 * count])], axis=0)
    base = values.shape[0] + 8 * count
    return jnp.concatenate([turned(values[base:]), values[:base]], axis=0)


def later(values, spacing, place):
    if spacing == 1:
        return jnp.where(place == 3, roll_rows(groups_on(values, 1), 3), roll_rows(values, -1))
    return groups_on(values, spacing // FR)


def earlier(values, spacing, place):
    if spacing == 1:
        return jnp.where(place == 0, roll_rows(groups_on(values, -1), -3), roll_rows(values, 1))
    return groups_on(values, -(spacing // FR))


def own_rows(values):
    tiles = values.reshape(values.shape[0] // 8, 8, values.shape[1])
    return jnp.sum(jnp.sum(tiles, axis=0)[:4], axis=0, keepdims=True)


def one_bin(message_ref, first, slot):
    if slot < 2:
        both = message_ref[:, 8 * first : 8 * first + 8].astype(F32).reshape(256, 128)
        return both[:, 64 * slot : 64 * slot + 64]
    edge = message_ref[:, 16:24].astype(F32)[:, 4 * first : 4 * first + 4]
    return jnp.concatenate([edge[:, :, :64], edge[:, :, 64:]], axis=1).reshape(256, 64)


def time_kernel(flag_ref, message_ref, marks_ref, gathered_ref, gain_ref, out_ref, grad_ref, tap_ref, gain_out):
    gain = gain_ref[...]
    valid, inside = marks_ref[:, 0:1], marks_ref[:, 1:2]
    spot = lax.broadcasted_iota(jnp.int32, (256, 1), 0)
    place = lax.broadcasted_iota(jnp.int32, (256, 128), 0) & 3
    for slot in range(3):
        share = jnp.where(flag_ref[0] > 0, 1.0, 0.0).astype(F32) if slot == 2 else 1.0

        def keep(ref, rows, lanes, value):
            if slot == 0:
                ref[rows, lanes] = value
            else:
                ref[rows, lanes] += value

        counted = jnp.where((spot & 7) < 4, share, 0.0).astype(F32)
        features, grad_wide = one_bin(message_ref, 0, slot), one_bin(message_ref, 1, slot)
        grad = grad_wide.astype(BF)
        grad_own = (grad_wide * counted).astype(BF)
        scale = inverse_norm(features)
        normed = features * scale * gain
        normed_own = (normed * counted).astype(BF)
        normed = normed.astype(BF)
        mixed, d_normed = features, None
        for half, lanes in enumerate(HALVES):
            weights = half_weights(gathered_ref, half, 64)
            weight_in, weight_out = weights[:, :64], weights[:, 64:]
            taps = half_taps(gathered_ref, half, 3, 9)
            state = nt(normed, weight_in) * valid
            states, slopes = [], []
            for layer in range(3):
                spacing = (1, 4, 16)[layer]
                row = taps[3 * layer : 3 * layer + 3]
                drive = (
                    row[0:1] * earlier(state, spacing, place)
                    + row[1:2] * state
                    + row[2:3] * later(state, spacing, place)
                )
                gate = sigmoid(drive)
                active = drive * gate
                states.append(state)
                slopes.append(gate + active * (1.0 - gate))
                state = state + active
                if layer < 2:
                    state = state * inside
            top = state.astype(BF)
            mixed = mixed + nn(top, weight_out)
            keep(grad_ref, lanes, slice(0, 64), tn(top, grad_own))
            d_state = nt(grad, weight_out)
            for layer in reversed(range(3)):
                spacing = (1, 4, 16)[layer]
                row = taps[3 * layer : 3 * layer + 3]
                d_drive = d_state * slopes[layer]
                if layer < 2:
                    d_drive = d_drive * inside
                held = states[layer]
                for j, moved in enumerate((earlier(held, spacing, place), held, later(held, spacing, place))):
                    at = 3 * layer + j
                    keep(tap_ref, slice(at, at + 1), lanes, own_rows(d_drive * moved) * share)
                d_state = d_state + (
                    row[0:1] * later(d_drive, spacing, place)
                    + row[1:2] * d_drive
                    + row[2:3] * earlier(d_drive, spacing, place)
                )
            d_pre = (d_state * valid).astype(BF)
            keep(grad_ref, lanes, slice(64, 128), tn(d_pre, normed_own))
            part = nn(d_pre, weight_in)
            d_normed = part if d_normed is None else d_normed + part
        keep(gain_out, slice(0, 1), slice(0, 64), own_rows(d_normed * features * scale) * share)
        d_one = grad_wide + norm_back(d_normed, features, scale, gain)
        both = jnp.concatenate([mixed, d_one], axis=1).reshape(32, 8, 128)
        out_ref[:, 4 * slot : 4 * slot + 4] = both[:, :4].astype(BF)


def time_path(message, marks, gathered, gain, flag):
    vmem = pl.BlockSpec(memory_space=pltpu.VMEM)
    return pl.pallas_call(
        time_kernel,
        out_shape=(
            jax.ShapeDtypeStruct((32, 12, 128), BF),
            jax.ShapeDtypeStruct((256, 128), F32),
            jax.ShapeDtypeStruct((9, 256), F32),
            jax.ShapeDtypeStruct((1, 64), F32),
        ),
        in_specs=[pl.BlockSpec(memory_space=pltpu.SMEM)] + [vmem] * 4,
        name="time_path",
    )(flag.reshape(1), message, marks, gathered, gain)


def finish_kernel(
    scale, part_ref, freq_gain, freq_in, freq_taps, freq_out, time_gain, time_in, time_taps, time_out, rows_ref
):
    for i in range(8):
        rows_ref[18 * i : 18 * i + 18, :] = part_ref[i] * scale
    freq_out[...] = rows_ref[0:64, :64]
    freq_in[...] = rows_ref[0:64, :][:, 64:].T
    time_out[...] = rows_ref[64:128, :64]
    time_in[...] = rows_ref[64:128, :][:, 64:].T
    gains = rows_ref[140:141, :]
    freq_gain[...] = gains[:, :64]
    time_gain[...] = gains[:, 64:]
    freq_taps[...] = rows_ref[128:131, :64]
    for k in range(3):
        time_taps[k] = rows_ref[131 + 3 * k : 134 + 3 * k, :64]


def finish(total, scale):
    shape = lambda *dims: jax.ShapeDtypeStruct(dims, F32)
    got = pl.pallas_call(
        functools.partial(finish_kernel, scale),
        out_shape=(
            shape(1, 64),
            shape(64, 64),
            shape(3, 64),
            shape(64, 64),
            shape(1, 64),
            shape(64, 64),
            shape(3, 3, 64),
            shape(64, 64),
        ),
        scratch_shapes=[pltpu.VMEM((144, 128), F32)],
        name="finish",
    )(total)
    return (got[0][0], got[1], got[2], got[3], got[4][0], got[5], got[6], got[7])


def plane_lanes(values, plane):
    frames, width = values.shape
    padded = jnp.pad(values, ((0, 0), (LEAD * 64, (ROWS - LEAD + 192) * 64 - width)))
    return lax.dynamic_slice(padded, (0, plane * 4096), (frames, ROWS * 64))


def cot_message(own, halo):
    both = jnp.concatenate([own, halo], axis=0)
    mine = both[:, LEAD * 64 : LEAD * 64 + 4096].reshape(2 * FR, 32, 128).transpose(1, 0, 2)
    edge = jnp.stack([both[:, LEAD * 64 - 64 : LEAD * 64], both[:, LEAD * 64 + 4096 : LEAD * 64 + 4160]], axis=0)
    return mine, jnp.concatenate([edge[:, :FR], edge[:, FR:]], axis=2)


def frame_marks(counts, x_at):
    by_plane = jnp.pad(counts.reshape(4, 32), ((1, 1), (0, 0)))
    window = lax.dynamic_slice(by_plane, (x_at, 0), (3, 32))
    spot = jnp.arange(32)
    halo_count = jnp.where(spot >= 16, window[0], window[2])
    halo_in = jnp.where(spot >= 16, (spot >= 21) & (x_at > 0), (spot <= 10) & (x_at < 3))
    limit = jnp.stack([window[1], halo_count], axis=1)
    valid = (jnp.arange(4) < limit[:, :, None]) & jnp.stack([spot >= 0, halo_in], axis=1)[:, :, None]
    inside = jnp.stack([spot >= 0, halo_in], axis=1)[:, :, None] & (jnp.arange(4) >= 0)
    return jnp.stack([valid.reshape(256), inside.reshape(256)], axis=1).astype(F32)


def outputs_of(arrived):
    rows = arrived[:, :288].reshape(4, FR, 72, 128)
    whole = jnp.concatenate([rows[0, :, :64], rows[1, :, :64], rows[2, :, :64], rows[3, :, :65]], axis=1)
    return whole[:, :, :64].reshape(FR, -1), whole[:, :, 64:].reshape(FR, -1)


def halo_pairs():
    pairs = []
    for x_at in range(4):
        for spot in range(32):
            if spot <= 10 and x_at < 3:
                pairs.append(((x_at + 1) * 32 + spot, x_at * 32 + spot))
            if spot >= 21 and x_at > 0:
                pairs.append(((x_at - 1) * 32 + spot, x_at * 32 + spot))
    return pairs


SEQ = ("x", "z", "core")


def exchange(values, axes):
    return lax.all_to_all(values, axes, 0, 0)


def shards(
    signal, cotangent, counts, freq_gain, freq_in, freq_taps, freq_out, time_gain, time_in, time_taps, time_out
):
    plane = lax.axis_index("ch")
    x_at = lax.axis_index("x")
    spot = lax.axis_index(("z", "core"))
    grad_scale = 1.0 / math.sqrt(FR * 128 * (signal.shape[1] // 64))
    packed = pack(freq_in, freq_taps, freq_out, time_in, time_taps, time_out)
    gathered = exchange(packed, "ch")
    lanes = jnp.stack([plane_lanes(signal, plane), plane_lanes(cotangent, plane)], axis=0)
    halo = lax.ppermute(lanes, SEQ, halo_pairs())
    gain_f, gain_t = freq_gain[None], time_gain[None]
    x_rows, x_halo = lanes[0].reshape(FR * ROWS, 64), halo[0].reshape(FR * ROWS, 64)
    message, hidden = freq_forward(x_rows, x_halo, *cot_message(lanes[1], halo[1]), gathered, gain_f)
    bands = exchange(message, ("z", "core"))
    marks = frame_marks(counts, x_at)
    edge = jnp.where((plane == 3) & (spot == 1), 1, 0)
    mixed, *sums = time_path(bands, marks, gathered, gain_t, edge)
    arrived = exchange(mixed, ("z", "core"))
    flags = jnp.stack([jnp.where(plane == 3, 1, 0), jnp.where(plane > 0, 1, 0)])
    planes = exchange(freq_backward(x_rows, hidden, arrived, gathered, gain_f, flags, sums), "ch")
    part = jnp.sum(planes[:, 288:].astype(F32), axis=0).reshape(8, 18, 128)
    part = jnp.sum(exchange(part, ("x", "core")), axis=0).astype(BF)
    part = jnp.sum(exchange(jnp.broadcast_to(part, (16, 18, 128)), "z").astype(F32), axis=0)
    total = exchange(jnp.broadcast_to(part, (8, 18, 128)), ("x", "core"))
    return outputs_of(planes) + finish(total, grad_scale)


def solution(mesh):
    torus = Mesh(mesh.devices.reshape(4, 16, 2, 4), ("x", "z", "core", "ch"))
    return jax.shard_map(
        shards,
        mesh=torus,
        in_specs=(
            P(SEQ, None),
            P(SEQ, None),
            P(),
            P(),
            P(None, "ch"),
            P(None, "ch"),
            P("ch", None),
            P(),
            P(None, "ch"),
            P(None, None, "ch"),
            P("ch", None),
        ),
        out_specs=(
            P(SEQ, None),
            P(SEQ, None),
            P(),
            P(None, "ch"),
            P(None, "ch"),
            P("ch", None),
            P(),
            P(None, "ch"),
            P(None, None, "ch"),
            P("ch", None),
        ),
        check_vma=False,
    )
```

time: 166 us -> 140 us (0.84)
  waiting for transfers between devices: 69.7 us -> 53.8 us
  local copies, waits for them, and re-layouts: 22.1 us -> 11 us
  blocking collectives: 0 us -> 10.8 us
  starting transfers between devices: 54 us -> 45.1 us
  Pallas kernels: 13.7 us -> 15.7 us
  other arithmetic: 3.97 us -> 2.29 us
    all_to_all x8 -> x6, waiting for transfers between devices: 69.7 us -> 53.8 us  [exchange(): return lax.all_to_all(values, axes, 0, 0)]
    all_to_all x0 -> x1, blocking collectives: none -> 10.8 us  [exchange(): return lax.all_to_all(values, axes, 0, 0)]
    all_to_all x8 -> x6, starting transfers between devices: 52.8 us -> 43.8 us  [exchange(): return lax.all_to_all(values, axes, 0, 0)]
    reshape x12 -> x1, local copies, waits for them, and re-layouts: 4.01 us -> 0.65 us  [shards(): part = jnp.sum(planes[:, 288:].astype(F32), axis=0).reshape(8, 18, 128)]
    slice x11 -> x1, local copies, waits for them, and re-layouts: 2.37 us -> 0.02 us  [outputs_of(): rows = arrived[:, :288].reshape(4, FR, 72, 128)]
    concatenate x3 -> x0, local copies, waits for them, and re-layouts: 1.97 us -> none  [the longest x1 1.89 us: from_frames(): jnp.concatenate([jnp.zeros((FR, LEAD - 1, 128), BF), left, mine, right, j...]
    pallas_call x2 -> x3, Pallas kernels: 5.39 us -> 7.3 us  [the longest x1 3.03 us: freq_backward(): pl.pallas_call(freq_backward_kernel, out_shape=jax.ShapeDtypeStruct((4, 4...]
    unnamed x43 -> x11, local copies, waits for them, and re-layouts: 4.96 us -> 3.38 us
  transfers between devices with their start and end apart: 9 -> 7, of which waited for: 8 -> 6; matrix products, arithmetic and copies ran while one was open for 7% -> 5% of each run, Pallas kernels for 2% -> 1%
where the time goes in v4:
time: 140 us
  waiting for transfers between devices  53.8 us (38%)
  starting transfers between devices  45.1 us (32%)
  Pallas kernels  15.7 us (11%)
  local copies, waits for them, and re-layouts  11 us (8%)
  blocking collectives  10.8 us (8%)
  other arithmetic  2.29 us (2%)
    all_to_all x6, waiting for transfers between devices, exchange(): return lax.all_to_all(values, axes, 0, 0)  53.8 us
    all_to_all x6, starting transfers between devices, exchange(): return lax.all_to_all(values, axes, 0, 0)  43.8 us
    all_to_all x1, blocking collectives, exchange(): return lax.all_to_all(values, axes, 0, 0)  10.8 us
    pallas_call x1, Pallas kernels, time_path(): pl.pallas_call(time_kernel, out_shape=(jax.ShapeDtypeStruct((32, 12, 128)...  6.72 us
    unnamed x11, local copies, waits for them, and re-layouts  3.38 us
    pallas_call x1, Pallas kernels, freq_backward(): pl.pallas_call(freq_backward_kernel, out_shape=jax.ShapeDtypeStruct((4, 4...  3.03 us
  transfers between devices with their start and end apart: 7, of which 6 were waited for; matrix products, arithmetic and copies ran while one was open for 5% of the time, Pallas kernels for 1%

profile of v4, /device:TPU:1, one launch (start us, length us, event | category | flops | bytes accessed | tf_op | source)
XLA Modules:
  0.0 139.5 jit_solution(2198797822591010331)
XLA Ops:
  0.6 0.9 pad_dynamic-slice_fusion
  1.5 0.1 pad_maximum_fusion.1
  1.6 1.3 collective-permute-start
  2.9 1.6 %pack.1 = bf16[4,144,128]{2,1,0:T(8,128)(2,1)} custom-call(bf16[64,64]{1,0:T(8,128)(2,1)} %freq_in.1, f32[3,64]{1,0:T(4,128)} %freq_taps.1, bf16[64,64]{1,0:T(8,128)(2,1)} %freq_out.1, bf16[64,64]{1,0:T(8,128)(2,1)} %time_in.1, f32[3,3,64]{2,1,0:T(4,128)} %time_taps.1, bf16[64,64]{1,0:T(8,128)(2,1)} %time_out.1), custom_call_target="tpu_custom_call" | custom-call | tf_op jit(solution)/shard_map/pack/pallas_call | solution.py:85
  4.5 5.0 %all-to-all-start = ((bf16[4,144,128]{2,1,0:T(8,128)(2,1)}), bf16[4,144,128]{2,1,0:T(8,128)(2,1)S(1)}, u32[]{:S(2)}, u32[]{:S(2)}) async-start(bf16[4,144,128]{2,1,0:T(8,128)(2,1)} %pack.1), calls=%async_computation | async-start | bytes 294912 | tf_op jit(solution)/shard_map/all_to_all | solution.py:430
  9.5 0.7 copy-done.4
  10.1 0.1 reshape.129
  10.3 0.8 reshape_squeeze_stack.3.own_ref.pair_ref
  11.0 0.0 collective-permute-done
  11.1 0.1 fusion.6
  11.1 0.7 fusion.1.cot_ref
  11.8 0.8 reshape_squeeze.3.halo_ref
  12.6 0.7 fusion.4.cot_edge_ref
  13.2 1.2 all-to-all-done.gathered_ref
  14.4 0.6 copy-done
  15.0 2.7 %freq_forward.1 = (bf16[32,24,128]{2,1,0:T(8,128)(2,1)}, f32[320,256]{1,0:T(8,128)}) custom-call(bf16[320,64]{1,0:T(8,128)(2,1)} %reshape_squeeze_stack.3.own_ref.pair_ref, bf16[320,64]{1,0:T(8,128)(2,1)} %reshape_squeeze.3.halo_ref, bf16[32,8,128]{2,1,0:T(8,128)(2,1)} %fusion.1.cot_ref, bf16[2,4,128]{2,1,0:T(4,128)(2,1)} %fusion.4.cot_edge_ref, ...), custom_call_target="tpu_custom_call" | custom-call | tf_op jit(solution)/shard_map/freq_forward/pallas_call | solution.py:126
  17.7 18.1 %all-to-all-start.1 = ((bf16[32,24,128]{2,1,0:T(8,128)(2,1)}), bf16[32,24,128]{2,1,0:T(8,128)(2,1)S(1)}, u32[]{:S(2)}, u32[]{:S(2)}) async-start(bf16[32,24,128]{2,1,0:T(8,128)(2,1)} %get-tuple-element.25), calls=%async_computation.1 | async-start | bytes 393216 | tf_op jit(solution)/shard_map/all_to_all | solution.py:430
  35.9 0.1 copy.42
  36.0 0.1 stack.52.clone
  36.1 0.1 and.63
  36.2 0.1 and.64
  36.3 0.1 copy.38
  36.4 0.1 iota_compare_fusion
  36.5 0.1 lt.38
  36.7 0.8 copy.40.marks_ref
  37.5 17.2 %all-to-all-done.1.message_ref = bf16[32,24,128]{2,1,0:T(8,128)(2,1)S(1)} async-done(((bf16[32,24,128]{2,1,0:T(8,128)(2,1)}), bf16[32,24,128]{2,1,0:T(8,128)(2,1)S(1)}, u32[]{:S(2)}, u32[]{:S(2)}) %all-to-all-start.1) | async-done | bytes 196640 | tf_op jit(solution)/shard_map/all_to_all | solution.py:430
  54.7 0.7 copy-done.1
  55.3 6.7 %time_path.1 = (bf16[32,12,128]{2,1,0:T(8,128)(2,1)}, f32[256,128]{1,0:T(8,128)}, f32[9,256]{1,0:T(8,128)}, f32[1,64]{1,0:T(1,128)}) custom-call(s32[1]{0:T(128)} %bitcast.10.flag_ref, bf16[32,24,128]{2,1,0:T(8,128)(2,1)} %copy-done.1, f32[256,2]{1,0:T(8,128)} %copy.40.marks_ref, bf16[4,144,128]{2,1,0:T(8,128)(2,1)} %copy-done, f32[1,64]{1,0:T(1,128)} %bitcast.40), custom_call_target="tpu_custom_call" | custom-call | tf_op jit(solution)/shard_map/time_path/pallas_call | solution.py:334
  62.0 5.0 %all-to-all-start.2 = ((bf16[32,12,128]{2,1,0:T(8,128)(2,1)}), bf16[32,12,128]{2,1,0:T(8,128)(2,1)S(1)}, u32[]{:S(2)}, u32[]{:S(2)}) async-start(bf16[32,12,128]{2,1,0:T(8,128)(2,1)} %get-tuple-element.26), calls=%async_computation.2 | async-start | bytes 262144 | tf_op jit(solution)/shard_map/all_to_all | solution.py:430
  67.0 0.6 pad_add_fusion.1.flag_ref
  67.6 15.6 %all-to-all-done.2.arrived_ref = bf16[32,12,128]{2,1,0:T(8,128)(2,1)S(1)} async-done(((bf16[32,12,128]{2,1,0:T(8,128)(2,1)}), bf16[32,12,128]{2,1,0:T(8,128)(2,1)S(1)}, u32[]{:S(2)}, u32[]{:S(2)}) %all-to-all-start.2) | async-done | bytes 98336 | tf_op jit(solution)/shard_map/all_to_all | solution.py:430
  83.2 0.7 copy-done.2
  83.9 3.0 %freq_backward.1 = bf16[4,432,128]{2,1,0:T(8,128)(2,1)} custom-call(s32[2]{0:T(128)} %pad_add_fusion.1.flag_ref, bf16[320,64]{1,0:T(8,128)(2,1)} %reshape_squeeze_stack.3.own_ref.pair_ref, f32[320,256]{1,0:T(8,128)} %get-tuple-element.24.hidden_ref, bf16[32,12,128]{2,1,0:T(8,128)(2,1)} %copy-done.2, bf16[4,144,128]{2,1,0:T(8,128)(2,1)} %copy-done, ...), custom_call_target="tpu_custom_call" | custom-call | tf_op jit(solution)/shard_map/freq_backward/pallas_call | solution.py:212
  86.9 10.8 %all_to_all.35 = bf16[4,432,128]{2,1,0:T(8,128)(2,1)S(1)} all-to-all(bf16[4,432,128]{2,1,0:T(8,128)(2,1)} %freq_backward.1), channel_id=1, replica_groups=mesh['x'=4,'z'=16,'core'=2,'ch'=4] {'ch'}, dimensions={0} | all-to-all | bytes 884736 | tf_op jit(solution)/shard_map/all_to_all | solution.py:430
  97.7 0.6 reshape.133
  98.4 6.2 %all-to-all-start.4 = ((f32[8,18,128]{2,1,0:T(8,128)}), f32[8,18,128]{2,1,0:T(8,128)S(1)}, u32[]{:S(2)}, u32[]{:S(2)}) async-start(f32[8,18,128]{2,1,0:T(8,128)} %reshape.133), calls=%async_computation.4 | async-start | bytes 196608 | tf_op jit(solution)/shard_map/all_to_all | solution.py:430
  104.6 4.9 %all-to-all-done.4 = f32[8,18,128]{2,1,0:T(8,128)S(1)} async-done(((f32[8,18,128]{2,1,0:T(8,128)}), f32[8,18,128]{2,1,0:T(8,128)S(1)}, u32[]{:S(2)}, u32[]{:S(2)}) %all-to-all-start.4) | async-done | bytes 73760 | tf_op jit(solution)/shard_map/all_to_all | solution.py:430
  109.6 0.7 broadcast_in_dim.19
  110.2 3.5 %all-to-all-start.5 = ((bf16[16,18,128]{2,1,0:T(8,128)(2,1)}), bf16[16,18,128]{2,1,0:T(8,128)(2,1)S(1)}, u32[]{:S(2)}, u32[]{:S(2)}) async-start(bf16[16,18,128]{2,1,0:T(8,128)(2,1)} %broadcast_in_dim.19), calls=%async_computation.5 | async-start | bytes 196608 | tf_op jit(solution)/shard_map/all_to_all | solution.py:430
  113.8 11.8 %all-to-all-done.5 = bf16[16,18,128]{2,1,0:T(8,128)(2,1)S(1)} async-done(((bf16[16,18,128]{2,1,0:T(8,128)(2,1)}), bf16[16,18,128]{2,1,0:T(8,128)(2,1)S(1)}, u32[]{:S(2)}, u32[]{:S(2)}) %all-to-all-start.5) | async-done | bytes 73760 | tf_op jit(solution)/shard_map/all_to_all | solution.py:430
  125.6 0.7 broadcast_in_dim.20
  126.2 6.0 %all-to-all-start.6 = ((f32[8,18,128]{2,1,0:T(8,128)}), f32[8,18,128]{2,1,0:T(8,128)S(1)}, u32[]{:S(2)}, u32[]{:S(2)}) async-start(f32[8,18,128]{2,1,0:T(8,128)} %broadcast_in_dim.20), calls=%async_computation.6 | async-start | bytes 196608 | tf_op jit(solution)/shard_map/all_to_all | solution.py:430
  132.2 0.1 fusion.7
  132.3 0.9 reshape.132
  133.2 0.9 reshape.131
  134.1 3.1 %all-to-all-done.6.part_ref = f32[8,18,128]{2,1,0:T(8,128)S(1)} async-done(((f32[8,18,128]{2,1,0:T(8,128)}), f32[8,18,128]{2,1,0:T(8,128)S(1)}, u32[]{:S(2)}, u32[]{:S(2)}) %all-to-all-start.6) | async-done | bytes 73760 | tf_op jit(solution)/shard_map/all_to_all | solution.py:430
  137.2 0.6 copy-done.3
  137.9 1.7 %finish.1 = (f32[1,64]{1,0:T(1,128)}, f32[64,64]{1,0:T(8,128)}, f32[3,64]{1,0:T(4,128)}, f32[64,64]{1,0:T(8,128)}, f32[1,64]{1,0:T(1,128)}, /*index=5*/f32[64,64...) custom-call(f32[8,18,128]{2,1,0:T(8,128)} %copy-done.3), custom_call_target="tpu_custom_call" | custom-call | tf_op jit(solution)/shard_map/finish/pallas_call | solution.py:366
  (21 shorter events, 0.2 us)
Async XLA Ops:
  1.6 9.4 %collective-permute-start = (bf16[2,4,5120]{2,1,0:T(4,128)(2,1)S(1)}, bf16[2,4,5120]{2,1,0:T(4,128)(2,1)S(1)}, u32[]{:S(2)}, u32[]{:S(2)}) collective-permute-start(bf16[2,4,5120]{2,1,0:T(4,128)(2,1)S(1)} %pad_maximum_fusion.1), channel_id=1, source_target_pairs={{128,0},{132,4},{136,8},{140,12},{144,16},{148,20},{152,24},{156,2... | collective-permute-start | bytes 245768 | tf_op jit(solution)/shard_map/ppermute | solution.py:443
  4.5 9.9 %all-to-all-start = ((bf16[4,144,128]{2,1,0:T(8,128)(2,1)}), bf16[4,144,128]{2,1,0:T(8,128)(2,1)S(1)}, u32[]{:S(2)}, u32[]{:S(2)}) async-start(bf16[4,144,128]{2,1,0:T(8,128)(2,1)} %pack.1), calls=%async_computation | async-start | bytes 294912 | tf_op jit(solution)/shard_map/all_to_all | solution.py:430
  9.5 0.7 copy-start.4
  14.4 0.7 copy-start
  17.7 36.9 %all-to-all-start.1 = ((bf16[32,24,128]{2,1,0:T(8,128)(2,1)}), bf16[32,24,128]{2,1,0:T(8,128)(2,1)S(1)}, u32[]{:S(2)}, u32[]{:S(2)}) async-start(bf16[32,24,128]{2,1,0:T(8,128)(2,1)} %get-tuple-element.25), calls=%async_computation.1 | async-start | bytes 393216 | tf_op jit(solution)/shard_map/all_to_all | solution.py:430
  54.7 0.7 copy-start.1
  62.0 21.2 %all-to-all-start.2 = ((bf16[32,12,128]{2,1,0:T(8,128)(2,1)}), bf16[32,12,128]{2,1,0:T(8,128)(2,1)S(1)}, u32[]{:S(2)}, u32[]{:S(2)}) async-start(bf16[32,12,128]{2,1,0:T(8,128)(2,1)} %get-tuple-element.26), calls=%async_computation.2 | async-start | bytes 262144 | tf_op jit(solution)/shard_map/all_to_all | solution.py:430
  83.2 0.7 copy-start.2
  98.4 11.2 %all-to-all-start.4 = ((f32[8,18,128]{2,1,0:T(8,128)}), f32[8,18,128]{2,1,0:T(8,128)S(1)}, u32[]{:S(2)}, u32[]{:S(2)}) async-start(f32[8,18,128]{2,1,0:T(8,128)} %reshape.133), calls=%async_computation.4 | async-start | bytes 196608 | tf_op jit(solution)/shard_map/all_to_all | solution.py:430
  110.2 15.3 %all-to-all-start.5 = ((bf16[16,18,128]{2,1,0:T(8,128)(2,1)}), bf16[16,18,128]{2,1,0:T(8,128)(2,1)S(1)}, u32[]{:S(2)}, u32[]{:S(2)}) async-start(bf16[16,18,128]{2,1,0:T(8,128)(2,1)} %broadcast_in_dim.19), calls=%async_computation.5 | async-start | bytes 196608 | tf_op jit(solution)/shard_map/all_to_all | solution.py:430
  126.2 11.0 %all-to-all-start.6 = ((f32[8,18,128]{2,1,0:T(8,128)}), f32[8,18,128]{2,1,0:T(8,128)S(1)}, u32[]{:S(2)}, u32[]{:S(2)}) async-start(f32[8,18,128]{2,1,0:T(8,128)} %broadcast_in_dim.20), calls=%async_computation.6 | async-start | bytes 196608 | tf_op jit(solution)/shard_map/all_to_all | solution.py:430
  137.2 0.6 copy-start.3

commit v5 on v4

--- a/solution.py
+++ b/solution.py
@@ -12,6 +12,7 @@
 FR = 4
 ROWS = 80
 LEAD = 8
+EDGE = 16
 BF = jnp.bfloat16
 F32 = jnp.float32
 
@@ -48,6 +49,10 @@
 
 def bins_conv(values, taps):
     return taps[0:1] * roll_rows(values, 1) + taps[1:2] * values + taps[2:3] * roll_rows(values, -1)
+
+
+VMEM = pl.BlockSpec(memory_space=pltpu.VMEM)
+SMEM = pl.BlockSpec(memory_space=pltpu.SMEM)
 
 
 HALVES = (slice(0, 128), slice(128, 256))
@@ -115,10 +120,11 @@
             )
     out_ref[:, 0:8, :] = tiles_ref[...].reshape(32, 8, 128).astype(BF)
     out_ref[:, 8:16, :] = cot_ref[...]
-    out_ref[2:32, 16:24, :] = jnp.zeros((30, 8, 128), BF)
+    out_ref[0:EDGE, 16:24, :] = jnp.zeros((EDGE, 8, 128), BF)
+    out_ref[EDGE + 2 : 32, 16:24, :] = jnp.zeros((30 - EDGE, 8, 128), BF)
     for side in range(2):
         x_edge = jnp.concatenate([edges[side], edges[2 + side]], axis=1)
-        out_ref[side, 16:24, :] = jnp.concatenate([x_edge, cot_edge_ref[side].astype(F32)], axis=0).astype(BF)
+        out_ref[EDGE + side, 16:24, :] = jnp.concatenate([x_edge, cot_edge_ref[side].astype(F32)], axis=0).astype(BF)
 
 
 def freq_forward(pair, halo, cot, cot_edge, gathered, gain):
@@ -126,7 +132,10 @@
     return pl.pallas_call(
         freq_forward_kernel,
         out_shape=(jax.ShapeDtypeStruct((32, 24, 128), BF), jax.ShapeDtypeStruct((rows, 256), F32)),
-        scratch_shapes=[pltpu.VMEM((rows, 64), F32), pltpu.VMEM((256, 128), F32)],
+        scratch_shapes=[
+            pltpu.VMEM((rows, 64), F32),
+            pltpu.VMEM((256, 128), F32),
+        ],
         name="freq_forward",
     )(pair, halo, cot, cot_edge, gathered, gain)
 
@@ -153,8 +162,8 @@
     for f in range(FR):
         back_ref[pl.ds(f * ROWS + LEAD, 32, stride=2), :] = tiles_ref[pl.ds(f, 32, stride=16), :]
         back_ref[pl.ds(f * ROWS + LEAD + 1, 32, stride=2), :] = tiles_ref[pl.ds(FR + f, 32, stride=16), :]
-        back_ref[f * ROWS + LEAD - 1 : f * ROWS + LEAD, :] = tiles_ref[8 + f : 9 + f, :] * left
-        back_ref[f * ROWS + LEAD + 64 : f * ROWS + LEAD + 65, :] = tiles_ref[24 + f : 25 + f, :]
+        back_ref[f * ROWS + LEAD - 1 : f * ROWS + LEAD, :] = tiles_ref[16 * EDGE + 8 + f : 16 * EDGE + 9 + f, :] * left
+        back_ref[f * ROWS + LEAD + 64 : f * ROWS + LEAD + 65, :] = tiles_ref[16 * EDGE + 24 + f : 16 * EDGE + 25 + f, :]
     row = lax.broadcasted_iota(jnp.int32, (ROWS, 1), 0)
     upper = LEAD + 64 + flag_ref[0]
     one = jnp.where((row >= LEAD) & (row < upper), 1.0, 0.0).astype(F32)
@@ -166,7 +175,7 @@
     grad_own = (grad_wide * own).astype(BF)
     normed = (features * scale * gain * own).astype(BF)
     d_normed = None
-    tap_halves = []
+    tap_halves, freq_w = [], []
     for half, lanes in enumerate(HALVES):
         weights = half_weights(gathered_ref, half, 0)
         taps = half_taps(gathered_ref, half, 0, 3)
@@ -186,9 +195,7 @@
             taps[0:1] * roll_rows(d_drive, -1) + taps[1:2] * d_drive + taps[2:3] * roll_rows(d_drive, 1)
         ).astype(BF)
         grad_in = tn(d_hidden, normed)
-        both = jnp.concatenate([grad_out, grad_in], axis=1).astype(BF)
-        for i in range(2):
-            out_ref[2 * half + i, 288:352, :] = both[64 * i : 64 * i + 64]
+        freq_w.append(jnp.concatenate([grad_out, grad_in], axis=1))
         part = nn(d_hidden, weights[:, :64])
         d_normed = part if d_normed is None else d_normed + part
     freq_g = jnp.sum(d_normed * features * (scale * own), axis=0, keepdims=True)
@@ -203,17 +210,26 @@
         taps = jnp.concatenate(rows, axis=0)
         taps = jnp.concatenate([taps, jnp.zeros((12, 64), F32)], axis=1)
         out_ref[peer, 0:288, :] = done
-        out_ref[peer, 352:416, :] = time_w_ref[64 * peer : 64 * peer + 64, :].astype(BF)
-        out_ref[peer, 416:432, :] = jnp.concatenate([taps, gains, jnp.zeros((3, 128), F32)], axis=0).astype(BF)
+        taps = jnp.concatenate([taps, gains, jnp.zeros((3, 128), F32)], axis=0)
+        pieces = []
+        for i in range(8):
+            if i < 4:
+                pieces.append(freq_w[half][at + 16 * i : at + 16 * i + 16])
+            else:
+                pieces.append(time_w_ref[64 * peer + 16 * i - 64 : 64 * peer + 16 * i - 48, :])
+            pieces.append(taps[8 * i : 8 * i + 8] if i < 2 else jnp.zeros((8, 128), F32))
+        out_ref[peer, 288:480, :] = jnp.concatenate(pieces, axis=0).astype(BF)
 
 
 def freq_backward(pair, hidden, arrived, gathered, gain, flags, sums):
-    vmem = pl.BlockSpec(memory_space=pltpu.VMEM)
     return pl.pallas_call(
         freq_backward_kernel,
-        out_shape=jax.ShapeDtypeStruct((4, 432, 128), BF),
-        in_specs=[pl.BlockSpec(memory_space=pltpu.SMEM)] + [vmem] * 8,
-        scratch_shapes=[pltpu.VMEM((512, 128), F32), pltpu.VMEM((FR * ROWS, 128), F32)],
+        out_shape=jax.ShapeDtypeStruct((4, 480, 128), BF),
+        in_specs=[SMEM] + [VMEM] * 8,
+        scratch_shapes=[
+            pltpu.VMEM((512, 128), F32),
+            pltpu.VMEM((FR * ROWS, 128), F32),
+        ],
         name="freq_backward",
     )(flags, pair, hidden, arrived, gathered, gain, *sums)
 
@@ -256,12 +272,22 @@
     return jnp.concatenate([edge[:, :, :64], edge[:, :, 64:]], axis=1).reshape(256, 64)
 
 
-def time_kernel(flag_ref, message_ref, marks_ref, gathered_ref, gain_ref, out_ref, grad_ref, tap_ref, gain_out):
+def time_kernel(
+    flag_ref,
+    message_ref,
+    marks_ref,
+    gathered_ref,
+    gain_ref,
+    out_ref,
+    grad_ref,
+    tap_ref,
+    gain_out,
+):
     gain = gain_ref[...]
     valid, inside = marks_ref[:, 0:1], marks_ref[:, 1:2]
     spot = lax.broadcasted_iota(jnp.int32, (256, 1), 0)
     place = lax.broadcasted_iota(jnp.int32, (256, 128), 0) & 3
-    for slot in range(3):
+    def work(slot):
         share = jnp.where(flag_ref[0] > 0, 1.0, 0.0).astype(F32) if slot == 2 else 1.0
 
         def keep(ref, rows, lanes, value):
@@ -328,9 +354,19 @@
         both = jnp.concatenate([mixed, d_one], axis=1).reshape(32, 8, 128)
         out_ref[:, 4 * slot : 4 * slot + 4] = both[:, :4].astype(BF)
 
-
-def time_path(message, marks, gathered, gain, flag):
-    vmem = pl.BlockSpec(memory_space=pltpu.VMEM)
+    work(0)
+    work(1)
+
+    @pl.when(flag_ref[1] > 0)
+    def _():
+        work(2)
+
+    @pl.when(flag_ref[1] == 0)
+    def _():
+        out_ref[:, 8:12] = jnp.zeros((32, 4, 128), BF)
+
+
+def time_path(message, marks, gathered, gain, flags):
     return pl.pallas_call(
         time_kernel,
         out_shape=(
@@ -339,26 +375,28 @@
             jax.ShapeDtypeStruct((9, 256), F32),
             jax.ShapeDtypeStruct((1, 64), F32),
         ),
-        in_specs=[pl.BlockSpec(memory_space=pltpu.SMEM)] + [vmem] * 4,
+        in_specs=[SMEM] + [VMEM] * 4,
         name="time_path",
-    )(flag.reshape(1), message, marks, gathered, gain)
+    )(flags, message, marks, gathered, gain)
 
 
 def finish_kernel(
-    scale, part_ref, freq_gain, freq_in, freq_taps, freq_out, time_gain, time_in, time_taps, time_out, rows_ref
+    scale, part_ref, freq_gain, freq_in, freq_taps, freq_out, time_gain, time_in, time_taps, time_out
 ):
-    for i in range(8):
-        rows_ref[18 * i : 18 * i + 18, :] = part_ref[i] * scale
-    freq_out[...] = rows_ref[0:64, :64]
-    freq_in[...] = rows_ref[0:64, :][:, 64:].T
-    time_out[...] = rows_ref[64:128, :64]
-    time_in[...] = rows_ref[64:128, :][:, 64:].T
-    gains = rows_ref[140:141, :]
-    freq_gain[...] = gains[:, :64]
-    time_gain[...] = gains[:, 64:]
-    freq_taps[...] = rows_ref[128:131, :64]
-    for k in range(3):
-        time_taps[k] = rows_ref[131 + 3 * k : 134 + 3 * k, :64]
+    freq_w = jnp.concatenate([part_ref[i, 0:16, :] for i in range(4)], axis=0) * scale
+    time_w = jnp.concatenate([part_ref[i, 0:16, :] for i in range(4, 8)], axis=0) * scale
+    freq_out[...] = freq_w[:, :64]
+    freq_in[...] = freq_w[:, 64:].T
+    time_out[...] = time_w[:, :64]
+    time_in[...] = time_w[:, 64:].T
+    first, second = part_ref[0, 16:24, :] * scale, part_ref[1, 16:24, :] * scale
+    freq_gain[...] = second[4:5, :64]
+    time_gain[...] = second[4:5, 64:]
+    freq_taps[...] = first[0:3, :64]
+    time_taps[0] = first[3:6, :64]
+    time_taps[1, 0:2] = first[6:8, :64]
+    time_taps[1, 2:3] = second[0:1, :64]
+    time_taps[2] = second[1:4, :64]
 
 
 def finish(total, scale):
@@ -375,7 +413,7 @@
             shape(3, 3, 64),
             shape(64, 64),
         ),
-        scratch_shapes=[pltpu.VMEM((144, 128), F32)],
+        in_specs=[VMEM],
         name="finish",
     )(total)
     return (got[0][0], got[1], got[2], got[3], got[4][0], got[5], got[6], got[7])
@@ -391,7 +429,7 @@
     both = jnp.concatenate([own, halo], axis=0)
     mine = both[:, LEAD * 64 : LEAD * 64 + 4096].reshape(2 * FR, 32, 128).transpose(1, 0, 2)
     edge = jnp.stack([both[:, LEAD * 64 - 64 : LEAD * 64], both[:, LEAD * 64 + 4096 : LEAD * 64 + 4160]], axis=0)
-    return mine, jnp.concatenate([edge[:, :FR], edge[:, FR:]], axis=2)
+    return near(mine), near(jnp.concatenate([edge[:, :FR], edge[:, FR:]], axis=2))
 
 
 def frame_marks(counts, x_at):
@@ -430,6 +468,10 @@
     return lax.all_to_all(values, axes, 0, 0)
 
 
+def near(values):
+    return pltpu.with_memory_space_constraint(values, pltpu.VMEM)
+
+
 def shards(
     signal, cotangent, counts, freq_gain, freq_in, freq_taps, freq_out, time_gain, time_in, time_taps, time_out
 ):
@@ -438,23 +480,24 @@
     spot = lax.axis_index(("z", "core"))
     grad_scale = 1.0 / math.sqrt(FR * 128 * (signal.shape[1] // 64))
     packed = pack(freq_in, freq_taps, freq_out, time_in, time_taps, time_out)
-    gathered = exchange(packed, "ch")
+    gathered = near(exchange(packed, "ch"))
     lanes = jnp.stack([plane_lanes(signal, plane), plane_lanes(cotangent, plane)], axis=0)
     halo = lax.ppermute(lanes, SEQ, halo_pairs())
     gain_f, gain_t = freq_gain[None], time_gain[None]
-    x_rows, x_halo = lanes[0].reshape(FR * ROWS, 64), halo[0].reshape(FR * ROWS, 64)
+    x_rows, x_halo = near(lanes[0].reshape(FR * ROWS, 64)), near(halo[0].reshape(FR * ROWS, 64))
     message, hidden = freq_forward(x_rows, x_halo, *cot_message(lanes[1], halo[1]), gathered, gain_f)
-    bands = exchange(message, ("z", "core"))
-    marks = frame_marks(counts, x_at)
-    edge = jnp.where((plane == 3) & (spot == 1), 1, 0)
+    bands = near(exchange(message, ("z", "core")))
+    marks = near(frame_marks(counts, x_at))
+    beside = (spot == EDGE) | (spot == EDGE + 1)
+    edge = jnp.stack([jnp.where((plane == 3) & (spot == EDGE + 1), 1, 0), jnp.where(beside, 1, 0)])
     mixed, *sums = time_path(bands, marks, gathered, gain_t, edge)
-    arrived = exchange(mixed, ("z", "core"))
+    arrived = near(exchange(mixed, ("z", "core")))
     flags = jnp.stack([jnp.where(plane == 3, 1, 0), jnp.where(plane > 0, 1, 0)])
     planes = exchange(freq_backward(x_rows, hidden, arrived, gathered, gain_f, flags, sums), "ch")
-    part = jnp.sum(planes[:, 288:].astype(F32), axis=0).reshape(8, 18, 128)
-    part = jnp.sum(exchange(part, ("x", "core")), axis=0).astype(BF)
-    part = jnp.sum(exchange(jnp.broadcast_to(part, (16, 18, 128)), "z").astype(F32), axis=0)
-    total = exchange(jnp.broadcast_to(part, (8, 18, 128)), ("x", "core"))
+    part = jnp.sum(planes[:, 288:].astype(F32), axis=0).reshape(8, 24, 128).astype(BF)
+    part = jnp.sum(exchange(part, ("x", "core")).astype(F32), axis=0).astype(BF)
+    part = jnp.sum(exchange(jnp.broadcast_to(part, (16, 24, 128)), "z").astype(F32), axis=0)
+    total = near(exchange(jnp.broadcast_to(part, (8, 24, 128)), ("x", "core")))
     return outputs_of(planes) + finish(total, grad_scale)
 
 

time: 140 us -> 134 us (0.957)
  local copies, waits for them, and re-layouts: 11 us -> 5.79 us
  Pallas kernels: 15.7 us -> 12.3 us
  waiting for transfers between devices: 53.8 us -> 55.8 us
    unnamed x11 -> x3, local copies, waits for them, and re-layouts: 3.38 us -> 0.75 us
    pallas_call x1, Pallas kernels: 6.72 us -> 4.73 us  [time_path(): pl.pallas_call(time_kernel, out_shape=(jax.ShapeDtypeStruct((32, 12, 128)...]
    all_to_all x6, waiting for transfers between devices: 53.8 us -> 55.8 us  [exchange(): return lax.all_to_all(values, axes, 0, 0)]
  transfers between devices with their start and end apart: 7 -> 7, of which waited for: 6 -> 6; matrix products, arithmetic and copies ran while one was open for 5% -> 3% of each run, Pallas kernels for 1% -> 1%
where the time goes in v5:
time: 134 us
  waiting for transfers between devices  55.8 us (42%)
  starting transfers between devices  45.4 us (34%)
  Pallas kernels  12.3 us (9%)
  blocking collectives  11.1 us (8%)
  local copies, waits for them, and re-layouts  5.79 us (4%)
  other arithmetic  2.29 us (2%)
    all_to_all x6, waiting for transfers between devices, exchange(): return lax.all_to_all(values, axes, 0, 0)  55.8 us
    all_to_all x6, starting transfers between devices, exchange(): return lax.all_to_all(values, axes, 0, 0)  44.1 us
    all_to_all x1, blocking collectives, exchange(): return lax.all_to_all(values, axes, 0, 0)  11.1 us
    pallas_call x1, Pallas kernels, time_path(): pl.pallas_call(time_kernel, out_shape=(jax.ShapeDtypeStruct((32, 12, 128)...  4.73 us
    pallas_call x1, Pallas kernels, freq_backward(): pl.pallas_call(freq_backward_kernel, out_shape=jax.ShapeDtypeStruct((4, 4...  2.9 us
  transfers between devices with their start and end apart: 7, of which 6 were waited for; matrix products, arithmetic and copies ran while one was open for 3% of the time, Pallas kernels for 1%

profile of v5, /device:TPU:1, one launch (start us, length us, event | category | flops | bytes accessed | tf_op | source)
XLA Modules:
  0.0 133.5 jit_solution(4517818389966360679)
XLA Ops:
  0.6 0.9 pad_dynamic-slice_fusion
  1.5 0.1 pad_maximum_fusion.1
  1.6 1.3 collective-permute-start
  2.9 1.6 %pack.1 = bf16[4,144,128]{2,1,0:T(8,128)(2,1)} custom-call(bf16[64,64]{1,0:T(8,128)(2,1)} %freq_in.1, f32[3,64]{1,0:T(4,128)} %freq_taps.1, bf16[64,64]{1,0:T(8,128)(2,1)} %freq_out.1, bf16[64,64]{1,0:T(8,128)(2,1)} %time_in.1, f32[3,3,64]{2,1,0:T(4,128)} %time_taps.1, bf16[64,64]{1,0:T(8,128)(2,1)} %time_out.1), custom_call_target="tpu_custom_call" | custom-call | tf_op jit(solution)/shard_map/pack/pallas_call | solution.py:90
  4.5 5.0 %all-to-all-start = ((bf16[4,144,128]{2,1,0:T(8,128)(2,1)}), bf16[4,144,128]{2,1,0:T(8,128)(2,1)S(1)}, u32[]{:S(2)}, u32[]{:S(2)}) async-start(bf16[4,144,128]{2,1,0:T(8,128)(2,1)} %pack.1), calls=%async_computation | async-start | bytes 294912 | tf_op jit(solution)/shard_map/all_to_all | solution.py:468
  9.5 0.1 reshape_squeeze_stack.3.own_ref.pair_ref
  9.6 0.0 copy-start
  9.6 0.6 copy-done
  10.3 0.1 reshape.124
  10.4 0.1 copy.37
  10.5 0.1 stack.64.clone
  10.6 0.1 and.63
  10.7 0.1 and.64
  10.8 0.0 collective-permute-done
  10.9 0.1 fusion.6
  11.0 0.1 reshape_squeeze.3.halo_ref
  11.1 0.1 fusion.4.cot_edge_ref
  11.2 3.2 %all-to-all-done.gathered_ref = bf16[4,144,128]{2,1,0:T(8,128)(2,1)S(1)} async-done(((bf16[4,144,128]{2,1,0:T(8,128)(2,1)}), bf16[4,144,128]{2,1,0:T(8,128)(2,1)S(1)}, u32[]{:S(2)}, u32[]{:S(2)}) %all-to-all-start) | async-done | bytes 147488 | tf_op jit(solution)/shard_map/all_to_all | solution.py:468
  14.4 2.3 %freq_forward.1 = (bf16[32,24,128]{2,1,0:T(8,128)(2,1)}, f32[320,256]{1,0:T(8,128)}) custom-call(bf16[320,64]{1,0:T(8,128)(2,1)S(1)} %reshape_squeeze_stack.3.own_ref.pair_ref, bf16[320,64]{1,0:T(8,128)(2,1)S(1)} %reshape_squeeze.3.halo_ref, bf16[32,8,128]{2,1,0:T(8,128)(2,1)S(1)} %fusion.1.cot_ref, bf16[2,4,128]{2,1,0:T(4,128)(2,1)S(1)} %fusion.4.cot_edge_ref, ...), custom_call_target="tpu_custom_call" | custom-call | tf_op jit(solution)/shard_map/freq_forward/pallas_call | solution.py:132
  16.7 18.1 %all-to-all-start.1 = ((bf16[32,24,128]{2,1,0:T(8,128)(2,1)}), bf16[32,24,128]{2,1,0:T(8,128)(2,1)S(1)}, u32[]{:S(2)}, u32[]{:S(2)}) async-start(bf16[32,24,128]{2,1,0:T(8,128)(2,1)} %get-tuple-element.25), calls=%async_computation.1 | async-start | bytes 393216 | tf_op jit(solution)/shard_map/all_to_all | solution.py:468
  34.9 0.1 copy.34
  34.9 0.1 iota_compare_fusion
  35.1 0.1 lt.38
  35.2 0.1 copy.36.marks_ref
  35.3 0.6 pad_add_fusion.2.flag_ref
  35.9 17.7 %all-to-all-done.1.message_ref = bf16[32,24,128]{2,1,0:T(8,128)(2,1)S(1)} async-done(((bf16[32,24,128]{2,1,0:T(8,128)(2,1)}), bf16[32,24,128]{2,1,0:T(8,128)(2,1)S(1)}, u32[]{:S(2)}, u32[]{:S(2)}) %all-to-all-start.1) | async-done | bytes 196640 | tf_op jit(solution)/shard_map/all_to_all | solution.py:468
  53.6 4.7 %time_path.1 = (bf16[32,12,128]{2,1,0:T(8,128)(2,1)}, f32[256,128]{1,0:T(8,128)}, f32[9,256]{1,0:T(8,128)}, f32[1,64]{1,0:T(1,128)}) custom-call(s32[2]{0:T(128)} %pad_add_fusion.2.flag_ref, bf16[32,24,128]{2,1,0:T(8,128)(2,1)S(1)} %all-to-all-done.1.message_ref, f32[256,2]{1,0:T(8,128)S(1)} %copy.36.marks_ref, ...), custom_call_target="tpu_custom_call" | custom-call | tf_op jit(solution)/shard_map/time_path/pallas_call | solution.py:370
  58.3 5.1 %all-to-all-start.2 = ((bf16[32,12,128]{2,1,0:T(8,128)(2,1)}), bf16[32,12,128]{2,1,0:T(8,128)(2,1)S(1)}, u32[]{:S(2)}, u32[]{:S(2)}) async-start(bf16[32,12,128]{2,1,0:T(8,128)(2,1)} %get-tuple-element.26), calls=%async_computation.2 | async-start | bytes 262144 | tf_op jit(solution)/shard_map/all_to_all | solution.py:468
  63.4 0.6 pad_add_fusion.1.flag_ref
  64.0 15.2 %all-to-all-done.2.arrived_ref = bf16[32,12,128]{2,1,0:T(8,128)(2,1)S(1)} async-done(((bf16[32,12,128]{2,1,0:T(8,128)(2,1)}), bf16[32,12,128]{2,1,0:T(8,128)(2,1)S(1)}, u32[]{:S(2)}, u32[]{:S(2)}) %all-to-all-start.2) | async-done | bytes 98336 | tf_op jit(solution)/shard_map/all_to_all | solution.py:468
  79.3 2.9 %freq_backward.1 = bf16[4,480,128]{2,1,0:T(8,128)(2,1)} custom-call(s32[2]{0:T(128)} %pad_add_fusion.1.flag_ref, bf16[320,64]{1,0:T(8,128)(2,1)S(1)} %reshape_squeeze_stack.3.own_ref.pair_ref, f32[320,256]{1,0:T(8,128)} %get-tuple-element.24.hidden_ref, bf16[32,12,128]{2,1,0:T(8,128)(2,1)S(1)} %all-to-all-done.2.arrived_ref, ...), custom_call_target="tpu_custom_call" | custom-call | tf_op jit(solution)/shard_map/freq_backward/pallas_call | solution.py:225
  82.2 11.1 %all_to_all.35 = bf16[4,480,128]{2,1,0:T(8,128)(2,1)S(1)} all-to-all(bf16[4,480,128]{2,1,0:T(8,128)(2,1)} %freq_backward.1), channel_id=1, replica_groups=mesh['x'=4,'z'=16,'core'=2,'ch'=4] {'ch'}, dimensions={0} | all-to-all | bytes 983040 | tf_op jit(solution)/shard_map/all_to_all | solution.py:468
  93.2 0.6 slice_reduce_fusion
  93.9 6.4 %all-to-all-start.4 = ((bf16[8,24,128]{2,1,0:T(8,128)(2,1)}), bf16[8,24,128]{2,1,0:T(8,128)(2,1)S(1)}, u32[]{:S(2)}, u32[]{:S(2)}) async-start(bf16[8,24,128]{2,1,0:T(8,128)(2,1)} %bitcast.21), calls=%async_computation.4 | async-start | bytes 98304 | tf_op jit(solution)/shard_map/all_to_all | solution.py:468
  100.3 4.8 %all-to-all-done.4 = bf16[8,24,128]{2,1,0:T(8,128)(2,1)S(1)} async-done(((bf16[8,24,128]{2,1,0:T(8,128)(2,1)}), bf16[8,24,128]{2,1,0:T(8,128)(2,1)S(1)}, u32[]{:S(2)}, u32[]{:S(2)}) %all-to-all-start.4) | async-done | bytes 49184 | tf_op jit(solution)/shard_map/all_to_all | solution.py:468
  105.1 0.7 broadcast_in_dim.19
  105.8 3.5 %all-to-all-start.5 = ((bf16[16,24,128]{2,1,0:T(8,128)(2,1)}), bf16[16,24,128]{2,1,0:T(8,128)(2,1)S(1)}, u32[]{:S(2)}, u32[]{:S(2)}) async-start(bf16[16,24,128]{2,1,0:T(8,128)(2,1)} %broadcast_in_dim.19), calls=%async_computation.5 | async-start | bytes 196608 | tf_op jit(solution)/shard_map/all_to_all | solution.py:468
  109.4 11.7 %all-to-all-done.5 = bf16[16,24,128]{2,1,0:T(8,128)(2,1)S(1)} async-done(((bf16[16,24,128]{2,1,0:T(8,128)(2,1)}), bf16[16,24,128]{2,1,0:T(8,128)(2,1)S(1)}, u32[]{:S(2)}, u32[]{:S(2)}) %all-to-all-start.5) | async-done | bytes 98336 | tf_op jit(solution)/shard_map/all_to_all | solution.py:468
  121.1 0.6 broadcast_in_dim.20
  121.7 6.0 %all-to-all-start.6 = ((f32[8,24,128]{2,1,0:T(8,128)}), f32[8,24,128]{2,1,0:T(8,128)S(1)}, u32[]{:S(2)}, u32[]{:S(2)}) async-start(f32[8,24,128]{2,1,0:T(8,128)} %broadcast_in_dim.20), calls=%async_computation.6 | async-start | bytes 196608 | tf_op jit(solution)/shard_map/all_to_all | solution.py:468
  127.7 0.1 fusion.7
  127.9 0.9 reshape.127
  128.7 0.9 reshape.126
  129.6 3.1 %all-to-all-done.6.part_ref = f32[8,24,128]{2,1,0:T(8,128)S(1)} async-done(((f32[8,24,128]{2,1,0:T(8,128)}), f32[8,24,128]{2,1,0:T(8,128)S(1)}, u32[]{:S(2)}, u32[]{:S(2)}) %all-to-all-start.6) | async-done | bytes 98336 | tf_op jit(solution)/shard_map/all_to_all | solution.py:468
  132.7 0.8 finish.1
  (16 shorter events, 0.2 us)
Async XLA Ops:
  1.6 9.2 %collective-permute-start = (bf16[2,4,5120]{2,1,0:T(4,128)(2,1)S(1)}, bf16[2,4,5120]{2,1,0:T(4,128)(2,1)S(1)}, u32[]{:S(2)}, u32[]{:S(2)}) collective-permute-start(bf16[2,4,5120]{2,1,0:T(4,128)(2,1)S(1)} %pad_maximum_fusion.1), channel_id=1, source_target_pairs={{128,0},{132,4},{136,8},{140,12},{144,16},{148,20},{152,24},{156,2... | collective-permute-start | bytes 245768 | tf_op jit(solution)/shard_map/ppermute | solution.py:485
  4.5 9.9 %all-to-all-start = ((bf16[4,144,128]{2,1,0:T(8,128)(2,1)}), bf16[4,144,128]{2,1,0:T(8,128)(2,1)S(1)}, u32[]{:S(2)}, u32[]{:S(2)}) async-start(bf16[4,144,128]{2,1,0:T(8,128)(2,1)} %pack.1), calls=%async_computation | async-start | bytes 294912 | tf_op jit(solution)/shard_map/all_to_all | solution.py:468
  9.6 0.7 copy-start
  16.7 36.9 %all-to-all-start.1 = ((bf16[32,24,128]{2,1,0:T(8,128)(2,1)}), bf16[32,24,128]{2,1,0:T(8,128)(2,1)S(1)}, u32[]{:S(2)}, u32[]{:S(2)}) async-start(bf16[32,24,128]{2,1,0:T(8,128)(2,1)} %get-tuple-element.25), calls=%async_computation.1 | async-start | bytes 393216 | tf_op jit(solution)/shard_map/all_to_all | solution.py:468
  58.3 20.9 %all-to-all-start.2 = ((bf16[32,12,128]{2,1,0:T(8,128)(2,1)}), bf16[32,12,128]{2,1,0:T(8,128)(2,1)S(1)}, u32[]{:S(2)}, u32[]{:S(2)}) async-start(bf16[32,12,128]{2,1,0:T(8,128)(2,1)} %get-tuple-element.26), calls=%async_computation.2 | async-start | bytes 262144 | tf_op jit(solution)/shard_map/all_to_all | solution.py:468
  93.9 11.2 %all-to-all-start.4 = ((bf16[8,24,128]{2,1,0:T(8,128)(2,1)}), bf16[8,24,128]{2,1,0:T(8,128)(2,1)S(1)}, u32[]{:S(2)}, u32[]{:S(2)}) async-start(bf16[8,24,128]{2,1,0:T(8,128)(2,1)} %bitcast.21), calls=%async_computation.4 | async-start | bytes 98304 | tf_op jit(solution)/shard_map/all_to_all | solution.py:468
  105.8 15.3 %all-to-all-start.5 = ((bf16[16,24,128]{2,1,0:T(8,128)(2,1)}), bf16[16,24,128]{2,1,0:T(8,128)(2,1)S(1)}, u32[]{:S(2)}, u32[]{:S(2)}) async-start(bf16[16,24,128]{2,1,0:T(8,128)(2,1)} %broadcast_in_dim.19), calls=%async_computation.5 | async-start | bytes 196608 | tf_op jit(solution)/shard_map/all_to_all | solution.py:468
  121.7 11.0 %all-to-all-start.6 = ((f32[8,24,128]{2,1,0:T(8,128)}), f32[8,24,128]{2,1,0:T(8,128)S(1)}, u32[]{:S(2)}, u32[]{:S(2)}) async-start(f32[8,24,128]{2,1,0:T(8,128)} %broadcast_in_dim.20), calls=%async_computation.6 | async-start | bytes 196608 | tf_op jit(solution)/shard_map/all_to_all | solution.py:468

commit v6 on v5

--- a/solution.py
+++ b/solution.py
@@ -7,6 +7,7 @@
 from jax.experimental import pallas as pl
 from jax.experimental.pallas import tpu as pltpu
 from jax.sharding import Mesh, PartitionSpec as P
+
 
 EPS = 1e-05
 FR = 4
@@ -150,6 +151,7 @@
     time_w_ref,
     time_t_ref,
     time_g_ref,
+    done_ref,
     out_ref,
     tiles_ref,
     back_ref,
@@ -202,6 +204,7 @@
     d_signal = grad_wide + norm_back(d_normed, features, scale, gain)
     done = jnp.concatenate([output, d_signal], axis=1)
     done = jnp.concatenate([done[f * ROWS + LEAD : (f + 1) * ROWS] for f in range(FR)], axis=0).astype(BF)
+    done_ref[...] = done
     gains = jnp.concatenate([freq_g, time_g_ref[...]], axis=1)
     for peer in range(4):
         half, at = peer // 2, 64 * (peer % 2)
@@ -209,22 +212,20 @@
         rows.append(time_t_ref[:, 64 * peer : 64 * peer + 64])
         taps = jnp.concatenate(rows, axis=0)
         taps = jnp.concatenate([taps, jnp.zeros((12, 64), F32)], axis=1)
-        out_ref[peer, 0:288, :] = done
         taps = jnp.concatenate([taps, gains, jnp.zeros((3, 128), F32)], axis=0)
-        pieces = []
         for i in range(8):
             if i < 4:
-                pieces.append(freq_w[half][at + 16 * i : at + 16 * i + 16])
+                piece = freq_w[half][at + 16 * i : at + 16 * i + 16]
             else:
-                pieces.append(time_w_ref[64 * peer + 16 * i - 64 : 64 * peer + 16 * i - 48, :])
-            pieces.append(taps[8 * i : 8 * i + 8] if i < 2 else jnp.zeros((8, 128), F32))
-        out_ref[peer, 288:480, :] = jnp.concatenate(pieces, axis=0).astype(BF)
+                piece = time_w_ref[64 * peer + 16 * i - 64 : 64 * peer + 16 * i - 48, :]
+            small = taps[8 * i : 8 * i + 8] if i < 2 else jnp.zeros((8, 128), F32)
+            out_ref[4 * i + peer] = jnp.concatenate([piece, small], axis=0).astype(BF)
 
 
 def freq_backward(pair, hidden, arrived, gathered, gain, flags, sums):
     return pl.pallas_call(
         freq_backward_kernel,
-        out_shape=jax.ShapeDtypeStruct((4, 480, 128), BF),
+        out_shape=(jax.ShapeDtypeStruct((288, 128), BF), jax.ShapeDtypeStruct((32, 24, 128), BF)),
         in_specs=[SMEM] + [VMEM] * 8,
         scratch_shapes=[
             pltpu.VMEM((512, 128), F32),
@@ -287,6 +288,7 @@
     valid, inside = marks_ref[:, 0:1], marks_ref[:, 1:2]
     spot = lax.broadcasted_iota(jnp.int32, (256, 1), 0)
     place = lax.broadcasted_iota(jnp.int32, (256, 128), 0) & 3
+
     def work(slot):
         share = jnp.where(flag_ref[0] > 0, 1.0, 0.0).astype(F32) if slot == 2 else 1.0
 
@@ -444,8 +446,9 @@
     return jnp.stack([valid.reshape(256), inside.reshape(256)], axis=1).astype(F32)
 
 
-def outputs_of(arrived):
-    rows = arrived[:, :288].reshape(4, FR, 72, 128)
+def outputs_of(blocks, plane):
+    twice = jnp.stack(blocks[::-1] + blocks[::-1], axis=0)
+    rows = lax.dynamic_slice(twice, (3 - plane, 0, 0), (4, 288, 128)).reshape(4, FR, 72, 128)
     whole = jnp.concatenate([rows[0, :, :64], rows[1, :, :64], rows[2, :, :64], rows[3, :, :65]], axis=1)
     return whole[:, :, :64].reshape(FR, -1), whole[:, :, 64:].reshape(FR, -1)
 
@@ -493,12 +496,16 @@
     mixed, *sums = time_path(bands, marks, gathered, gain_t, edge)
     arrived = near(exchange(mixed, ("z", "core")))
     flags = jnp.stack([jnp.where(plane == 3, 1, 0), jnp.where(plane > 0, 1, 0)])
-    planes = exchange(freq_backward(x_rows, hidden, arrived, gathered, gain_f, flags, sums), "ch")
-    part = jnp.sum(planes[:, 288:].astype(F32), axis=0).reshape(8, 24, 128).astype(BF)
-    part = jnp.sum(exchange(part, ("x", "core")).astype(F32), axis=0).astype(BF)
-    part = jnp.sum(exchange(jnp.broadcast_to(part, (16, 24, 128)), "z").astype(F32), axis=0)
+    done, pieces = freq_backward(x_rows, hidden, arrived, gathered, gain_f, flags, sums)
+    part = exchange(pieces, ("x", "core", "ch"))
+    part = jnp.broadcast_to(jnp.sum(part.astype(F32), axis=0).astype(BF), (16, 24, 128))
+    blocks = [done]
+    for shift in (1, 2, 3):
+        blocks.append(lax.ppermute(done, "ch", [(i, (i + shift) % 4) for i in range(4)]))
+    part = exchange(part, "z")
+    part = jnp.sum(part.astype(F32), axis=0)
     total = near(exchange(jnp.broadcast_to(part, (8, 24, 128)), ("x", "core")))
-    return outputs_of(planes) + finish(total, grad_scale)
+    return outputs_of(blocks, plane) + finish(total, grad_scale)
 
 
 def solution(mesh):

time: 134 us -> 136 us (1.015)
  blocking collectives: 11.1 us -> 0 us
  starting transfers between devices: 45.4 us -> 55.5 us
  waiting for transfers between devices: 55.8 us -> 58 us
    all_to_all x1 -> x0, blocking collectives: 11.1 us -> none  [exchange(): return lax.all_to_all(values, axes, 0, 0)]
    ppermute x0 -> x3, starting transfers between devices: none -> 7.8 us  [shards(): lax.ppermute(done, 'ch', [(i, (i + shift) % 4) for i in range(4)])]
    all_to_all x6, waiting for transfers between devices: 55.8 us -> 58 us  [exchange(): return lax.all_to_all(values, axes, 0, 0)]
    all_to_all x6, starting transfers between devices: 44.1 us -> 46.4 us  [exchange(): return lax.all_to_all(values, axes, 0, 0)]
  transfers between devices with their start and end apart: 7 -> 10, of which waited for: 6 -> 6; matrix products, arithmetic and copies ran while one was open for 3% -> 3% of each run, Pallas kernels for 1% -> 1%
where the time goes in v6:
time: 136 us; the launch traced here: 135 us
  waiting for transfers between devices  58 us (43%)
  starting transfers between devices  55.5 us (41%)
  Pallas kernels  12.2 us (9%)
  local copies, waits for them, and re-layouts  6.78 us (5%)
  other arithmetic  1.67 us (1%)
    all_to_all x6, waiting for transfers between devices, exchange(): return lax.all_to_all(values, axes, 0, 0)  58 us
    all_to_all x6, starting transfers between devices, exchange(): return lax.all_to_all(values, axes, 0, 0)  46.4 us
    ppermute x3, starting transfers between devices, shards(): lax.ppermute(done, 'ch', [(i, (i + shift) % 4) for i in range(4)])  7.8 us
    pallas_call x1, Pallas kernels, time_path(): pl.pallas_call(time_kernel, out_shape=(jax.ShapeDtypeStruct((32, 12, 128)...  4.73 us
    pallas_call x1, Pallas kernels, freq_backward(): pl.pallas_call(freq_backward_kernel, out_shape=(jax.ShapeDtypeStruct((288...  2.81 us
  transfers between devices with their start and end apart: 10, of which 6 were waited for; matrix products, arithmetic and copies ran while one was open for 3% of the time, Pallas kernels for 1%

profile of v6, /device:TPU:1, one launch (start us, length us, event | category | flops | bytes accessed | tf_op | source)
XLA Modules:
  0.0 135.1 jit_solution(10500779634950241625)
XLA Ops:
  0.6 0.9 pad_dynamic-slice_fusion
  1.5 0.1 pad_maximum_fusion.1
  1.6 1.3 collective-permute-start
  2.9 1.6 %pack.1 = bf16[4,144,128]{2,1,0:T(8,128)(2,1)} custom-call(bf16[64,64]{1,0:T(8,128)(2,1)} %freq_in.1, f32[3,64]{1,0:T(4,128)} %freq_taps.1, bf16[64,64]{1,0:T(8,128)(2,1)} %freq_out.1, bf16[64,64]{1,0:T(8,128)(2,1)} %time_in.1, f32[3,3,64]{2,1,0:T(4,128)} %time_taps.1, bf16[64,64]{1,0:T(8,128)(2,1)} %time_out.1), custom_call_target="tpu_custom_call" | custom-call | tf_op jit(solution)/shard_map/pack/pallas_call | solution.py:91
  4.5 5.0 %all-to-all-start = ((bf16[4,144,128]{2,1,0:T(8,128)(2,1)}), bf16[4,144,128]{2,1,0:T(8,128)(2,1)S(1)}, u32[]{:S(2)}, u32[]{:S(2)}) async-start(bf16[4,144,128]{2,1,0:T(8,128)(2,1)} %pack.1), calls=%async_computation | async-start | bytes 294912 | tf_op jit(solution)/shard_map/all_to_all | solution.py:471
  9.5 0.1 reshape_squeeze_stack.3.own_ref.pair_ref
  9.6 0.0 copy-start.1
  9.6 0.6 copy-done.1
  10.3 0.1 reshape.122
  10.4 0.1 copy.37
  10.5 0.1 stack.83.clone
  10.6 0.1 and.63
  10.7 0.1 and.64
  10.9 0.1 fusion.6
  11.0 0.1 reshape_squeeze.3.halo_ref
  11.1 0.1 fusion.4.cot_edge_ref
  11.2 3.2 %all-to-all-done.gathered_ref = bf16[4,144,128]{2,1,0:T(8,128)(2,1)S(1)} async-done(((bf16[4,144,128]{2,1,0:T(8,128)(2,1)}), bf16[4,144,128]{2,1,0:T(8,128)(2,1)S(1)}, u32[]{:S(2)}, u32[]{:S(2)}) %all-to-all-start) | async-done | bytes 147488 | tf_op jit(solution)/shard_map/all_to_all | solution.py:471
  14.4 2.3 %freq_forward.1 = (bf16[32,24,128]{2,1,0:T(8,128)(2,1)}, f32[320,256]{1,0:T(8,128)}) custom-call(bf16[320,64]{1,0:T(8,128)(2,1)S(1)} %reshape_squeeze_stack.3.own_ref.pair_ref, bf16[320,64]{1,0:T(8,128)(2,1)S(1)} %reshape_squeeze.3.halo_ref, bf16[32,8,128]{2,1,0:T(8,128)(2,1)S(1)} %fusion.1.cot_ref, bf16[2,4,128]{2,1,0:T(4,128)(2,1)S(1)} %fusion.4.cot_edge_ref, ...), custom_call_target="tpu_custom_call" | custom-call | tf_op jit(solution)/shard_map/freq_forward/pallas_call | solution.py:133
  16.7 18.1 %all-to-all-start.1 = ((bf16[32,24,128]{2,1,0:T(8,128)(2,1)}), bf16[32,24,128]{2,1,0:T(8,128)(2,1)S(1)}, u32[]{:S(2)}, u32[]{:S(2)}) async-start(bf16[32,24,128]{2,1,0:T(8,128)(2,1)} %get-tuple-element.27), calls=%async_computation.1 | async-start | bytes 393216 | tf_op jit(solution)/shard_map/all_to_all | solution.py:471
  34.8 0.1 copy.34
  34.9 0.1 iota_compare_fusion
  35.0 0.1 lt.41
  35.2 0.1 copy.36.marks_ref
  35.3 0.6 pad_add_fusion.2.flag_ref
  35.9 17.7 %all-to-all-done.1.message_ref = bf16[32,24,128]{2,1,0:T(8,128)(2,1)S(1)} async-done(((bf16[32,24,128]{2,1,0:T(8,128)(2,1)}), bf16[32,24,128]{2,1,0:T(8,128)(2,1)S(1)}, u32[]{:S(2)}, u32[]{:S(2)}) %all-to-all-start.1) | async-done | bytes 196640 | tf_op jit(solution)/shard_map/all_to_all | solution.py:471
  53.6 4.7 %time_path.1 = (bf16[32,12,128]{2,1,0:T(8,128)(2,1)}, f32[256,128]{1,0:T(8,128)}, f32[9,256]{1,0:T(8,128)}, f32[1,64]{1,0:T(1,128)}) custom-call(s32[2]{0:T(128)} %pad_add_fusion.2.flag_ref, bf16[32,24,128]{2,1,0:T(8,128)(2,1)S(1)} %all-to-all-done.1.message_ref, f32[256,2]{1,0:T(8,128)S(1)} %copy.36.marks_ref, ...), custom_call_target="tpu_custom_call" | custom-call | tf_op jit(solution)/shard_map/time_path/pallas_call | solution.py:372
  58.3 5.0 %all-to-all-start.2 = ((bf16[32,12,128]{2,1,0:T(8,128)(2,1)}), bf16[32,12,128]{2,1,0:T(8,128)(2,1)S(1)}, u32[]{:S(2)}, u32[]{:S(2)}) async-start(bf16[32,12,128]{2,1,0:T(8,128)(2,1)} %get-tuple-element.28), calls=%async_computation.2 | async-start | bytes 262144 | tf_op jit(solution)/shard_map/all_to_all | solution.py:471
  63.4 0.6 pad_add_fusion.1.flag_ref
  64.0 15.2 %all-to-all-done.2.arrived_ref = bf16[32,12,128]{2,1,0:T(8,128)(2,1)S(1)} async-done(((bf16[32,12,128]{2,1,0:T(8,128)(2,1)}), bf16[32,12,128]{2,1,0:T(8,128)(2,1)S(1)}, u32[]{:S(2)}, u32[]{:S(2)}) %all-to-all-start.2) | async-done | bytes 98336 | tf_op jit(solution)/shard_map/all_to_all | solution.py:471
  79.2 2.8 %freq_backward.1 = (bf16[288,128]{1,0:T(8,128)(2,1)}, bf16[32,24,128]{2,1,0:T(8,128)(2,1)}) custom-call(s32[2]{0:T(128)} %pad_add_fusion.1.flag_ref, bf16[320,64]{1,0:T(8,128)(2,1)S(1)} %reshape_squeeze_stack.3.own_ref.pair_ref, f32[320,256]{1,0:T(8,128)} %get-tuple-element.26.hidden_ref, bf16[32,12,128]{2,1,0:T(8,128)(2,1)S(1)} %all-to-all-done.2.arrived_ref, ...), custom_call_target="tpu_custom_call" | custom-call | tf_op jit(solution)/shard_map/freq_backward/pallas_call | solution.py:226
  82.1 2.8 %collective-permute-start.1 = (bf16[288,128]{1,0:T(8,128)(2,1)}, bf16[288,128]{1,0:T(8,128)(2,1)S(1)}, u32[]{:S(2)}, u32[]{:S(2)}) collective-permute-start(bf16[288,128]{1,0:T(8,128)(2,1)} %get-tuple-element.32), channel_id=1, source_target_pairs={{0,3},{1,0},{2,1},{3,2},{4,7},{5,4},{6,5},{7,6},{8,11},{9,8},{10,9... | collective-permute-start | bytes 221192 | tf_op jit(solution)/shard_map/ppermute | solution.py:504
  84.8 2.5 %collective-permute-start.3 = (bf16[288,128]{1,0:T(8,128)(2,1)}, bf16[288,128]{1,0:T(8,128)(2,1)S(1)}, u32[]{:S(2)}, u32[]{:S(2)}) collective-permute-start(bf16[288,128]{1,0:T(8,128)(2,1)} %get-tuple-element.32), channel_id=1, source_target_pairs={{0,1},{1,2},{2,3},{3,0},{4,5},{5,6},{6,7},{7,4},{8,9},{9,10},{10,1... | collective-permute-start | bytes 221192 | tf_op jit(solution)/shard_map/ppermute | solution.py:504
  87.3 2.5 %collective-permute-start.2 = (bf16[288,128]{1,0:T(8,128)(2,1)}, bf16[288,128]{1,0:T(8,128)(2,1)S(1)}, u32[]{:S(2)}, u32[]{:S(2)}) collective-permute-start(bf16[288,128]{1,0:T(8,128)(2,1)} %get-tuple-element.32), channel_id=1, source_target_pairs={{0,2},{1,3},{2,0},{3,1},{4,6},{5,7},{6,4},{7,5},{8,10},{9,11},{10,... | collective-permute-start | bytes 221192 | tf_op jit(solution)/shard_map/ppermute | solution.py:504
  89.9 8.7 %all-to-all-start.3 = ((bf16[32,24,128]{2,1,0:T(8,128)(2,1)}), bf16[32,24,128]{2,1,0:T(8,128)(2,1)S(1)}, u32[]{:S(2)}, u32[]{:S(2)}) async-start(bf16[32,24,128]{2,1,0:T(8,128)(2,1)} %get-tuple-element.33), calls=%async_computation.3 | async-start | bytes 393216 | tf_op jit(solution)/shard_map/all_to_all | solution.py:471
  98.5 0.0 collective-permute-done.1
  98.6 0.0 copy-start
  98.6 0.8 copy-done
  99.6 7.1 %all-to-all-done.3 = bf16[32,24,128]{2,1,0:T(8,128)(2,1)S(1)} async-done(((bf16[32,24,128]{2,1,0:T(8,128)(2,1)}), bf16[32,24,128]{2,1,0:T(8,128)(2,1)S(1)}, u32[]{:S(2)}, u32[]{:S(2)}) %all-to-all-start.3) | async-done | bytes 196640 | tf_op jit(solution)/shard_map/all_to_all | solution.py:471
  106.8 0.7 broadcast_in_dim.19
  107.4 3.5 %all-to-all-start.4 = ((bf16[16,24,128]{2,1,0:T(8,128)(2,1)}), bf16[16,24,128]{2,1,0:T(8,128)(2,1)S(1)}, u32[]{:S(2)}, u32[]{:S(2)}) async-start(bf16[16,24,128]{2,1,0:T(8,128)(2,1)} %broadcast_in_dim.19), calls=%async_computation.4 | async-start | bytes 196608 | tf_op jit(solution)/shard_map/all_to_all | solution.py:471
  111.0 11.7 %all-to-all-done.4 = bf16[16,24,128]{2,1,0:T(8,128)(2,1)S(1)} async-done(((bf16[16,24,128]{2,1,0:T(8,128)(2,1)}), bf16[16,24,128]{2,1,0:T(8,128)(2,1)S(1)}, u32[]{:S(2)}, u32[]{:S(2)}) %all-to-all-start.4) | async-done | bytes 98336 | tf_op jit(solution)/shard_map/all_to_all | solution.py:471
  122.7 0.6 broadcast_in_dim.20
  123.3 6.0 %all-to-all-start.5 = ((f32[8,24,128]{2,1,0:T(8,128)}), f32[8,24,128]{2,1,0:T(8,128)S(1)}, u32[]{:S(2)}, u32[]{:S(2)}) async-start(f32[8,24,128]{2,1,0:T(8,128)} %broadcast_in_dim.20), calls=%async_computation.5 | async-start | bytes 196608 | tf_op jit(solution)/shard_map/all_to_all | solution.py:471
  129.4 0.1 fusion.7
  129.5 0.9 reshape.125
  130.4 0.9 reshape.124
  131.2 3.1 %all-to-all-done.5.part_ref = f32[8,24,128]{2,1,0:T(8,128)S(1)} async-done(((f32[8,24,128]{2,1,0:T(8,128)}), f32[8,24,128]{2,1,0:T(8,128)S(1)}, u32[]{:S(2)}, u32[]{:S(2)}) %all-to-all-start.5) | async-done | bytes 98336 | tf_op jit(solution)/shard_map/all_to_all | solution.py:471
  134.4 0.8 finish.1
  (27 shorter events, 0.4 us)
Async XLA Ops:
  1.6 9.2 %collective-permute-start = (bf16[2,4,5120]{2,1,0:T(4,128)(2,1)S(1)}, bf16[2,4,5120]{2,1,0:T(4,128)(2,1)S(1)}, u32[]{:S(2)}, u32[]{:S(2)}) collective-permute-start(bf16[2,4,5120]{2,1,0:T(4,128)(2,1)S(1)} %pad_maximum_fusion.1), channel_id=1, source_target_pairs={{128,0},{132,4},{136,8},{140,12},{144,16},{148,20},{152,24},{156,2... | collective-permute-start | bytes 245768 | tf_op jit(solution)/shard_map/ppermute | solution.py:488
  4.5 9.9 %all-to-all-start = ((bf16[4,144,128]{2,1,0:T(8,128)(2,1)}), bf16[4,144,128]{2,1,0:T(8,128)(2,1)S(1)}, u32[]{:S(2)}, u32[]{:S(2)}) async-start(bf16[4,144,128]{2,1,0:T(8,128)(2,1)} %pack.1), calls=%async_computation | async-start | bytes 294912 | tf_op jit(solution)/shard_map/all_to_all | solution.py:471
  9.6 0.7 copy-start.1
  16.7 36.9 %all-to-all-start.1 = ((bf16[32,24,128]{2,1,0:T(8,128)(2,1)}), bf16[32,24,128]{2,1,0:T(8,128)(2,1)S(1)}, u32[]{:S(2)}, u32[]{:S(2)}) async-start(bf16[32,24,128]{2,1,0:T(8,128)(2,1)} %get-tuple-element.27), calls=%async_computation.1 | async-start | bytes 393216 | tf_op jit(solution)/shard_map/all_to_all | solution.py:471
  58.3 20.9 %all-to-all-start.2 = ((bf16[32,12,128]{2,1,0:T(8,128)(2,1)}), bf16[32,12,128]{2,1,0:T(8,128)(2,1)S(1)}, u32[]{:S(2)}, u32[]{:S(2)}) async-start(bf16[32,12,128]{2,1,0:T(8,128)(2,1)} %get-tuple-element.28), calls=%async_computation.2 | async-start | bytes 262144 | tf_op jit(solution)/shard_map/all_to_all | solution.py:471
  82.1 16.5 %collective-permute-start.1 = (bf16[288,128]{1,0:T(8,128)(2,1)}, bf16[288,128]{1,0:T(8,128)(2,1)S(1)}, u32[]{:S(2)}, u32[]{:S(2)}) collective-permute-start(bf16[288,128]{1,0:T(8,128)(2,1)} %get-tuple-element.32), channel_id=1, source_target_pairs={{0,3},{1,0},{2,1},{3,2},{4,7},{5,4},{6,5},{7,6},{8,11},{9,8},{10,9... | collective-permute-start | bytes 221192 | tf_op jit(solution)/shard_map/ppermute | solution.py:504
  84.8 13.8 %collective-permute-start.3 = (bf16[288,128]{1,0:T(8,128)(2,1)}, bf16[288,128]{1,0:T(8,128)(2,1)S(1)}, u32[]{:S(2)}, u32[]{:S(2)}) collective-permute-start(bf16[288,128]{1,0:T(8,128)(2,1)} %get-tuple-element.32), channel_id=1, source_target_pairs={{0,1},{1,2},{2,3},{3,0},{4,5},{5,6},{6,7},{7,4},{8,9},{9,10},{10,1... | collective-permute-start | bytes 221192 | tf_op jit(solution)/shard_map/ppermute | solution.py:504
  87.3 11.2 %collective-permute-start.2 = (bf16[288,128]{1,0:T(8,128)(2,1)}, bf16[288,128]{1,0:T(8,128)(2,1)S(1)}, u32[]{:S(2)}, u32[]{:S(2)}) collective-permute-start(bf16[288,128]{1,0:T(8,128)(2,1)} %get-tuple-element.32), channel_id=1, source_target_pairs={{0,2},{1,3},{2,0},{3,1},{4,6},{5,7},{6,4},{7,5},{8,10},{9,11},{10,... | collective-permute-start | bytes 221192 | tf_op jit(solution)/shard_map/ppermute | solution.py:504
  89.9 16.8 %all-to-all-start.3 = ((bf16[32,24,128]{2,1,0:T(8,128)(2,1)}), bf16[32,24,128]{2,1,0:T(8,128)(2,1)S(1)}, u32[]{:S(2)}, u32[]{:S(2)}) async-start(bf16[32,24,128]{2,1,0:T(8,128)(2,1)} %get-tuple-element.33), calls=%async_computation.3 | async-start | bytes 393216 | tf_op jit(solution)/shard_map/all_to_all | solution.py:471
  98.6 0.9 copy-start
  107.4 15.3 %all-to-all-start.4 = ((bf16[16,24,128]{2,1,0:T(8,128)(2,1)}), bf16[16,24,128]{2,1,0:T(8,128)(2,1)S(1)}, u32[]{:S(2)}, u32[]{:S(2)}) async-start(bf16[16,24,128]{2,1,0:T(8,128)(2,1)} %broadcast_in_dim.19), calls=%async_computation.4 | async-start | bytes 196608 | tf_op jit(solution)/shard_map/all_to_all | solution.py:471
  123.3 11.0 %all-to-all-start.5 = ((f32[8,24,128]{2,1,0:T(8,128)}), f32[8,24,128]{2,1,0:T(8,128)S(1)}, u32[]{:S(2)}, u32[]{:S(2)}) async-start(f32[8,24,128]{2,1,0:T(8,128)} %broadcast_in_dim.20), calls=%async_computation.5 | async-start | bytes 196608 | tf_op jit(solution)/shard_map/all_to_all | solution.py:471

commit v7 on v6

--- a/solution.py
+++ b/solution.py
@@ -132,7 +132,7 @@
     rows = pair.shape[0]
     return pl.pallas_call(
         freq_forward_kernel,
-        out_shape=(jax.ShapeDtypeStruct((32, 24, 128), BF), jax.ShapeDtypeStruct((rows, 256), F32)),
+        out_shape=(jax.ShapeDtypeStruct((32, 24, 128), BF), pltpu.VMEM((rows, 256), F32)),
         scratch_shapes=[
             pltpu.VMEM((rows, 64), F32),
             pltpu.VMEM((256, 128), F32),
@@ -232,7 +232,7 @@
             pltpu.VMEM((FR * ROWS, 128), F32),
         ],
         name="freq_backward",
-    )(flags, pair, hidden, arrived, gathered, gain, *sums)
+    )(flags, pair, near(hidden), arrived, gathered, gain, *[near(part) for part in sums])
 
 
 def turned(tiles):
@@ -248,15 +248,20 @@
     return jnp.concatenate([turned(values[base:]), values[:base]], axis=0)
 
 
+def in_tiles(values, amount):
+    tiles = values.reshape(values.shape[0] // 8, 8, values.shape[1])
+    return pltpu.roll(tiles, amount % 8, 1).reshape(values.shape)
+
+
 def later(values, spacing, place):
     if spacing == 1:
-        return jnp.where(place == 3, roll_rows(groups_on(values, 1), 3), roll_rows(values, -1))
+        return jnp.where(place == 3, in_tiles(groups_on(values, 1), 3), in_tiles(values, -1))
     return groups_on(values, spacing // FR)
 
 
 def earlier(values, spacing, place):
     if spacing == 1:
-        return jnp.where(place == 0, roll_rows(groups_on(values, -1), -3), roll_rows(values, 1))
+        return jnp.where(place == 0, in_tiles(groups_on(values, -1), -3), in_tiles(values, 1))
     return groups_on(values, -(spacing // FR))
 
 
@@ -307,24 +312,21 @@
         normed_own = (normed * counted).astype(BF)
         normed = normed.astype(BF)
         mixed, d_normed = features, None
-        for half, lanes in enumerate(HALVES):
-            weights = half_weights(gathered_ref, half, 64)
+        for side, lanes in enumerate(HALVES):
+            weights = half_weights(gathered_ref, side, 64)
             weight_in, weight_out = weights[:, :64], weights[:, 64:]
-            taps = half_taps(gathered_ref, half, 3, 9)
+            half = 0.5 * half_taps(gathered_ref, side, 3, 9)
             state = nt(normed, weight_in) * valid
             states, slopes = [], []
             for layer in range(3):
                 spacing = (1, 4, 16)[layer]
-                row = taps[3 * layer : 3 * layer + 3]
-                drive = (
-                    row[0:1] * earlier(state, spacing, place)
-                    + row[1:2] * state
-                    + row[2:3] * later(state, spacing, place)
-                )
-                gate = sigmoid(drive)
-                active = drive * gate
-                states.append(state)
-                slopes.append(gate + active * (1.0 - gate))
+                row = half[3 * layer : 3 * layer + 3]
+                around = (earlier(state, spacing, place), state, later(state, spacing, place))
+                drive = row[0:1] * around[0] + row[1:2] * state + row[2:3] * around[2]
+                opened = jnp.tanh(drive) + 1.0
+                active = drive * opened
+                states.append(around)
+                slopes.append(opened + active * (2.0 - opened))
                 state = state + active
                 if layer < 2:
                     state = state * inside
@@ -334,14 +336,13 @@
             d_state = nt(grad, weight_out)
             for layer in reversed(range(3)):
                 spacing = (1, 4, 16)[layer]
-                row = taps[3 * layer : 3 * layer + 3]
+                row = half[3 * layer : 3 * layer + 3]
                 d_drive = d_state * slopes[layer]
                 if layer < 2:
                     d_drive = d_drive * inside
-                held = states[layer]
-                for j, moved in enumerate((earlier(held, spacing, place), held, later(held, spacing, place))):
+                for j, moved in enumerate(states[layer]):
                     at = 3 * layer + j
-                    keep(tap_ref, slice(at, at + 1), lanes, own_rows(d_drive * moved) * share)
+                    keep(tap_ref, slice(at, at + 1), lanes, own_rows(d_drive * moved) * (0.5 * share))
                 d_state = d_state + (
                     row[0:1] * later(d_drive, spacing, place)
                     + row[1:2] * d_drive
@@ -373,9 +374,9 @@
         time_kernel,
         out_shape=(
             jax.ShapeDtypeStruct((32, 12, 128), BF),
-            jax.ShapeDtypeStruct((256, 128), F32),
-            jax.ShapeDtypeStruct((9, 256), F32),
-            jax.ShapeDtypeStruct((1, 64), F32),
+            pltpu.VMEM((256, 128), F32),
+            pltpu.VMEM((9, 256), F32),
+            pltpu.VMEM((1, 64), F32),
         ),
         in_specs=[SMEM] + [VMEM] * 4,
         name="time_path",
@@ -483,7 +484,8 @@
     spot = lax.axis_index(("z", "core"))
     grad_scale = 1.0 / math.sqrt(FR * 128 * (signal.shape[1] // 64))
     packed = pack(freq_in, freq_taps, freq_out, time_in, time_taps, time_out)
-    gathered = near(exchange(packed, "ch"))
+    gathered = exchange(packed, "ch")
+    gathered = near(gathered)
     lanes = jnp.stack([plane_lanes(signal, plane), plane_lanes(cotangent, plane)], axis=0)
     halo = lax.ppermute(lanes, SEQ, halo_pairs())
     gain_f, gain_t = freq_gain[None], time_gain[None]

time: 136 us -> 135 us (level)
  no operation moved by 1% of the time
where the time goes in v7:
time: 135 us; the launch traced here: 134 us
  waiting for transfers between devices  58.4 us (43%)
  starting transfers between devices  55.1 us (41%)
  Pallas kernels  11.5 us (9%)
  local copies, waits for them, and re-layouts  6.78 us (5%)
  other arithmetic  1.67 us (1%)
    all_to_all x6, waiting for transfers between devices, exchange(): return lax.all_to_all(values, axes, 0, 0)  58.4 us
    all_to_all x6, starting transfers between devices, exchange(): return lax.all_to_all(values, axes, 0, 0)  46 us
    ppermute x3, starting transfers between devices, shards(): lax.ppermute(done, 'ch', [(i, (i + shift) % 4) for i in range(4)])  7.79 us
    pallas_call x1, Pallas kernels, time_path(): pl.pallas_call(time_kernel, out_shape=(jax.ShapeDtypeStruct((32, 12, 128)...  4.47 us
  transfers between devices with their start and end apart: 10, of which 6 were waited for; matrix products, arithmetic and copies ran while one was open for 3% of the time, Pallas kernels for 1%

profile of v7, /device:TPU:1, one launch (start us, length us, event | category | flops | bytes accessed | tf_op | source)
XLA Modules:
  0.0 134.5 jit_solution(9176830929768962019)
XLA Ops:
  0.6 0.9 pad_dynamic-slice_fusion
  1.5 0.1 pad_maximum_fusion.1
  1.6 1.3 collective-permute-start
  2.9 1.6 %pack.1 = bf16[4,144,128]{2,1,0:T(8,128)(2,1)} custom-call(bf16[64,64]{1,0:T(8,128)(2,1)} %freq_in.1, f32[3,64]{1,0:T(4,128)} %freq_taps.1, bf16[64,64]{1,0:T(8,128)(2,1)} %freq_out.1, bf16[64,64]{1,0:T(8,128)(2,1)} %time_in.1, f32[3,3,64]{2,1,0:T(4,128)} %time_taps.1, bf16[64,64]{1,0:T(8,128)(2,1)} %time_out.1), custom_call_target="tpu_custom_call" | custom-call | tf_op jit(solution)/shard_map/pack/pallas_call | solution.py:91
  4.5 5.0 %all-to-all-start = ((bf16[4,144,128]{2,1,0:T(8,128)(2,1)}), bf16[4,144,128]{2,1,0:T(8,128)(2,1)S(1)}, u32[]{:S(2)}, u32[]{:S(2)}) async-start(bf16[4,144,128]{2,1,0:T(8,128)(2,1)} %pack.1), calls=%async_computation | async-start | bytes 294912 | tf_op jit(solution)/shard_map/all_to_all | solution.py:472
  9.5 0.1 reshape_squeeze_stack.3.own_ref.pair_ref
  9.6 0.0 copy-start.1
  9.6 0.6 copy-done.1
  10.3 0.1 reshape.122
  10.4 0.1 copy.37
  10.5 0.1 stack.83.clone
  10.6 0.1 and.63
  10.7 0.1 and.64
  10.9 0.1 fusion.6
  11.0 0.1 reshape_squeeze.3.halo_ref
  11.1 0.1 fusion.4.cot_edge_ref
  11.2 3.2 %all-to-all-done.gathered_ref = bf16[4,144,128]{2,1,0:T(8,128)(2,1)S(1)} async-done(((bf16[4,144,128]{2,1,0:T(8,128)(2,1)}), bf16[4,144,128]{2,1,0:T(8,128)(2,1)S(1)}, u32[]{:S(2)}, u32[]{:S(2)}) %all-to-all-start) | async-done | bytes 147488 | tf_op jit(solution)/shard_map/all_to_all | solution.py:472
  14.4 2.3 %freq_forward.1 = (bf16[32,24,128]{2,1,0:T(8,128)(2,1)}, f32[320,256]{1,0:T(8,128)S(1)}) custom-call(bf16[320,64]{1,0:T(8,128)(2,1)S(1)} %reshape_squeeze_stack.3.own_ref.pair_ref, bf16[320,64]{1,0:T(8,128)(2,1)S(1)} %reshape_squeeze.3.halo_ref, bf16[32,8,128]{2,1,0:T(8,128)(2,1)S(1)} %fusion.1.cot_ref, bf16[2,4,128]{2,1,0:T(4,128)(2,1)S(1)} %fusion.4.cot_edge_ref, ...), custom_call_target="tpu_custom_call" | custom-call | tf_op jit(solution)/shard_map/freq_forward/pallas_call | solution.py:133
  16.7 18.1 %all-to-all-start.1 = ((bf16[32,24,128]{2,1,0:T(8,128)(2,1)}), bf16[32,24,128]{2,1,0:T(8,128)(2,1)S(1)}, u32[]{:S(2)}, u32[]{:S(2)}) async-start(bf16[32,24,128]{2,1,0:T(8,128)(2,1)} %get-tuple-element.27), calls=%async_computation.1 | async-start | bytes 393216 | tf_op jit(solution)/shard_map/all_to_all | solution.py:472
  34.8 0.1 copy.34
  34.9 0.1 iota_compare_fusion
  35.0 0.1 lt.41
  35.2 0.1 copy.36.marks_ref
  35.3 0.6 pad_add_fusion.2.flag_ref
  35.9 17.7 %all-to-all-done.1.message_ref = bf16[32,24,128]{2,1,0:T(8,128)(2,1)S(1)} async-done(((bf16[32,24,128]{2,1,0:T(8,128)(2,1)}), bf16[32,24,128]{2,1,0:T(8,128)(2,1)S(1)}, u32[]{:S(2)}, u32[]{:S(2)}) %all-to-all-start.1) | async-done | bytes 196640 | tf_op jit(solution)/shard_map/all_to_all | solution.py:472
  53.6 4.5 %time_path.1 = (bf16[32,12,128]{2,1,0:T(8,128)(2,1)}, f32[256,128]{1,0:T(8,128)S(1)}, f32[9,256]{1,0:T(8,128)S(1)}, f32[1,64]{1,0:T(1,128)S(1)}) custom-call(s32[2]{0:T(128)} %pad_add_fusion.2.flag_ref, bf16[32,24,128]{2,1,0:T(8,128)(2,1)S(1)} %all-to-all-done.1.message_ref, f32[256,2]{1,0:T(8,128)S(1)} %copy.36.marks_ref, ...), custom_call_target="tpu_custom_call" | custom-call | tf_op jit(solution)/shard_map/time_path/pallas_call | solution.py:373
  58.1 5.0 %all-to-all-start.2 = ((bf16[32,12,128]{2,1,0:T(8,128)(2,1)}), bf16[32,12,128]{2,1,0:T(8,128)(2,1)S(1)}, u32[]{:S(2)}, u32[]{:S(2)}) async-start(bf16[32,12,128]{2,1,0:T(8,128)(2,1)} %get-tuple-element.28), calls=%async_computation.2 | async-start | bytes 262144 | tf_op jit(solution)/shard_map/all_to_all | solution.py:472
  63.0 0.6 pad_add_fusion.1.flag_ref
  63.6 15.6 %all-to-all-done.2.arrived_ref = bf16[32,12,128]{2,1,0:T(8,128)(2,1)S(1)} async-done(((bf16[32,12,128]{2,1,0:T(8,128)(2,1)}), bf16[32,12,128]{2,1,0:T(8,128)(2,1)S(1)}, u32[]{:S(2)}, u32[]{:S(2)}) %all-to-all-start.2) | async-done | bytes 98336 | tf_op jit(solution)/shard_map/all_to_all | solution.py:472
  79.2 2.4 %freq_backward.1 = (bf16[288,128]{1,0:T(8,128)(2,1)}, bf16[32,24,128]{2,1,0:T(8,128)(2,1)}) custom-call(s32[2]{0:T(128)} %pad_add_fusion.1.flag_ref, bf16[320,64]{1,0:T(8,128)(2,1)S(1)} %reshape_squeeze_stack.3.own_ref.pair_ref, f32[320,256]{1,0:T(8,128)S(1)} %get-tuple-element.26.hidden_ref, bf16[32,12,128]{2,1,0:T(8,128)(2,1)S(1)} %all-to-all-done.2.arrived_ref, ...), custom_call_target="tpu_custom_call" | custom-call | tf_op jit(solution)/shard_map/freq_backward/pallas_call | solution.py:226
  81.6 2.8 %collective-permute-start.1 = (bf16[288,128]{1,0:T(8,128)(2,1)}, bf16[288,128]{1,0:T(8,128)(2,1)S(1)}, u32[]{:S(2)}, u32[]{:S(2)}) collective-permute-start(bf16[288,128]{1,0:T(8,128)(2,1)} %get-tuple-element.32), channel_id=1, source_target_pairs={{0,3},{1,0},{2,1},{3,2},{4,7},{5,4},{6,5},{7,6},{8,11},{9,8},{10,9... | collective-permute-start | bytes 221192 | tf_op jit(solution)/shard_map/ppermute | solution.py:506
  84.4 2.5 %collective-permute-start.3 = (bf16[288,128]{1,0:T(8,128)(2,1)}, bf16[288,128]{1,0:T(8,128)(2,1)S(1)}, u32[]{:S(2)}, u32[]{:S(2)}) collective-permute-start(bf16[288,128]{1,0:T(8,128)(2,1)} %get-tuple-element.32), channel_id=1, source_target_pairs={{0,1},{1,2},{2,3},{3,0},{4,5},{5,6},{6,7},{7,4},{8,9},{9,10},{10,1... | collective-permute-start | bytes 221192 | tf_op jit(solution)/shard_map/ppermute | solution.py:506
  86.9 2.5 %collective-permute-start.2 = (bf16[288,128]{1,0:T(8,128)(2,1)}, bf16[288,128]{1,0:T(8,128)(2,1)S(1)}, u32[]{:S(2)}, u32[]{:S(2)}) collective-permute-start(bf16[288,128]{1,0:T(8,128)(2,1)} %get-tuple-element.32), channel_id=1, source_target_pairs={{0,2},{1,3},{2,0},{3,1},{4,6},{5,7},{6,4},{7,5},{8,10},{9,11},{10,... | collective-permute-start | bytes 221192 | tf_op jit(solution)/shard_map/ppermute | solution.py:506
  89.5 8.4 %all-to-all-start.3 = ((bf16[32,24,128]{2,1,0:T(8,128)(2,1)}), bf16[32,24,128]{2,1,0:T(8,128)(2,1)S(1)}, u32[]{:S(2)}, u32[]{:S(2)}) async-start(bf16[32,24,128]{2,1,0:T(8,128)(2,1)} %get-tuple-element.33), calls=%async_computation.3 | async-start | bytes 393216 | tf_op jit(solution)/shard_map/all_to_all | solution.py:472
  97.9 0.0 collective-permute-done.2
  97.9 0.0 copy-start
  98.0 0.8 copy-done
  99.0 7.1 %all-to-all-done.3 = bf16[32,24,128]{2,1,0:T(8,128)(2,1)S(1)} async-done(((bf16[32,24,128]{2,1,0:T(8,128)(2,1)}), bf16[32,24,128]{2,1,0:T(8,128)(2,1)S(1)}, u32[]{:S(2)}, u32[]{:S(2)}) %all-to-all-start.3) | async-done | bytes 196640 | tf_op jit(solution)/shard_map/all_to_all | solution.py:472
  106.1 0.7 broadcast_in_dim.19
  106.8 3.5 %all-to-all-start.4 = ((bf16[16,24,128]{2,1,0:T(8,128)(2,1)}), bf16[16,24,128]{2,1,0:T(8,128)(2,1)S(1)}, u32[]{:S(2)}, u32[]{:S(2)}) async-start(bf16[16,24,128]{2,1,0:T(8,128)(2,1)} %broadcast_in_dim.19), calls=%async_computation.4 | async-start | bytes 196608 | tf_op jit(solution)/shard_map/all_to_all | solution.py:472
  110.3 11.7 %all-to-all-done.4 = bf16[16,24,128]{2,1,0:T(8,128)(2,1)S(1)} async-done(((bf16[16,24,128]{2,1,0:T(8,128)(2,1)}), bf16[16,24,128]{2,1,0:T(8,128)(2,1)S(1)}, u32[]{:S(2)}, u32[]{:S(2)}) %all-to-all-start.4) | async-done | bytes 98336 | tf_op jit(solution)/shard_map/all_to_all | solution.py:472
  122.0 0.6 broadcast_in_dim.20
  122.7 6.0 %all-to-all-start.5 = ((f32[8,24,128]{2,1,0:T(8,128)}), f32[8,24,128]{2,1,0:T(8,128)S(1)}, u32[]{:S(2)}, u32[]{:S(2)}) async-start(f32[8,24,128]{2,1,0:T(8,128)} %broadcast_in_dim.20), calls=%async_computation.5 | async-start | bytes 196608 | tf_op jit(solution)/shard_map/all_to_all | solution.py:472
  128.7 0.1 fusion.7
  128.8 0.9 reshape.125
  129.7 0.9 reshape.124
  130.5 3.1 %all-to-all-done.5.part_ref = f32[8,24,128]{2,1,0:T(8,128)S(1)} async-done(((f32[8,24,128]{2,1,0:T(8,128)}), f32[8,24,128]{2,1,0:T(8,128)S(1)}, u32[]{:S(2)}, u32[]{:S(2)}) %all-to-all-start.5) | async-done | bytes 98336 | tf_op jit(solution)/shard_map/all_to_all | solution.py:472
  133.7 0.8 finish.1
  (27 shorter events, 0.4 us)
Async XLA Ops:
  1.6 9.2 %collective-permute-start = (bf16[2,4,5120]{2,1,0:T(4,128)(2,1)S(1)}, bf16[2,4,5120]{2,1,0:T(4,128)(2,1)S(1)}, u32[]{:S(2)}, u32[]{:S(2)}) collective-permute-start(bf16[2,4,5120]{2,1,0:T(4,128)(2,1)S(1)} %pad_maximum_fusion.1), channel_id=1, source_target_pairs={{128,0},{132,4},{136,8},{140,12},{144,16},{148,20},{152,24},{156,2... | collective-permute-start | bytes 245768 | tf_op jit(solution)/shard_map/ppermute | solution.py:490
  4.5 9.9 %all-to-all-start = ((bf16[4,144,128]{2,1,0:T(8,128)(2,1)}), bf16[4,144,128]{2,1,0:T(8,128)(2,1)S(1)}, u32[]{:S(2)}, u32[]{:S(2)}) async-start(bf16[4,144,128]{2,1,0:T(8,128)(2,1)} %pack.1), calls=%async_computation | async-start | bytes 294912 | tf_op jit(solution)/shard_map/all_to_all | solution.py:472
  9.6 0.7 copy-start.1
  16.7 36.9 %all-to-all-start.1 = ((bf16[32,24,128]{2,1,0:T(8,128)(2,1)}), bf16[32,24,128]{2,1,0:T(8,128)(2,1)S(1)}, u32[]{:S(2)}, u32[]{:S(2)}) async-start(bf16[32,24,128]{2,1,0:T(8,128)(2,1)} %get-tuple-element.27), calls=%async_computation.1 | async-start | bytes 393216 | tf_op jit(solution)/shard_map/all_to_all | solution.py:472
  58.1 21.2 %all-to-all-start.2 = ((bf16[32,12,128]{2,1,0:T(8,128)(2,1)}), bf16[32,12,128]{2,1,0:T(8,128)(2,1)S(1)}, u32[]{:S(2)}, u32[]{:S(2)}) async-start(bf16[32,12,128]{2,1,0:T(8,128)(2,1)} %get-tuple-element.28), calls=%async_computation.2 | async-start | bytes 262144 | tf_op jit(solution)/shard_map/all_to_all | solution.py:472
  81.6 16.2 %collective-permute-start.1 = (bf16[288,128]{1,0:T(8,128)(2,1)}, bf16[288,128]{1,0:T(8,128)(2,1)S(1)}, u32[]{:S(2)}, u32[]{:S(2)}) collective-permute-start(bf16[288,128]{1,0:T(8,128)(2,1)} %get-tuple-element.32), channel_id=1, source_target_pairs={{0,3},{1,0},{2,1},{3,2},{4,7},{5,4},{6,5},{7,6},{8,11},{9,8},{10,9... | collective-permute-start | bytes 221192 | tf_op jit(solution)/shard_map/ppermute | solution.py:506
  84.4 13.5 %collective-permute-start.3 = (bf16[288,128]{1,0:T(8,128)(2,1)}, bf16[288,128]{1,0:T(8,128)(2,1)S(1)}, u32[]{:S(2)}, u32[]{:S(2)}) collective-permute-start(bf16[288,128]{1,0:T(8,128)(2,1)} %get-tuple-element.32), channel_id=1, source_target_pairs={{0,1},{1,2},{2,3},{3,0},{4,5},{5,6},{6,7},{7,4},{8,9},{9,10},{10,1... | collective-permute-start | bytes 221192 | tf_op jit(solution)/shard_map/ppermute | solution.py:506
  86.9 11.0 %collective-permute-start.2 = (bf16[288,128]{1,0:T(8,128)(2,1)}, bf16[288,128]{1,0:T(8,128)(2,1)S(1)}, u32[]{:S(2)}, u32[]{:S(2)}) collective-permute-start(bf16[288,128]{1,0:T(8,128)(2,1)} %get-tuple-element.32), channel_id=1, source_target_pairs={{0,2},{1,3},{2,0},{3,1},{4,6},{5,7},{6,4},{7,5},{8,10},{9,11},{10,... | collective-permute-start | bytes 221192 | tf_op jit(solution)/shard_map/ppermute | solution.py:506
  89.5 16.6 %all-to-all-start.3 = ((bf16[32,24,128]{2,1,0:T(8,128)(2,1)}), bf16[32,24,128]{2,1,0:T(8,128)(2,1)S(1)}, u32[]{:S(2)}, u32[]{:S(2)}) async-start(bf16[32,24,128]{2,1,0:T(8,128)(2,1)} %get-tuple-element.33), calls=%async_computation.3 | async-start | bytes 393216 | tf_op jit(solution)/shard_map/all_to_all | solution.py:472
  97.9 0.9 copy-start
  106.8 15.3 %all-to-all-start.4 = ((bf16[16,24,128]{2,1,0:T(8,128)(2,1)}), bf16[16,24,128]{2,1,0:T(8,128)(2,1)S(1)}, u32[]{:S(2)}, u32[]{:S(2)}) async-start(bf16[16,24,128]{2,1,0:T(8,128)(2,1)} %broadcast_in_dim.19), calls=%async_computation.4 | async-start | bytes 196608 | tf_op jit(solution)/shard_map/all_to_all | solution.py:472
  122.7 11.0 %all-to-all-start.5 = ((f32[8,24,128]{2,1,0:T(8,128)}), f32[8,24,128]{2,1,0:T(8,128)S(1)}, u32[]{:S(2)}, u32[]{:S(2)}) async-start(f32[8,24,128]{2,1,0:T(8,128)} %broadcast_in_dim.20), calls=%async_computation.5 | async-start | bytes 196608 | tf_op jit(solution)/shard_map/all_to_all | solution.py:472

commit v8 on v7

--- a/solution.py
+++ b/solution.py
@@ -89,7 +89,7 @@
 
 def pack(*weights):
     return pl.pallas_call(
-        pack_kernel, out_shape=jax.ShapeDtypeStruct((4, 144, 128), BF), name="pack"
+        pack_kernel, out_shape=pltpu.VMEM((4, 144, 128), BF), name="pack"
     )(*weights)
 
 
@@ -132,7 +132,7 @@
     rows = pair.shape[0]
     return pl.pallas_call(
         freq_forward_kernel,
-        out_shape=(jax.ShapeDtypeStruct((32, 24, 128), BF), pltpu.VMEM((rows, 256), F32)),
+        out_shape=(pltpu.VMEM((32, 24, 128), BF), pltpu.VMEM((rows, 256), F32)),
         scratch_shapes=[
             pltpu.VMEM((rows, 64), F32),
             pltpu.VMEM((256, 128), F32),
@@ -225,7 +225,7 @@
 def freq_backward(pair, hidden, arrived, gathered, gain, flags, sums):
     return pl.pallas_call(
         freq_backward_kernel,
-        out_shape=(jax.ShapeDtypeStruct((288, 128), BF), jax.ShapeDtypeStruct((32, 24, 128), BF)),
+        out_shape=(pltpu.VMEM((288, 128), BF), pltpu.VMEM((32, 24, 128), BF)),
         in_specs=[SMEM] + [VMEM] * 8,
         scratch_shapes=[
             pltpu.VMEM((512, 128), F32),
@@ -248,21 +248,22 @@
     return jnp.concatenate([turned(values[base:]), values[:base]], axis=0)
 
 
-def in_tiles(values, amount):
-    tiles = values.reshape(values.shape[0] // 8, 8, values.shape[1])
-    return pltpu.roll(tiles, amount % 8, 1).reshape(values.shape)
+def tiled(values):
+    return values.reshape(values.shape[0] // 8, 8, values.shape[1])
+
+
+def next_frame(values, place, edge, amount):
+    near_rows = pltpu.roll(tiled(values), amount % 8, 1)
+    far_rows = pltpu.roll(tiled(groups_on(values, -amount)), (-3 * amount) % 8, 1)
+    return jnp.where((place == edge)[None], far_rows, near_rows).reshape(values.shape)
 
 
 def later(values, spacing, place):
-    if spacing == 1:
-        return jnp.where(place == 3, in_tiles(groups_on(values, 1), 3), in_tiles(values, -1))
-    return groups_on(values, spacing // FR)
+    return next_frame(values, place, 3, -1) if spacing == 1 else groups_on(values, spacing // FR)
 
 
 def earlier(values, spacing, place):
-    if spacing == 1:
-        return jnp.where(place == 0, in_tiles(groups_on(values, -1), -3), in_tiles(values, 1))
-    return groups_on(values, -(spacing // FR))
+    return next_frame(values, place, 0, 1) if spacing == 1 else groups_on(values, -(spacing // FR))
 
 
 def own_rows(values):
@@ -292,7 +293,7 @@
     gain = gain_ref[...]
     valid, inside = marks_ref[:, 0:1], marks_ref[:, 1:2]
     spot = lax.broadcasted_iota(jnp.int32, (256, 1), 0)
-    place = lax.broadcasted_iota(jnp.int32, (256, 128), 0) & 3
+    place = lax.broadcasted_iota(jnp.int32, (8, 128), 0) & 3
 
     def work(slot):
         share = jnp.where(flag_ref[0] > 0, 1.0, 0.0).astype(F32) if slot == 2 else 1.0
@@ -373,7 +374,7 @@
     return pl.pallas_call(
         time_kernel,
         out_shape=(
-            jax.ShapeDtypeStruct((32, 12, 128), BF),
+            pltpu.VMEM((32, 12, 128), BF),
             pltpu.VMEM((256, 128), F32),
             pltpu.VMEM((9, 256), F32),
             pltpu.VMEM((1, 64), F32),

time: 135 us -> 135 us (level)
  no operation moved by 1% of the time
where the time goes in v8:
time: 135 us; the launch traced here: 134 us
  waiting for transfers between devices  59.2 us (44%)
  starting transfers between devices  55.1 us (41%)
  Pallas kernels  11.5 us (9%)
  local copies, waits for them, and re-layouts  5.93 us (4%)
  other arithmetic  1.67 us (1%)
    all_to_all x6, waiting for transfers between devices, exchange(): return lax.all_to_all(values, axes, 0, 0)  59.2 us
    all_to_all x6, starting transfers between devices, exchange(): return lax.all_to_all(values, axes, 0, 0)  46 us
    ppermute x3, starting transfers between devices, shards(): lax.ppermute(done, 'ch', [(i, (i + shift) % 4) for i in range(4)])  7.8 us
    pallas_call x1, Pallas kernels, time_path(): pl.pallas_call(time_kernel, out_shape=(pltpu.VMEM((32, 12, 128), BF), plt...  4.42 us
  transfers between devices with their start and end apart: 10, of which 6 were waited for; matrix products, arithmetic and copies ran while one was open for 3% of the time, Pallas kernels for 1%

profile of v8, /device:TPU:1, one launch (start us, length us, event | category | flops | bytes accessed | tf_op | source)
XLA Modules:
  0.0 134.4 jit_solution(8123137285878945594)
XLA Ops:
  0.6 0.9 pad_dynamic-slice_fusion
  1.5 0.1 pad_maximum_fusion.1
  1.6 1.3 collective-permute-start
  2.9 1.6 %pack.1 = bf16[4,144,128]{2,1,0:T(8,128)(2,1)} custom-call(bf16[64,64]{1,0:T(8,128)(2,1)} %freq_in.1, f32[3,64]{1,0:T(4,128)} %freq_taps.1, bf16[64,64]{1,0:T(8,128)(2,1)} %freq_out.1, bf16[64,64]{1,0:T(8,128)(2,1)} %time_in.1, f32[3,3,64]{2,1,0:T(4,128)} %time_taps.1, bf16[64,64]{1,0:T(8,128)(2,1)} %time_out.1), custom_call_target="tpu_custom_call" | custom-call | tf_op jit(solution)/shard_map/pack/pallas_call | solution.py:91
  4.4 5.0 %all-to-all-start = ((bf16[4,144,128]{2,1,0:T(8,128)(2,1)}), bf16[4,144,128]{2,1,0:T(8,128)(2,1)S(1)}, u32[]{:S(2)}, u32[]{:S(2)}) async-start(bf16[4,144,128]{2,1,0:T(8,128)(2,1)} %pack.1), calls=%async_computation | async-start | bytes 294912 | tf_op jit(solution)/shard_map/all_to_all | solution.py:473
  9.5 0.1 reshape_squeeze_stack.3.own_ref.pair_ref
  9.6 0.0 copy-start
  9.6 0.6 copy-done
  10.3 0.1 reshape.122
  10.4 0.1 copy.37
  10.5 0.1 stack.83.clone
  10.6 0.1 and.63
  10.7 0.1 and.64
  10.8 0.0 collective-permute-done
  10.8 0.1 fusion.6
  11.0 0.1 reshape_squeeze.3.halo_ref
  11.1 0.1 fusion.4.cot_edge_ref
  11.2 3.2 %all-to-all-done.gathered_ref = bf16[4,144,128]{2,1,0:T(8,128)(2,1)S(1)} async-done(((bf16[4,144,128]{2,1,0:T(8,128)(2,1)}), bf16[4,144,128]{2,1,0:T(8,128)(2,1)S(1)}, u32[]{:S(2)}, u32[]{:S(2)}) %all-to-all-start) | async-done | bytes 147488 | tf_op jit(solution)/shard_map/all_to_all | solution.py:473
  14.4 2.3 %freq_forward.1 = (bf16[32,24,128]{2,1,0:T(8,128)(2,1)}, f32[320,256]{1,0:T(8,128)S(1)}) custom-call(bf16[320,64]{1,0:T(8,128)(2,1)S(1)} %reshape_squeeze_stack.3.own_ref.pair_ref, bf16[320,64]{1,0:T(8,128)(2,1)S(1)} %reshape_squeeze.3.halo_ref, bf16[32,8,128]{2,1,0:T(8,128)(2,1)S(1)} %fusion.1.cot_ref, bf16[2,4,128]{2,1,0:T(4,128)(2,1)S(1)} %fusion.4.cot_edge_ref, ...), custom_call_target="tpu_custom_call" | custom-call | tf_op jit(solution)/shard_map/freq_forward/pallas_call | solution.py:133
  16.7 18.1 %all-to-all-start.1 = ((bf16[32,24,128]{2,1,0:T(8,128)(2,1)}), bf16[32,24,128]{2,1,0:T(8,128)(2,1)S(1)}, u32[]{:S(2)}, u32[]{:S(2)}) async-start(bf16[32,24,128]{2,1,0:T(8,128)(2,1)} %get-tuple-element.27), calls=%async_computation.1 | async-start | bytes 393216 | tf_op jit(solution)/shard_map/all_to_all | solution.py:473
  34.8 0.1 copy.34
  34.9 0.1 iota_compare_fusion
  35.0 0.1 lt.41
  35.2 0.1 copy.36.marks_ref
  35.3 0.6 pad_add_fusion.2.flag_ref
  35.9 17.7 %all-to-all-done.1.message_ref = bf16[32,24,128]{2,1,0:T(8,128)(2,1)S(1)} async-done(((bf16[32,24,128]{2,1,0:T(8,128)(2,1)}), bf16[32,24,128]{2,1,0:T(8,128)(2,1)S(1)}, u32[]{:S(2)}, u32[]{:S(2)}) %all-to-all-start.1) | async-done | bytes 196640 | tf_op jit(solution)/shard_map/all_to_all | solution.py:473
  53.6 4.4 %time_path.1 = (bf16[32,12,128]{2,1,0:T(8,128)(2,1)}, f32[256,128]{1,0:T(8,128)S(1)}, f32[9,256]{1,0:T(8,128)S(1)}, f32[1,64]{1,0:T(1,128)S(1)}) custom-call(s32[2]{0:T(128)} %pad_add_fusion.2.flag_ref, bf16[32,24,128]{2,1,0:T(8,128)(2,1)S(1)} %all-to-all-done.1.message_ref, f32[256,2]{1,0:T(8,128)S(1)} %copy.36.marks_ref, ...), custom_call_target="tpu_custom_call" | custom-call | tf_op jit(solution)/shard_map/time_path/pallas_call | solution.py:374
  58.0 5.0 %all-to-all-start.2 = ((bf16[32,12,128]{2,1,0:T(8,128)(2,1)}), bf16[32,12,128]{2,1,0:T(8,128)(2,1)S(1)}, u32[]{:S(2)}, u32[]{:S(2)}) async-start(bf16[32,12,128]{2,1,0:T(8,128)(2,1)} %get-tuple-element.28), calls=%async_computation.2 | async-start | bytes 262144 | tf_op jit(solution)/shard_map/all_to_all | solution.py:473
  63.0 0.6 pad_add_fusion.1.flag_ref
  63.6 15.6 %all-to-all-done.2.arrived_ref = bf16[32,12,128]{2,1,0:T(8,128)(2,1)S(1)} async-done(((bf16[32,12,128]{2,1,0:T(8,128)(2,1)}), bf16[32,12,128]{2,1,0:T(8,128)(2,1)S(1)}, u32[]{:S(2)}, u32[]{:S(2)}) %all-to-all-start.2) | async-done | bytes 98336 | tf_op jit(solution)/shard_map/all_to_all | solution.py:473
  79.2 2.4 %freq_backward.1 = (bf16[288,128]{1,0:T(8,128)(2,1)S(1)}, bf16[32,24,128]{2,1,0:T(8,128)(2,1)}) custom-call(s32[2]{0:T(128)} %pad_add_fusion.1.flag_ref, bf16[320,64]{1,0:T(8,128)(2,1)S(1)} %reshape_squeeze_stack.3.own_ref.pair_ref, f32[320,256]{1,0:T(8,128)S(1)} %get-tuple-element.26.hidden_ref, bf16[32,12,128]{2,1,0:T(8,128)(2,1)S(1)} %all-to-all-done.2.arrived_ref, ...), custom_call_target="tpu_custom_call" | custom-call | tf_op jit(solution)/shard_map/freq_backward/pallas_call | solution.py:226
  81.6 2.8 %collective-permute-start.1 = (bf16[288,128]{1,0:T(8,128)(2,1)S(1)}, bf16[288,128]{1,0:T(8,128)(2,1)S(1)}, u32[]{:S(2)}, u32[]{:S(2)}) collective-permute-start(bf16[288,128]{1,0:T(8,128)(2,1)S(1)} %get-tuple-element.32), channel_id=1, source_target_pairs={{0,3},{1,0},{2,1},{3,2},{4,7},{5,4},{6,5},{7,6},{8,11},{9,8},{10,9... | collective-permute-start | bytes 221192 | tf_op jit(solution)/shard_map/ppermute | solution.py:507
  84.4 2.5 %collective-permute-start.3 = (bf16[288,128]{1,0:T(8,128)(2,1)S(1)}, bf16[288,128]{1,0:T(8,128)(2,1)S(1)}, u32[]{:S(2)}, u32[]{:S(2)}) collective-permute-start(bf16[288,128]{1,0:T(8,128)(2,1)S(1)} %get-tuple-element.32), channel_id=1, source_target_pairs={{0,1},{1,2},{2,3},{3,0},{4,5},{5,6},{6,7},{7,4},{8,9},{9,10},{10,1... | collective-permute-start | bytes 221192 | tf_op jit(solution)/shard_map/ppermute | solution.py:507
  86.9 2.5 %collective-permute-start.2 = (bf16[288,128]{1,0:T(8,128)(2,1)S(1)}, bf16[288,128]{1,0:T(8,128)(2,1)S(1)}, u32[]{:S(2)}, u32[]{:S(2)}) collective-permute-start(bf16[288,128]{1,0:T(8,128)(2,1)S(1)} %get-tuple-element.32), channel_id=1, source_target_pairs={{0,2},{1,3},{2,0},{3,1},{4,6},{5,7},{6,4},{7,5},{8,10},{9,11},{10,... | collective-permute-start | bytes 221192 | tf_op jit(solution)/shard_map/ppermute | solution.py:507
  89.4 8.4 %all-to-all-start.3 = ((bf16[32,24,128]{2,1,0:T(8,128)(2,1)}), bf16[32,24,128]{2,1,0:T(8,128)(2,1)S(1)}, u32[]{:S(2)}, u32[]{:S(2)}) async-start(bf16[32,24,128]{2,1,0:T(8,128)(2,1)} %get-tuple-element.33), calls=%async_computation.3 | async-start | bytes 393216 | tf_op jit(solution)/shard_map/all_to_all | solution.py:473
  97.8 0.0 collective-permute-done.1
  97.9 0.0 collective-permute-done.2
  98.1 8.0 %all-to-all-done.3 = bf16[32,24,128]{2,1,0:T(8,128)(2,1)S(1)} async-done(((bf16[32,24,128]{2,1,0:T(8,128)(2,1)}), bf16[32,24,128]{2,1,0:T(8,128)(2,1)S(1)}, u32[]{:S(2)}, u32[]{:S(2)}) %all-to-all-start.3) | async-done | bytes 196640 | tf_op jit(solution)/shard_map/all_to_all | solution.py:473
  106.1 0.7 broadcast_in_dim.19
  106.7 3.5 %all-to-all-start.4 = ((bf16[16,24,128]{2,1,0:T(8,128)(2,1)}), bf16[16,24,128]{2,1,0:T(8,128)(2,1)S(1)}, u32[]{:S(2)}, u32[]{:S(2)}) async-start(bf16[16,24,128]{2,1,0:T(8,128)(2,1)} %broadcast_in_dim.19), calls=%async_computation.4 | async-start | bytes 196608 | tf_op jit(solution)/shard_map/all_to_all | solution.py:473
  110.3 11.7 %all-to-all-done.4 = bf16[16,24,128]{2,1,0:T(8,128)(2,1)S(1)} async-done(((bf16[16,24,128]{2,1,0:T(8,128)(2,1)}), bf16[16,24,128]{2,1,0:T(8,128)(2,1)S(1)}, u32[]{:S(2)}, u32[]{:S(2)}) %all-to-all-start.4) | async-done | bytes 98336 | tf_op jit(solution)/shard_map/all_to_all | solution.py:473
  122.0 0.7 broadcast_in_dim.20
  122.6 6.0 %all-to-all-start.5 = ((f32[8,24,128]{2,1,0:T(8,128)}), f32[8,24,128]{2,1,0:T(8,128)S(1)}, u32[]{:S(2)}, u32[]{:S(2)}) async-start(f32[8,24,128]{2,1,0:T(8,128)} %broadcast_in_dim.20), calls=%async_computation.5 | async-start | bytes 196608 | tf_op jit(solution)/shard_map/all_to_all | solution.py:473
  128.6 0.1 fusion.7
  128.8 0.9 reshape.125
  129.6 0.9 reshape.124
  130.5 3.1 %all-to-all-done.5.part_ref = f32[8,24,128]{2,1,0:T(8,128)S(1)} async-done(((f32[8,24,128]{2,1,0:T(8,128)}), f32[8,24,128]{2,1,0:T(8,128)S(1)}, u32[]{:S(2)}, u32[]{:S(2)}) %all-to-all-start.5) | async-done | bytes 98336 | tf_op jit(solution)/shard_map/all_to_all | solution.py:473
  133.6 0.8 finish.1
  (25 shorter events, 0.4 us)
Async XLA Ops:
  1.6 9.2 %collective-permute-start = (bf16[2,4,5120]{2,1,0:T(4,128)(2,1)S(1)}, bf16[2,4,5120]{2,1,0:T(4,128)(2,1)S(1)}, u32[]{:S(2)}, u32[]{:S(2)}) collective-permute-start(bf16[2,4,5120]{2,1,0:T(4,128)(2,1)S(1)} %pad_maximum_fusion.1), channel_id=1, source_target_pairs={{128,0},{132,4},{136,8},{140,12},{144,16},{148,20},{152,24},{156,2... | collective-permute-start | bytes 245768 | tf_op jit(solution)/shard_map/ppermute | solution.py:491
  4.4 9.9 %all-to-all-start = ((bf16[4,144,128]{2,1,0:T(8,128)(2,1)}), bf16[4,144,128]{2,1,0:T(8,128)(2,1)S(1)}, u32[]{:S(2)}, u32[]{:S(2)}) async-start(bf16[4,144,128]{2,1,0:T(8,128)(2,1)} %pack.1), calls=%async_computation | async-start | bytes 294912 | tf_op jit(solution)/shard_map/all_to_all | solution.py:473
  9.6 0.7 copy-start
  16.7 36.9 %all-to-all-start.1 = ((bf16[32,24,128]{2,1,0:T(8,128)(2,1)}), bf16[32,24,128]{2,1,0:T(8,128)(2,1)S(1)}, u32[]{:S(2)}, u32[]{:S(2)}) async-start(bf16[32,24,128]{2,1,0:T(8,128)(2,1)} %get-tuple-element.27), calls=%async_computation.1 | async-start | bytes 393216 | tf_op jit(solution)/shard_map/all_to_all | solution.py:473
  58.0 21.2 %all-to-all-start.2 = ((bf16[32,12,128]{2,1,0:T(8,128)(2,1)}), bf16[32,12,128]{2,1,0:T(8,128)(2,1)S(1)}, u32[]{:S(2)}, u32[]{:S(2)}) async-start(bf16[32,12,128]{2,1,0:T(8,128)(2,1)} %get-tuple-element.28), calls=%async_computation.2 | async-start | bytes 262144 | tf_op jit(solution)/shard_map/all_to_all | solution.py:473
  81.6 16.2 %collective-permute-start.1 = (bf16[288,128]{1,0:T(8,128)(2,1)S(1)}, bf16[288,128]{1,0:T(8,128)(2,1)S(1)}, u32[]{:S(2)}, u32[]{:S(2)}) collective-permute-start(bf16[288,128]{1,0:T(8,128)(2,1)S(1)} %get-tuple-element.32), channel_id=1, source_target_pairs={{0,3},{1,0},{2,1},{3,2},{4,7},{5,4},{6,5},{7,6},{8,11},{9,8},{10,9... | collective-permute-start | bytes 221192 | tf_op jit(solution)/shard_map/ppermute | solution.py:507
  84.4 13.5 %collective-permute-start.3 = (bf16[288,128]{1,0:T(8,128)(2,1)S(1)}, bf16[288,128]{1,0:T(8,128)(2,1)S(1)}, u32[]{:S(2)}, u32[]{:S(2)}) collective-permute-start(bf16[288,128]{1,0:T(8,128)(2,1)S(1)} %get-tuple-element.32), channel_id=1, source_target_pairs={{0,1},{1,2},{2,3},{3,0},{4,5},{5,6},{6,7},{7,4},{8,9},{9,10},{10,1... | collective-permute-start | bytes 221192 | tf_op jit(solution)/shard_map/ppermute | solution.py:507
  86.9 11.0 %collective-permute-start.2 = (bf16[288,128]{1,0:T(8,128)(2,1)S(1)}, bf16[288,128]{1,0:T(8,128)(2,1)S(1)}, u32[]{:S(2)}, u32[]{:S(2)}) collective-permute-start(bf16[288,128]{1,0:T(8,128)(2,1)S(1)} %get-tuple-element.32), channel_id=1, source_target_pairs={{0,2},{1,3},{2,0},{3,1},{4,6},{5,7},{6,4},{7,5},{8,10},{9,11},{10,... | collective-permute-start | bytes 221192 | tf_op jit(solution)/shard_map/ppermute | solution.py:507
  89.4 16.6 %all-to-all-start.3 = ((bf16[32,24,128]{2,1,0:T(8,128)(2,1)}), bf16[32,24,128]{2,1,0:T(8,128)(2,1)S(1)}, u32[]{:S(2)}, u32[]{:S(2)}) async-start(bf16[32,24,128]{2,1,0:T(8,128)(2,1)} %get-tuple-element.33), calls=%async_computation.3 | async-start | bytes 393216 | tf_op jit(solution)/shard_map/all_to_all | solution.py:473
  106.7 15.3 %all-to-all-start.4 = ((bf16[16,24,128]{2,1,0:T(8,128)(2,1)}), bf16[16,24,128]{2,1,0:T(8,128)(2,1)S(1)}, u32[]{:S(2)}, u32[]{:S(2)}) async-start(bf16[16,24,128]{2,1,0:T(8,128)(2,1)} %broadcast_in_dim.19), calls=%async_computation.4 | async-start | bytes 196608 | tf_op jit(solution)/shard_map/all_to_all | solution.py:473
  122.6 11.0 %all-to-all-start.5 = ((f32[8,24,128]{2,1,0:T(8,128)}), f32[8,24,128]{2,1,0:T(8,128)S(1)}, u32[]{:S(2)}, u32[]{:S(2)}) async-start(f32[8,24,128]{2,1,0:T(8,128)} %broadcast_in_dim.20), calls=%async_computation.5 | async-start | bytes 196608 | tf_op jit(solution)/shard_map/all_to_all | solution.py:473

commit v9 on v8

--- a/solution.py
+++ b/solution.py
@@ -490,15 +490,17 @@
     lanes = jnp.stack([plane_lanes(signal, plane), plane_lanes(cotangent, plane)], axis=0)
     halo = lax.ppermute(lanes, SEQ, halo_pairs())
     gain_f, gain_t = freq_gain[None], time_gain[None]
-    x_rows, x_halo = near(lanes[0].reshape(FR * ROWS, 64)), near(halo[0].reshape(FR * ROWS, 64))
+    marks = frame_marks(counts, x_at)
+    beside = (spot == EDGE) | (spot == EDGE + 1)
+    edge = jnp.stack([jnp.where((plane == 3) & (spot == EDGE + 1), 1, 0), jnp.where(beside, 1, 0)])
+    flags = jnp.stack([jnp.where(plane == 3, 1, 0), jnp.where(plane > 0, 1, 0)])
+    x_rows = lanes[0].reshape(FR * ROWS, 64)
+    x_rows, marks, edge, flags = lax.optimization_barrier((x_rows, marks, edge, flags))
+    marks, x_rows, x_halo = near(marks), near(x_rows), near(halo[0].reshape(FR * ROWS, 64))
     message, hidden = freq_forward(x_rows, x_halo, *cot_message(lanes[1], halo[1]), gathered, gain_f)
     bands = near(exchange(message, ("z", "core")))
-    marks = near(frame_marks(counts, x_at))
-    beside = (spot == EDGE) | (spot == EDGE + 1)
-    edge = jnp.stack([jnp.where((plane == 3) & (spot == EDGE + 1), 1, 0), jnp.where(beside, 1, 0)])
     mixed, *sums = time_path(bands, marks, gathered, gain_t, edge)
     arrived = near(exchange(mixed, ("z", "core")))
-    flags = jnp.stack([jnp.where(plane == 3, 1, 0), jnp.where(plane > 0, 1, 0)])
     done, pieces = freq_backward(x_rows, hidden, arrived, gathered, gain_f, flags, sums)
     part = exchange(pieces, ("x", "core", "ch"))
     part = jnp.broadcast_to(jnp.sum(part.astype(F32), axis=0).astype(BF), (16, 24, 128))

time: 135 us -> 134 us (level)
  blocking collectives: 0 us -> 57.3 us
  waiting for transfers between devices: 59.2 us -> 24.6 us
  starting transfers between devices: 55.1 us -> 32.4 us
    all_to_all x0 -> x2, blocking collectives: none -> 57.3 us  [exchange(): return lax.all_to_all(values, axes, 0, 0)]
    all_to_all x6 -> x4, waiting for transfers between devices: 59.2 us -> 24.6 us  [exchange(): return lax.all_to_all(values, axes, 0, 0)]
    all_to_all x6 -> x4, starting transfers between devices: 46 us -> 23.3 us  [exchange(): return lax.all_to_all(values, axes, 0, 0)]
  transfers between devices with their start and end apart: 10 -> 8, of which waited for: 6 -> 4; matrix products, arithmetic and copies ran while one was open for 3% -> 3% of each run, Pallas kernels for 1% -> 1%
where the time goes in v9:
time: 134 us; the launch traced here: 133 us
  blocking collectives  57.3 us (43%)
  starting transfers between devices  32.4 us (24%)
  waiting for transfers between devices  24.6 us (18%)
  Pallas kernels  10.2 us (8%)
  local copies, waits for them, and re-layouts  6.24 us (5%)
    all_to_all x2, blocking collectives, exchange(): return lax.all_to_all(values, axes, 0, 0)  57.3 us
    all_to_all x4, waiting for transfers between devices, exchange(): return lax.all_to_all(values, axes, 0, 0)  24.6 us
    all_to_all x4, starting transfers between devices, exchange(): return lax.all_to_all(values, axes, 0, 0)  23.3 us
    ppermute x3, starting transfers between devices, shards(): lax.ppermute(done, 'ch', [(i, (i + shift) % 4) for i in range(4)])  7.79 us
    pallas_call x1, Pallas kernels, time_path(): pl.pallas_call(time_kernel, out_shape=(pltpu.VMEM((32, 12, 128), BF), plt...  3.77 us
  transfers between devices with their start and end apart: 8, of which 4 were waited for; matrix products, arithmetic and copies ran while one was open for 3% of the time, Pallas kernels for 1%

profile of v9, /device:TPU:1, one launch (start us, length us, event | category | flops | bytes accessed | tf_op | source)
XLA Modules:
  0.0 132.9 jit_solution(13697708876536735906)
XLA Ops:
  0.7 0.9 fusion.8
  1.5 0.0 copy-done
  1.5 0.1 fusion.9
  1.6 0.1 pad_maximum_fusion.1
  1.7 1.3 collective-permute-start
  3.0 1.6 %pack.1 = bf16[4,144,128]{2,1,0:T(8,128)(2,1)} custom-call(bf16[64,64]{1,0:T(8,128)(2,1)} %freq_in.1, f32[3,64]{1,0:T(4,128)} %freq_taps.1, bf16[64,64]{1,0:T(8,128)(2,1)} %freq_out.1, bf16[64,64]{1,0:T(8,128)(2,1)} %time_in.1, f32[3,3,64]{2,1,0:T(4,128)} %time_taps.1, bf16[64,64]{1,0:T(8,128)(2,1)} %time_out.1), custom_call_target="tpu_custom_call" | custom-call | tf_op jit(solution)/shard_map/pack/pallas_call | solution.py:91
  4.6 5.1 %all-to-all-start = ((bf16[4,144,128]{2,1,0:T(8,128)(2,1)}), bf16[4,144,128]{2,1,0:T(8,128)(2,1)S(1)}, u32[]{:S(2)}, u32[]{:S(2)}) async-start(bf16[4,144,128]{2,1,0:T(8,128)(2,1)} %pack.1), calls=%async_computation | async-start | bytes 294912 | tf_op jit(solution)/shard_map/all_to_all | solution.py:473
  9.7 0.1 reshape.121
  9.8 0.1 pad_dynamic-slice_fusion
  9.9 0.7 copy-done.1
  10.6 0.1 pad_dynamic-slice_fusion.1
  10.7 0.1 copy.34
  10.8 0.1 stack.71.clone
  10.9 0.1 and.62
  11.0 0.1 and.63
  11.1 0.1 copy.31
  11.2 0.1 iota_compare_fusion
  11.3 0.1 lt.41
  11.5 0.2 copy.33
  11.6 0.1 reshape_squeeze_stack.3.own_ref.pair_ref
  11.8 0.6 pad_add_fusion.2
  12.4 0.0 collective-permute-done
  12.4 0.1 fusion.6
  12.5 0.1 reshape_squeeze.3.halo_ref
  12.7 0.1 fusion.4.cot_edge_ref
  12.8 1.8 %all-to-all-done.gathered_ref = bf16[4,144,128]{2,1,0:T(8,128)(2,1)S(1)} async-done(((bf16[4,144,128]{2,1,0:T(8,128)(2,1)}), bf16[4,144,128]{2,1,0:T(8,128)(2,1)S(1)}, u32[]{:S(2)}, u32[]{:S(2)}) %all-to-all-start) | async-done | bytes 147488 | tf_op jit(solution)/shard_map/all_to_all | solution.py:473
  14.6 1.6 %freq_forward.1 = (bf16[32,24,128]{2,1,0:T(8,128)(2,1)S(1)}, f32[320,256]{1,0:T(8,128)S(1)}) custom-call(bf16[320,64]{1,0:T(8,128)(2,1)S(1)} %reshape_squeeze_stack.3.own_ref.pair_ref, bf16[320,64]{1,0:T(8,128)(2,1)S(1)} %reshape_squeeze.3.halo_ref, bf16[32,8,128]{2,1,0:T(8,128)(2,1)S(1)} %fusion.1.cot_ref, bf16[2,4,128]{2,1,0:T(4,128)(2,1)S(1)} %fusion.4.cot_edge_ref, ...), custom_call_target="tpu_custom_call" | custom-call | tf_op jit(solution)/shard_map/freq_forward/pallas_call | solution.py:133
  16.3 36.7 %all_to_all.30.message_ref = bf16[32,24,128]{2,1,0:T(8,128)(2,1)S(1)} all-to-all(bf16[32,24,128]{2,1,0:T(8,128)(2,1)S(1)} %get-tuple-element.34), channel_id=1, replica_groups=mesh['x'=4,'z'=16,'core'=2,'ch'=4] {'z','core'}, dimensions={0} | all-to-all | bytes 393216 | tf_op jit(solution)/shard_map/all_to_all | solution.py:473
  53.0 3.8 %time_path.1 = (bf16[32,12,128]{2,1,0:T(8,128)(2,1)S(1)}, f32[256,128]{1,0:T(8,128)S(1)}, f32[9,256]{1,0:T(8,128)S(1)}, f32[1,64]{1,0:T(1,128)S(1)}) custom-call(s32[2]{0:T(128)} %get-tuple-element.33.flag_ref, bf16[32,24,128]{2,1,0:T(8,128)(2,1)S(1)} %all_to_all.30.message_ref, f32[256,2]{1,0:T(8,128)S(1)} %convert_element_type.11.marks_ref, ...), custom_call_target="tpu_custom_call" | custom-call | tf_op jit(solution)/shard_map/time_path/pallas_call | solution.py:374
  56.7 20.6 %all_to_all.31.arrived_ref = bf16[32,12,128]{2,1,0:T(8,128)(2,1)S(1)} all-to-all(bf16[32,12,128]{2,1,0:T(8,128)(2,1)S(1)} %get-tuple-element.36), channel_id=1, replica_groups=mesh['x'=4,'z'=16,'core'=2,'ch'=4] {'z','core'}, dimensions={0} | all-to-all | bytes 196608 | tf_op jit(solution)/shard_map/all_to_all | solution.py:473
  77.3 2.4 %freq_backward.1 = (bf16[288,128]{1,0:T(8,128)(2,1)S(1)}, bf16[32,24,128]{2,1,0:T(8,128)(2,1)}) custom-call(s32[2]{0:T(128)} %get-tuple-element.30.flag_ref, bf16[320,64]{1,0:T(8,128)(2,1)S(1)} %reshape_squeeze_stack.3.own_ref.pair_ref, f32[320,256]{1,0:T(8,128)S(1)} %get-tuple-element.32.hidden_ref, bf16[32,12,128]{2,1,0:T(8,128)(2,1)S(1)} %all_to_all.31.arrived_ref, ...), custom_call_target="tpu_custom_call" | custom-call | tf_op jit(solution)/shard_map/freq_backward/pallas_call | solution.py:226
  79.8 2.8 %collective-permute-start.1 = (bf16[288,128]{1,0:T(8,128)(2,1)S(1)}, bf16[288,128]{1,0:T(8,128)(2,1)S(1)}, u32[]{:S(2)}, u32[]{:S(2)}) collective-permute-start(bf16[288,128]{1,0:T(8,128)(2,1)S(1)} %get-tuple-element.40), channel_id=1, source_target_pairs={{0,3},{1,0},{2,1},{3,2},{4,7},{5,4},{6,5},{7,6},{8,11},{9,8},{10,9... | collective-permute-start | bytes 221192 | tf_op jit(solution)/shard_map/ppermute | solution.py:509
  82.6 2.5 %collective-permute-start.3 = (bf16[288,128]{1,0:T(8,128)(2,1)S(1)}, bf16[288,128]{1,0:T(8,128)(2,1)S(1)}, u32[]{:S(2)}, u32[]{:S(2)}) collective-permute-start(bf16[288,128]{1,0:T(8,128)(2,1)S(1)} %get-tuple-element.40), channel_id=1, source_target_pairs={{0,1},{1,2},{2,3},{3,0},{4,5},{5,6},{6,7},{7,4},{8,9},{9,10},{10,1... | collective-permute-start | bytes 221192 | tf_op jit(solution)/shard_map/ppermute | solution.py:509
  85.1 2.5 %collective-permute-start.2 = (bf16[288,128]{1,0:T(8,128)(2,1)S(1)}, bf16[288,128]{1,0:T(8,128)(2,1)S(1)}, u32[]{:S(2)}, u32[]{:S(2)}) collective-permute-start(bf16[288,128]{1,0:T(8,128)(2,1)S(1)} %get-tuple-element.40), channel_id=1, source_target_pairs={{0,2},{1,3},{2,0},{3,1},{4,6},{5,7},{6,4},{7,5},{8,10},{9,11},{10,... | collective-permute-start | bytes 221192 | tf_op jit(solution)/shard_map/ppermute | solution.py:509
  87.6 8.7 %all-to-all-start.3 = ((bf16[32,24,128]{2,1,0:T(8,128)(2,1)}), bf16[32,24,128]{2,1,0:T(8,128)(2,1)S(1)}, u32[]{:S(2)}, u32[]{:S(2)}) async-start(bf16[32,24,128]{2,1,0:T(8,128)(2,1)} %get-tuple-element.41), calls=%async_computation.3 | async-start | bytes 393216 | tf_op jit(solution)/shard_map/all_to_all | solution.py:473
  96.3 0.0 collective-permute-done.1
  96.3 0.0 collective-permute-done.2
  96.5 8.0 %all-to-all-done.3 = bf16[32,24,128]{2,1,0:T(8,128)(2,1)S(1)} async-done(((bf16[32,24,128]{2,1,0:T(8,128)(2,1)}), bf16[32,24,128]{2,1,0:T(8,128)(2,1)S(1)}, u32[]{:S(2)}, u32[]{:S(2)}) %all-to-all-start.3) | async-done | bytes 196640 | tf_op jit(solution)/shard_map/all_to_all | solution.py:473
  104.5 0.7 broadcast_in_dim.19
  105.1 3.5 %all-to-all-start.4 = ((bf16[16,24,128]{2,1,0:T(8,128)(2,1)}), bf16[16,24,128]{2,1,0:T(8,128)(2,1)S(1)}, u32[]{:S(2)}, u32[]{:S(2)}) async-start(bf16[16,24,128]{2,1,0:T(8,128)(2,1)} %broadcast_in_dim.19), calls=%async_computation.4 | async-start | bytes 196608 | tf_op jit(solution)/shard_map/all_to_all | solution.py:473
  108.7 11.7 %all-to-all-done.4 = bf16[16,24,128]{2,1,0:T(8,128)(2,1)S(1)} async-done(((bf16[16,24,128]{2,1,0:T(8,128)(2,1)}), bf16[16,24,128]{2,1,0:T(8,128)(2,1)S(1)}, u32[]{:S(2)}, u32[]{:S(2)}) %all-to-all-start.4) | async-done | bytes 98336 | tf_op jit(solution)/shard_map/all_to_all | solution.py:473
  120.4 0.7 broadcast_in_dim.20
  121.1 6.0 %all-to-all-start.5 = ((f32[8,24,128]{2,1,0:T(8,128)}), f32[8,24,128]{2,1,0:T(8,128)S(1)}, u32[]{:S(2)}, u32[]{:S(2)}) async-start(f32[8,24,128]{2,1,0:T(8,128)} %broadcast_in_dim.20), calls=%async_computation.5 | async-start | bytes 196608 | tf_op jit(solution)/shard_map/all_to_all | solution.py:473
  127.1 0.1 fusion.7
  127.2 0.9 reshape.125
  128.1 0.9 reshape.124
  128.9 3.1 %all-to-all-done.5.part_ref = f32[8,24,128]{2,1,0:T(8,128)S(1)} async-done(((f32[8,24,128]{2,1,0:T(8,128)}), f32[8,24,128]{2,1,0:T(8,128)S(1)}, u32[]{:S(2)}, u32[]{:S(2)}) %all-to-all-start.5) | async-done | bytes 98336 | tf_op jit(solution)/shard_map/all_to_all | solution.py:473
  132.1 0.8 finish.1
  (30 shorter events, 0.4 us)
Async XLA Ops:
  0.6 0.9 copy-start
  1.7 10.7 %collective-permute-start = (bf16[2,4,5120]{2,1,0:T(4,128)(2,1)S(1)}, bf16[2,4,5120]{2,1,0:T(4,128)(2,1)S(1)}, u32[]{:S(2)}, u32[]{:S(2)}) collective-permute-start(bf16[2,4,5120]{2,1,0:T(4,128)(2,1)S(1)} %pad_maximum_fusion.1), channel_id=1, source_target_pairs={{128,0},{132,4},{136,8},{140,12},{144,16},{148,20},{152,24},{156,2... | collective-permute-start | bytes 245768 | tf_op jit(solution)/shard_map/ppermute | solution.py:491
  4.6 5.1 %copy-start.2 = (s32[128]{0:T(128)S(1)}, s32[128]{0:T(128)}, u32[]{:S(2)}) copy-start(s32[128]{0:T(128)} %param.13) | copy-start | bytes 1540
  4.6 10.0 %all-to-all-start = ((bf16[4,144,128]{2,1,0:T(8,128)(2,1)}), bf16[4,144,128]{2,1,0:T(8,128)(2,1)S(1)}, u32[]{:S(2)}, u32[]{:S(2)}) async-start(bf16[4,144,128]{2,1,0:T(8,128)(2,1)} %pack.1), calls=%async_computation | async-start | bytes 294912 | tf_op jit(solution)/shard_map/all_to_all | solution.py:473
  9.7 0.9 copy-start.1
  79.8 16.5 %collective-permute-start.1 = (bf16[288,128]{1,0:T(8,128)(2,1)S(1)}, bf16[288,128]{1,0:T(8,128)(2,1)S(1)}, u32[]{:S(2)}, u32[]{:S(2)}) collective-permute-start(bf16[288,128]{1,0:T(8,128)(2,1)S(1)} %get-tuple-element.40), channel_id=1, source_target_pairs={{0,3},{1,0},{2,1},{3,2},{4,7},{5,4},{6,5},{7,6},{8,11},{9,8},{10,9... | collective-permute-start | bytes 221192 | tf_op jit(solution)/shard_map/ppermute | solution.py:509
  82.6 13.8 %collective-permute-start.3 = (bf16[288,128]{1,0:T(8,128)(2,1)S(1)}, bf16[288,128]{1,0:T(8,128)(2,1)S(1)}, u32[]{:S(2)}, u32[]{:S(2)}) collective-permute-start(bf16[288,128]{1,0:T(8,128)(2,1)S(1)} %get-tuple-element.40), channel_id=1, source_target_pairs={{0,1},{1,2},{2,3},{3,0},{4,5},{5,6},{6,7},{7,4},{8,9},{9,10},{10,1... | collective-permute-start | bytes 221192 | tf_op jit(solution)/shard_map/ppermute | solution.py:509
  85.1 11.2 %collective-permute-start.2 = (bf16[288,128]{1,0:T(8,128)(2,1)S(1)}, bf16[288,128]{1,0:T(8,128)(2,1)S(1)}, u32[]{:S(2)}, u32[]{:S(2)}) collective-permute-start(bf16[288,128]{1,0:T(8,128)(2,1)S(1)} %get-tuple-element.40), channel_id=1, source_target_pairs={{0,2},{1,3},{2,0},{3,1},{4,6},{5,7},{6,4},{7,5},{8,10},{9,11},{10,... | collective-permute-start | bytes 221192 | tf_op jit(solution)/shard_map/ppermute | solution.py:509
  87.6 16.8 %all-to-all-start.3 = ((bf16[32,24,128]{2,1,0:T(8,128)(2,1)}), bf16[32,24,128]{2,1,0:T(8,128)(2,1)S(1)}, u32[]{:S(2)}, u32[]{:S(2)}) async-start(bf16[32,24,128]{2,1,0:T(8,128)(2,1)} %get-tuple-element.41), calls=%async_computation.3 | async-start | bytes 393216 | tf_op jit(solution)/shard_map/all_to_all | solution.py:473
  105.1 15.3 %all-to-all-start.4 = ((bf16[16,24,128]{2,1,0:T(8,128)(2,1)}), bf16[16,24,128]{2,1,0:T(8,128)(2,1)S(1)}, u32[]{:S(2)}, u32[]{:S(2)}) async-start(bf16[16,24,128]{2,1,0:T(8,128)(2,1)} %broadcast_in_dim.19), calls=%async_computation.4 | async-start | bytes 196608 | tf_op jit(solution)/shard_map/all_to_all | solution.py:473
  121.1 11.0 %all-to-all-start.5 = ((f32[8,24,128]{2,1,0:T(8,128)}), f32[8,24,128]{2,1,0:T(8,128)S(1)}, u32[]{:S(2)}, u32[]{:S(2)}) async-start(f32[8,24,128]{2,1,0:T(8,128)} %broadcast_in_dim.20), calls=%async_computation.5 | async-start | bytes 196608 | tf_op jit(solution)/shard_map/all_to_all | solution.py:473

commit v10 on v9

--- a/solution.py
+++ b/solution.py
@@ -71,7 +71,21 @@
     return jnp.concatenate(parts, axis=1)
 
 
-def pack_kernel(freq_in, freq_taps, freq_out, time_in, time_taps, time_out, packed_ref):
+def pack_kernel(
+    plane_ref, signal, cotangent, freq_in, freq_taps, freq_out, time_in, time_taps, time_out, packed_ref, lanes_ref
+):
+    width = signal.shape[1]
+    for plane in range(4):
+
+        @pl.when(plane_ref[0] == plane)
+        def _():
+            first = 4096 * plane - 64 * LEAD
+            low, high = max(first, 0), min(first + 64 * ROWS, width)
+            if high - low < 64 * ROWS:
+                lanes_ref[...] = jnp.zeros_like(lanes_ref)
+            for i, source in enumerate((signal, cotangent)):
+                lanes_ref[i, :, low - first : high - first] = source[:, low:high]
+
     taps = jnp.concatenate(
         [freq_taps[...]] + [time_taps[k] for k in range(3)] + [jnp.zeros((4, 64), F32)], axis=0
     )
@@ -87,10 +101,13 @@
         packed_ref[peer, 128:144, :] = tap_w
 
 
-def pack(*weights):
+def pack(plane, signal, cotangent, *weights):
     return pl.pallas_call(
-        pack_kernel, out_shape=pltpu.VMEM((4, 144, 128), BF), name="pack"
-    )(*weights)
+        pack_kernel,
+        out_shape=(pltpu.VMEM((4, 144, 128), BF), pltpu.VMEM((2, FR, 64 * ROWS), BF)),
+        in_specs=[SMEM] + [VMEM] * 8,
+        name="pack",
+    )(plane.reshape(1), signal, cotangent, *weights)
 
 
 def freq_forward_kernel(
@@ -423,12 +440,6 @@
     return (got[0][0], got[1], got[2], got[3], got[4][0], got[5], got[6], got[7])
 
 
-def plane_lanes(values, plane):
-    frames, width = values.shape
-    padded = jnp.pad(values, ((0, 0), (LEAD * 64, (ROWS - LEAD + 192) * 64 - width)))
-    return lax.dynamic_slice(padded, (0, plane * 4096), (frames, ROWS * 64))
-
-
 def cot_message(own, halo):
     both = jnp.concatenate([own, halo], axis=0)
     mine = both[:, LEAD * 64 : LEAD * 64 + 4096].reshape(2 * FR, 32, 128).transpose(1, 0, 2)
@@ -484,10 +495,9 @@
     x_at = lax.axis_index("x")
     spot = lax.axis_index(("z", "core"))
     grad_scale = 1.0 / math.sqrt(FR * 128 * (signal.shape[1] // 64))
-    packed = pack(freq_in, freq_taps, freq_out, time_in, time_taps, time_out)
+    packed, lanes = pack(plane, signal, cotangent, freq_in, freq_taps, freq_out, time_in, time_taps, time_out)
     gathered = exchange(packed, "ch")
     gathered = near(gathered)
-    lanes = jnp.stack([plane_lanes(signal, plane), plane_lanes(cotangent, plane)], axis=0)
     halo = lax.ppermute(lanes, SEQ, halo_pairs())
     gain_f, gain_t = freq_gain[None], time_gain[None]
     marks = frame_marks(counts, x_at)

time: 134 us -> 132 us (0.985)
  blocking collectives: 57.3 us -> 55.9 us
    all_to_all x4, waiting for transfers between devices: 24.6 us -> 22.8 us  [exchange(): return lax.all_to_all(values, axes, 0, 0)]
    ppermute x3, starting transfers between devices: 7.79 us -> 9.38 us  [shards(): lax.ppermute(done, 'ch', [(i, (i + shift) % 4) for i in range(4)])]
    all_to_all x2, blocking collectives: 57.3 us -> 55.9 us  [exchange(): return lax.all_to_all(values, axes, 0, 0)]
  transfers between devices with their start and end apart: 8 -> 8, of which waited for: 4 -> 4; matrix products, arithmetic and copies ran while one was open for 3% -> 3% of each run, Pallas kernels for 1% -> 0%
where the time goes in v10:
time: 132 us; the launch traced here: 131 us
  blocking collectives  55.9 us (42%)
  starting transfers between devices  33.6 us (25%)
  waiting for transfers between devices  24.1 us (18%)
  Pallas kernels  10.5 us (8%)
  local copies, waits for them, and re-layouts  5.15 us (4%)
    all_to_all x2, blocking collectives, exchange(): return lax.all_to_all(values, axes, 0, 0)  55.9 us
    all_to_all x4, starting transfers between devices, exchange(): return lax.all_to_all(values, axes, 0, 0)  22.9 us
    all_to_all x4, waiting for transfers between devices, exchange(): return lax.all_to_all(values, axes, 0, 0)  22.8 us
    ppermute x3, starting transfers between devices, shards(): lax.ppermute(done, 'ch', [(i, (i + shift) % 4) for i in range(4)])  9.38 us
    pallas_call x1, Pallas kernels, time_path(): pl.pallas_call(time_kernel, out_shape=(pltpu.VMEM((32, 12, 128), BF), plt...  3.77 us
  transfers between devices with their start and end apart: 8, of which 4 were waited for; matrix products, arithmetic and copies ran while one was open for 3% of the time, Pallas kernels for 0%

profile of v10, /device:TPU:1, one launch (start us, length us, event | category | flops | bytes accessed | tf_op | source)
XLA Modules:
  0.0 131.2 jit_solution(1840286724395466601)
XLA Ops:
  0.7 1.8 %pack.1 = (bf16[4,144,128]{2,1,0:T(8,128)(2,1)}, bf16[2,4,5120]{2,1,0:T(4,128)(2,1)S(1)}) custom-call(s32[1]{0:T(128)} %bitcast.plane_ref, bf16[4,16448]{1,0:T(4,128)(2,1)} %signal.1, bf16[4,16448]{1,0:T(4,128)(2,1)} %cotangent.1, bf16[64,64]{1,0:T(8,128)(2,1)} %freq_in.1, f32[3,64]{1,0:T(4,128)} %freq_taps.1, bf16[64,64]{1,0:T(8,128)(2,1)} %freq_out.1, ...), custom_call_target="tpu_custom_call" | custom-call | tf_op jit(solution)/shard_map/pack/pallas_call | solution.py:105
  2.5 5.0 %all-to-all-start = ((bf16[4,144,128]{2,1,0:T(8,128)(2,1)}), bf16[4,144,128]{2,1,0:T(8,128)(2,1)S(1)}, u32[]{:S(2)}, u32[]{:S(2)}) async-start(bf16[4,144,128]{2,1,0:T(8,128)(2,1)} %get-tuple-element.35), calls=%async_computation | async-start | bytes 294912 | tf_op jit(solution)/shard_map/all_to_all | solution.py:484
  7.5 1.3 collective-permute-start
  8.8 0.0 copy-start
  8.8 0.6 copy-done
  9.4 0.1 reshape.125
  9.6 0.1 copy.34
  9.7 0.1 stack.62.clone
  9.8 0.1 and.62
  9.9 0.1 and.63
  10.1 0.1 copy.31
  10.1 0.1 iota_compare_fusion
  10.2 0.1 lt.36
  10.4 0.2 copy.33
  10.6 0.1 reshape_squeeze.6.own_ref.pair_ref
  10.7 0.6 pad_add_fusion.2
  11.3 1.3 collective-permute-done
  12.7 0.1 fusion.6
  12.8 0.1 reshape_squeeze.7.halo_ref
  12.9 0.1 fusion.4.cot_edge_ref
  13.0 0.0 all-to-all-done.gathered_ref
  13.0 1.6 %freq_forward.1 = (bf16[32,24,128]{2,1,0:T(8,128)(2,1)S(1)}, f32[320,256]{1,0:T(8,128)S(1)}) custom-call(bf16[320,64]{1,0:T(8,128)(2,1)S(1)} %reshape_squeeze.6.own_ref.pair_ref, bf16[320,64]{1,0:T(8,128)(2,1)S(1)} %reshape_squeeze.7.halo_ref, bf16[32,8,128]{2,1,0:T(8,128)(2,1)S(1)} %fusion.1.cot_ref, bf16[2,4,128]{2,1,0:T(4,128)(2,1)S(1)} %fusion.4.cot_edge_ref, ...), custom_call_target="tpu_custom_call" | custom-call | tf_op jit(solution)/shard_map/freq_forward/pallas_call | solution.py:150
  14.7 35.3 %all_to_all.30.message_ref = bf16[32,24,128]{2,1,0:T(8,128)(2,1)S(1)} all-to-all(bf16[32,24,128]{2,1,0:T(8,128)(2,1)S(1)} %get-tuple-element.38), channel_id=1, replica_groups=mesh['x'=4,'z'=16,'core'=2,'ch'=4] {'z','core'}, dimensions={0} | all-to-all | bytes 393216 | tf_op jit(solution)/shard_map/all_to_all | solution.py:484
  50.0 3.8 %time_path.1 = (bf16[32,12,128]{2,1,0:T(8,128)(2,1)S(1)}, f32[256,128]{1,0:T(8,128)S(1)}, f32[9,256]{1,0:T(8,128)S(1)}, f32[1,64]{1,0:T(1,128)S(1)}) custom-call(s32[2]{0:T(128)} %get-tuple-element.37.flag_ref, bf16[32,24,128]{2,1,0:T(8,128)(2,1)S(1)} %all_to_all.30.message_ref, f32[256,2]{1,0:T(8,128)S(1)} %convert_element_type.8.marks_ref, ...), custom_call_target="tpu_custom_call" | custom-call | tf_op jit(solution)/shard_map/time_path/pallas_call | solution.py:391
  53.7 20.6 %all_to_all.31.arrived_ref = bf16[32,12,128]{2,1,0:T(8,128)(2,1)S(1)} all-to-all(bf16[32,12,128]{2,1,0:T(8,128)(2,1)S(1)} %get-tuple-element.40), channel_id=1, replica_groups=mesh['x'=4,'z'=16,'core'=2,'ch'=4] {'z','core'}, dimensions={0} | all-to-all | bytes 196608 | tf_op jit(solution)/shard_map/all_to_all | solution.py:484
  74.3 2.4 %freq_backward.1 = (bf16[288,128]{1,0:T(8,128)(2,1)S(1)}, bf16[32,24,128]{2,1,0:T(8,128)(2,1)}) custom-call(s32[2]{0:T(128)} %get-tuple-element.33.flag_ref, bf16[320,64]{1,0:T(8,128)(2,1)S(1)} %reshape_squeeze.6.own_ref.pair_ref, f32[320,256]{1,0:T(8,128)S(1)} %get-tuple-element.36.hidden_ref, bf16[32,12,128]{2,1,0:T(8,128)(2,1)S(1)} %all_to_all.31.arrived_ref, ...), custom_call_target="tpu_custom_call" | custom-call | tf_op jit(solution)/shard_map/freq_backward/pallas_call | solution.py:243
  76.8 3.8 %collective-permute-start.1 = (bf16[288,128]{1,0:T(8,128)(2,1)S(1)}, bf16[288,128]{1,0:T(8,128)(2,1)S(1)}, u32[]{:S(2)}, u32[]{:S(2)}) collective-permute-start(bf16[288,128]{1,0:T(8,128)(2,1)S(1)} %get-tuple-element.44), channel_id=1, source_target_pairs={{0,3},{1,0},{2,1},{3,2},{4,7},{5,4},{6,5},{7,6},{8,11},{9,8},{10,9... | collective-permute-start | bytes 221192 | tf_op jit(solution)/shard_map/ppermute | solution.py:519
  80.6 1.9 %collective-permute-start.3 = (bf16[288,128]{1,0:T(8,128)(2,1)S(1)}, bf16[288,128]{1,0:T(8,128)(2,1)S(1)}, u32[]{:S(2)}, u32[]{:S(2)}) collective-permute-start(bf16[288,128]{1,0:T(8,128)(2,1)S(1)} %get-tuple-element.44), channel_id=1, source_target_pairs={{0,1},{1,2},{2,3},{3,0},{4,5},{5,6},{6,7},{7,4},{8,9},{9,10},{10,1... | collective-permute-start | bytes 221192 | tf_op jit(solution)/shard_map/ppermute | solution.py:519
  82.5 3.7 %collective-permute-start.2 = (bf16[288,128]{1,0:T(8,128)(2,1)S(1)}, bf16[288,128]{1,0:T(8,128)(2,1)S(1)}, u32[]{:S(2)}, u32[]{:S(2)}) collective-permute-start(bf16[288,128]{1,0:T(8,128)(2,1)S(1)} %get-tuple-element.44), channel_id=1, source_target_pairs={{0,2},{1,3},{2,0},{3,1},{4,6},{5,7},{6,4},{7,5},{8,10},{9,11},{10,... | collective-permute-start | bytes 221192 | tf_op jit(solution)/shard_map/ppermute | solution.py:519
  86.2 8.4 %all-to-all-start.3 = ((bf16[32,24,128]{2,1,0:T(8,128)(2,1)}), bf16[32,24,128]{2,1,0:T(8,128)(2,1)S(1)}, u32[]{:S(2)}, u32[]{:S(2)}) async-start(bf16[32,24,128]{2,1,0:T(8,128)(2,1)} %get-tuple-element.45), calls=%async_computation.3 | async-start | bytes 393216 | tf_op jit(solution)/shard_map/all_to_all | solution.py:484
  94.6 0.0 collective-permute-done.1
  94.6 0.0 collective-permute-done.2
  94.7 0.0 collective-permute-done.3
  94.8 8.0 %all-to-all-done.3 = bf16[32,24,128]{2,1,0:T(8,128)(2,1)S(1)} async-done(((bf16[32,24,128]{2,1,0:T(8,128)(2,1)}), bf16[32,24,128]{2,1,0:T(8,128)(2,1)S(1)}, u32[]{:S(2)}, u32[]{:S(2)}) %all-to-all-start.3) | async-done | bytes 196640 | tf_op jit(solution)/shard_map/all_to_all | solution.py:484
  102.8 0.7 broadcast_in_dim.19
  103.5 3.5 %all-to-all-start.4 = ((bf16[16,24,128]{2,1,0:T(8,128)(2,1)}), bf16[16,24,128]{2,1,0:T(8,128)(2,1)S(1)}, u32[]{:S(2)}, u32[]{:S(2)}) async-start(bf16[16,24,128]{2,1,0:T(8,128)(2,1)} %broadcast_in_dim.19), calls=%async_computation.4 | async-start | bytes 196608 | tf_op jit(solution)/shard_map/all_to_all | solution.py:484
  107.1 11.7 %all-to-all-done.4 = bf16[16,24,128]{2,1,0:T(8,128)(2,1)S(1)} async-done(((bf16[16,24,128]{2,1,0:T(8,128)(2,1)}), bf16[16,24,128]{2,1,0:T(8,128)(2,1)S(1)}, u32[]{:S(2)}, u32[]{:S(2)}) %all-to-all-start.4) | async-done | bytes 98336 | tf_op jit(solution)/shard_map/all_to_all | solution.py:484
  118.8 0.7 broadcast_in_dim.20
  119.4 6.0 %all-to-all-start.5 = ((f32[8,24,128]{2,1,0:T(8,128)}), f32[8,24,128]{2,1,0:T(8,128)S(1)}, u32[]{:S(2)}, u32[]{:S(2)}) async-start(f32[8,24,128]{2,1,0:T(8,128)} %broadcast_in_dim.20), calls=%async_computation.5 | async-start | bytes 196608 | tf_op jit(solution)/shard_map/all_to_all | solution.py:484
  125.4 0.1 fusion.7
  125.6 0.9 reshape.129
  126.4 0.9 reshape.128
  127.3 3.1 %all-to-all-done.5.part_ref = f32[8,24,128]{2,1,0:T(8,128)S(1)} async-done(((f32[8,24,128]{2,1,0:T(8,128)}), f32[8,24,128]{2,1,0:T(8,128)S(1)}, u32[]{:S(2)}, u32[]{:S(2)}) %all-to-all-start.5) | async-done | bytes 98336 | tf_op jit(solution)/shard_map/all_to_all | solution.py:484
  130.4 0.8 finish.1
  (26 shorter events, 0.4 us)
Async XLA Ops:
  2.5 10.5 %all-to-all-start = ((bf16[4,144,128]{2,1,0:T(8,128)(2,1)}), bf16[4,144,128]{2,1,0:T(8,128)(2,1)S(1)}, u32[]{:S(2)}, u32[]{:S(2)}) async-start(bf16[4,144,128]{2,1,0:T(8,128)(2,1)} %get-tuple-element.35), calls=%async_computation | async-start | bytes 294912 | tf_op jit(solution)/shard_map/all_to_all | solution.py:484
  7.5 5.2 %collective-permute-start = (bf16[2,4,5120]{2,1,0:T(4,128)(2,1)S(1)}, bf16[2,4,5120]{2,1,0:T(4,128)(2,1)S(1)}, u32[]{:S(2)}, u32[]{:S(2)}) collective-permute-start(bf16[2,4,5120]{2,1,0:T(4,128)(2,1)S(1)} %get-tuple-element.32), channel_id=1, source_target_pairs={{128,0},{132,4},{136,8},{140,12},{144,16},{148,20},{152,24},{156,2... | collective-permute-start | bytes 245768 | tf_op jit(solution)/shard_map/ppermute | solution.py:501
  8.8 0.7 copy-start
  76.8 17.9 %collective-permute-start.1 = (bf16[288,128]{1,0:T(8,128)(2,1)S(1)}, bf16[288,128]{1,0:T(8,128)(2,1)S(1)}, u32[]{:S(2)}, u32[]{:S(2)}) collective-permute-start(bf16[288,128]{1,0:T(8,128)(2,1)S(1)} %get-tuple-element.44), channel_id=1, source_target_pairs={{0,3},{1,0},{2,1},{3,2},{4,7},{5,4},{6,5},{7,6},{8,11},{9,8},{10,9... | collective-permute-start | bytes 221192 | tf_op jit(solution)/shard_map/ppermute | solution.py:519
  80.6 14.1 %collective-permute-start.3 = (bf16[288,128]{1,0:T(8,128)(2,1)S(1)}, bf16[288,128]{1,0:T(8,128)(2,1)S(1)}, u32[]{:S(2)}, u32[]{:S(2)}) collective-permute-start(bf16[288,128]{1,0:T(8,128)(2,1)S(1)} %get-tuple-element.44), channel_id=1, source_target_pairs={{0,1},{1,2},{2,3},{3,0},{4,5},{5,6},{6,7},{7,4},{8,9},{9,10},{10,1... | collective-permute-start | bytes 221192 | tf_op jit(solution)/shard_map/ppermute | solution.py:519
  82.5 12.1 %collective-permute-start.2 = (bf16[288,128]{1,0:T(8,128)(2,1)S(1)}, bf16[288,128]{1,0:T(8,128)(2,1)S(1)}, u32[]{:S(2)}, u32[]{:S(2)}) collective-permute-start(bf16[288,128]{1,0:T(8,128)(2,1)S(1)} %get-tuple-element.44), channel_id=1, source_target_pairs={{0,2},{1,3},{2,0},{3,1},{4,6},{5,7},{6,4},{7,5},{8,10},{9,11},{10,... | collective-permute-start | bytes 221192 | tf_op jit(solution)/shard_map/ppermute | solution.py:519
  86.2 16.6 %all-to-all-start.3 = ((bf16[32,24,128]{2,1,0:T(8,128)(2,1)}), bf16[32,24,128]{2,1,0:T(8,128)(2,1)S(1)}, u32[]{:S(2)}, u32[]{:S(2)}) async-start(bf16[32,24,128]{2,1,0:T(8,128)(2,1)} %get-tuple-element.45), calls=%async_computation.3 | async-start | bytes 393216 | tf_op jit(solution)/shard_map/all_to_all | solution.py:484
  103.5 15.3 %all-to-all-start.4 = ((bf16[16,24,128]{2,1,0:T(8,128)(2,1)}), bf16[16,24,128]{2,1,0:T(8,128)(2,1)S(1)}, u32[]{:S(2)}, u32[]{:S(2)}) async-start(bf16[16,24,128]{2,1,0:T(8,128)(2,1)} %broadcast_in_dim.19), calls=%async_computation.4 | async-start | bytes 196608 | tf_op jit(solution)/shard_map/all_to_all | solution.py:484
  119.4 11.0 %all-to-all-start.5 = ((f32[8,24,128]{2,1,0:T(8,128)}), f32[8,24,128]{2,1,0:T(8,128)S(1)}, u32[]{:S(2)}, u32[]{:S(2)}) async-start(f32[8,24,128]{2,1,0:T(8,128)} %broadcast_in_dim.20), calls=%async_computation.5 | async-start | bytes 196608 | tf_op jit(solution)/shard_map/all_to_all | solution.py:484
